TPU v7x, 128 devices: a whole 4x4x4 slice. The times are simulated.
128 devices in a mesh: req: 16 (over y, x), mlp: 8 (over z, core).
Axes of the slice: x: 4, y: 4, z: 4, core: 2. Of those that a mesh axis runs over, the one named last changes fastest.
Arguments:
- tokens: bfloat16 [16384, 1024], P(('req', 'mlp')), may hold values from -6 to 6
- token_owner: int32 [16384, 1], replicated, may hold values from 0 to 127; in each aligned block of 128 rows (0 to 127, 128 to 255, ...) at most 2 rows name the same one
- token_request: int32 [16384], replicated, may hold values from 0 to 3
- cache_len: int32 [512], P(('req', 'mlp')), may hold values from 1 to 512, 131072 in all
- cache_k: bfloat16 [512, 512, 1024], P(('req', 'mlp')), may hold values from -6 to 6
- cache_v: bfloat16 [512, 512, 1024], P(('req', 'mlp')), may hold values from -12 to 12
- w_qkv: bfloat16 [1024, 3072], replicated, may hold values from -0.1875 to 0.1875
- w_out: bfloat16 [1024, 1024], replicated, may hold values from -0.375 to 0.375
- w_fc1: bfloat16 [1024, 4096], P(None, 'mlp'), may hold values from -0.1875 to 0.1875
- w_fc2: bfloat16 [4096, 1024], P('mlp'), may hold values from -0.09375 to 0.09375
- ln1_gain: float32 [1024], replicated, may hold values from 0.1 to 1.9
- ln1_bias: float32 [1024], replicated, may hold values from -3 to 3
- ln2_gain: float32 [1024], replicated, may hold values from 0.1 to 1.9
- ln2_bias: float32 [1024], replicated, may hold values from -3 to 3
Outputs:
- layer_out: bfloat16 [16384, 1024], P(('req', 'mlp'))
Inputs may be any that keep to these rules, and one draw needn't show every extreme that they name: `token_owner`: in each aligned block of 128 rows (the rows of one device) no owner is named more than 2 times, a bound that some block reaches; every owner is named somewhere. `cache_len`: some request has exactly 512 cached positions.
All inputs are finite; a program needn't handle non-finite values. No bound on the sum of `cache_len` on one device may be relied on, other than what follows from the above.
Results may differ from a plain program's by a relative error of at most 0.01.
Values may be sent and summed in bfloat16 or wider, within the bound.
A program may use at most 128 MiB of HBM per device.

v0:
```python
import jax
import jax.numpy as jnp
from jax import lax
from jax.sharding import PartitionSpec as P

HEADS = 16


epsilon = 1e-05


def layer_norm(values, gain, shift):
    center = values - jnp.mean(values, axis=-1, keepdims=True)
    spread = jnp.mean(center * center, axis=-1, keepdims=True)
    return center * lax.rsqrt(spread + epsilon) * gain + shift


def slot_table(owners_flat, requests_flat, owner_index, devices, tok_dev, capacity):
    owners = owners_flat.reshape(devices, tok_dev)
    requests = requests_flat.reshape(devices, tok_dev)
    mine_mask = (owners == owner_index).astype(jnp.int32)
    ranking = jnp.cumsum(mine_mask, axis=1) - 1
    places = jnp.arange(capacity, dtype=jnp.int32)
    hit_table = mine_mask[:, :, None] * (ranking[:, :, None] == places[None, None, :]).astype(
        jnp.int32
    )
    filled = jnp.sum(hit_table, axis=1)
    positions = jnp.arange(tok_dev, dtype=jnp.int32)
    local_row = jnp.sum(hit_table * positions[None, :, None], axis=1)
    sources = jnp.arange(devices, dtype=jnp.int32)[:, None]
    global_row = jnp.where(filled > 0, sources * tok_dev + local_row, -1).reshape(-1)
    slot_request = jnp.sum(hit_table * requests[:, :, None], axis=1).reshape(-1)
    return (global_row, slot_request, filled.reshape(-1))


def attend(projections, cache_keys, cache_values, lengths, global_row, slot_request, filled):
    slot_count = projections.shape[0]
    width = projections.shape[1] // 3
    head_dim = width // HEADS
    context = cache_keys.shape[1]
    score_scale = head_dim ** (-0.5)
    queries = projections[:, :width].reshape(slot_count, HEADS, head_dim)
    key_new = projections[:, width : 2 * width].reshape(slot_count, HEADS, head_dim)
    value_new = projections[:, 2 * width :].reshape(slot_count, HEADS, head_dim)
    new_mask = (
        (filled[None, :] > 0)
        & (slot_request[None, :] == slot_request[:, None])
        & (global_row[None, :] <= global_row[:, None])
    )
    new_score = (
        jnp.einsum("rhd,shd->hrs", queries, key_new, preferred_element_type=jnp.float32)
        * score_scale
    )
    new_exp = jnp.where(new_mask[None], jnp.exp(new_score), jnp.float32(0.0))
    new_total = jnp.sum(new_exp, axis=-1)
    key_place = jnp.arange(context, dtype=jnp.int32)

    def one_request(items):
        keys_here, values_here, length, request_index = items
        mask = (slot_request[:, None] == request_index) & (key_place[None, :] < length)
        score = (
            jnp.einsum(
                "rhd,khd->hrk",
                queries,
                keys_here.reshape(context, HEADS, head_dim),
                preferred_element_type=jnp.float32,
            )
            * score_scale
        )
        old_exp = jnp.where(mask[None], jnp.exp(score), jnp.float32(0.0))
        old_total = jnp.sum(old_exp, axis=-1)
        total = old_total + new_total
        total = jnp.where(total > 0, total, jnp.float32(1.0))
        weight = (old_exp / total[:, :, None]).astype(jnp.bfloat16)
        part = jnp.einsum(
            "hrk,khd->rhd",
            weight,
            values_here.reshape(context, HEADS, head_dim),
            preferred_element_type=jnp.float32,
        )
        return (part, old_total)

    request_ids = jnp.arange(cache_keys.shape[0], dtype=jnp.int32)
    parts, totals = lax.map(one_request, (cache_keys, cache_values, lengths, request_ids))
    denominator = jnp.sum(totals, axis=0) + new_total
    denominator = jnp.where(denominator > 0, denominator, jnp.float32(1.0))
    new_weight = (new_exp / denominator[:, :, None]).astype(jnp.bfloat16)
    result = jnp.sum(parts, axis=0)
    result = result + jnp.einsum(
        "hrs,shd->rhd", new_weight, value_new, preferred_element_type=jnp.float32
    )
    return result.reshape(slot_count, width).astype(jnp.bfloat16)


def per_device(
    tokens,
    token_owner,
    token_request,
    cache_len,
    cache_k,
    cache_v,
    w_qkv,
    w_out,
    w_fc1,
    w_fc2,
    ln1_gain,
    ln1_bias,
    ln2_gain,
    ln2_bias,
):
    n_req = lax.axis_size("req")
    n_mlp = lax.axis_size("mlp")
    devices = n_req * n_mlp
    owner_index = lax.axis_index("req") * n_mlp + lax.axis_index("mlp")
    tok_dev, width = tokens.shape
    capacity = max(2, 2 * tok_dev // devices)
    slot_count = devices * capacity
    owners_flat = token_owner.reshape(-1)
    my_owners = lax.dynamic_slice_in_dim(owners_flat, owner_index * tok_dev, tok_dev)
    owner_onehot = (my_owners[:, None] == jnp.arange(devices, dtype=jnp.int32)[None, :]).astype(
        jnp.int32
    )
    ranking = jnp.cumsum(owner_onehot, axis=0) - 1
    my_rank = jnp.sum(owner_onehot * ranking, axis=1)
    column = my_owners * capacity + my_rank
    dispatch = (column[:, None] == jnp.arange(slot_count, dtype=jnp.int32)[None, :]).astype(
        jnp.bfloat16
    )
    outgoing = jnp.einsum("tr,td->rd", dispatch, tokens, preferred_element_type=jnp.float32).astype(
        jnp.bfloat16
    )
    arrived = lax.all_to_all(
        outgoing.reshape(devices, capacity, width),
        ("req", "mlp"),
        split_axis=0,
        concat_axis=0,
        tiled=True,
    )
    projections = jnp.dot(
        arrived.reshape(slot_count, width), w_qkv, preferred_element_type=jnp.float32
    ).astype(jnp.bfloat16)
    global_row, slot_request, filled = slot_table(
        owners_flat, token_request, owner_index, devices, tok_dev, capacity
    )
    attended = attend(projections, cache_k, cache_v, cache_len, global_row, slot_request, filled)
    returned = lax.all_to_all(
        attended.reshape(devices, capacity, width),
        ("req", "mlp"),
        split_axis=0,
        concat_axis=0,
        tiled=True,
    )
    attn_rows = jnp.dot(
        dispatch, returned.reshape(slot_count, width), preferred_element_type=jnp.float32
    ).astype(jnp.bfloat16)
    projected_out = jnp.dot(attn_rows, w_out, preferred_element_type=jnp.float32)
    normed = layer_norm(projected_out + tokens.astype(jnp.float32), ln1_gain, ln1_bias).astype(
        jnp.bfloat16
    )
    gathered = lax.all_gather(normed, "mlp", axis=0, tiled=True)
    hidden = jax.nn.gelu(
        jnp.dot(gathered, w_fc1, preferred_element_type=jnp.float32), approximate=False
    ).astype(jnp.bfloat16)
    summed = lax.psum_scatter(
        jnp.dot(hidden, w_fc2, preferred_element_type=jnp.float32).astype(jnp.bfloat16),
        "mlp",
        scatter_dimension=0,
        tiled=True,
    ).astype(jnp.float32)
    return layer_norm(normed.astype(jnp.float32) + summed, ln2_gain, ln2_bias).astype(jnp.bfloat16)


def solution(mesh):
    placed = (
        P(("req", "mlp"), None),
        P(),
        P(),
        P(("req", "mlp")),
        P(("req", "mlp"), None, None),
        P(("req", "mlp"), None, None),
        P(),
        P(),
        P(None, "mlp"),
        P("mlp", None),
        P(),
        P(),
        P(),
        P(),
    )
    return jax.shard_map(
        per_device, mesh=mesh, in_specs=placed, out_specs=P(("req", "mlp"), None), check_vma=False
    )
```

profile of v0, /device:TPU:0, one launch (start us, length us, event | category | flops | bytes accessed | tf_op | source)
XLA Modules:
  0.0 244.5 jit_solution(8810175562565531426)
XLA Ops:
  6.5 0.8 fusion.63
  7.8 0.7 fusion.62
  8.5 1.3 convolution_convert_fusion.2
  9.8 1.0 reshape.262
  10.8 11.1 %all-to-all-start = ((bf16[128,2,1024]{2,1,0:T(2,128)(2,1)}), bf16[128,2,1024]{2,1,0:T(2,128)(2,1)S(1)}, u32[]{:S(2)}, u32[]{:S(2)}) async-start(bf16[128,2,1024]{2,1,0:T(2,128)(2,1)} %reshape.262), calls=%async_computation | async-start | bytes 1048576 | tf_op jit(solution)/shard_map/all_to_all | solution.py:132
  23.7 12.0 %all-to-all-done = bf16[128,2,1024]{2,1,0:T(2,128)(2,1)S(1)} async-done(((bf16[128,2,1024]{2,1,0:T(2,128)(2,1)}), bf16[128,2,1024]{2,1,0:T(2,128)(2,1)S(1)}, u32[]{:S(2)}, u32[]{:S(2)}) %all-to-all-start) | async-done | bytes 524320 | tf_op jit(solution)/shard_map/all_to_all | solution.py:132
  35.7 0.2 reshape.263
  35.9 4.6 %convolution_convert_fusion = bf16[256,3072]{1,0:T(8,128)(2,1)S(1)} fusion(bf16[256,1024]{1,0:T(8,128)(2,1)S(1)} %reshape.263, bf16[1024,3072]{1,0:T(8,128)(2,1)} %param.22), kind=kOutput, calls=%fused_computation.18 | convolution fusion | flops 1611399168 | bytes 8388608 | tf_op jit(solution)/shard_map/dot_general | solution.py:139
  40.5 1.0 fusion.96
  41.4 1.0 copy.38
  42.4 0.2 copy.42
  42.7 4.1 %fusion.8 = (f32[16,256]{1,0:T(8,128)S(1)}, f32[16,256,256]{1,2,0:T(8,128)}) fusion(pred[256,256]{0,1:T(8,128)(4,1)S(1)} %compare_and_fusion, bf16[256,16,64]{0,2,1:T(8,128)(2,1)} %bitcast.82, bf16[256,16,64]{0,2,1:T(8,128)(2,1)S(1)} %bitcast.85), kind=kOutput, calls=%fused_computation.19 | convolution fusion | flops 137359360 | bytes 5324800 | tf_op jit(solution)/shard_map/rhd,shd->hrs/dot_general | solution.py:51
  46.7 88.6 %while.13 = (s32[]{:T(128)}, f32[4,256,16,64]{1,3,2,0:T(8,128)}, f32[4,16,256]{2,1,0:T(8,128)S(1)}, bf16[4,512,1024]{2,1,0:T(8,128)(2,1)}, s32[4]{0:T(128)S(1)},...) while((s32[]{:T(128)}, f32[4,256,16,64]{1,3,2,0:T(8,128)}, ...), condition=%wide.region_9.10_spmd.clone, body=%wide.region_7.9_spmd.clone.sunk | while | flops 551691008 | bytes 29347476 | solution.py:84
  46.7 0.6 dynamic_slice.33
  47.3 0.6 broadcast_compare_fusion.3
  48.0 0.6 dynamic_slice.34
  48.6 0.6 iota_compare_fusion.10
  49.3 2.7 %constant_dynamic-slice_fusion.4 = (bf16[1,512,1024]{2,1,0:T(8,128)(2,1)}, bf16[1,512,1024]{2,1,0:T(8,128)(2,1)S(1)}) fusion(bf16[4,512,1024]{2,1,0:T(8,128)(2,1)} %get-tuple-element.249, s32[]{:T(128)} %get-tuple-element.231, bf16[4,512,1024]{2,1,0:T(8,128)(2,1)} %get-tuple-element.245), kind=kLoop, calls=%fused_computation.12.clone.1 | loop fusion | bytes 4194308 | tf_op jit(solution)/shard_map/while/body/jit(dynamic_index_in_dim)/dynamic_slice | solution.py:84
  52.0 2.3 copy.56
  54.3 6.5 %fusion.122 = (f32[16,256]{1,0:T(8,128)S(1)}, f32[16,512,256]{2,1,0:T(8,128)}) fusion(pred[256,512]{0,1:T(8,128)(4,1)S(1)} %broadcast_and_fusion.2, bf16[512,16,64]{0,2,1:T(8,128)(2,1)} %bitcast.79, bf16[256,16,64]{0,2,1:T(8,128)(2,1)} %get-tuple-element.250), kind=kOutput, calls=%fused_computation.3.clone.1 | convolution fusion | flops 274722816 | bytes 10108928 | tf_op jit(solution)/shard_map/while/body/eval_jaxpr/rhd,khd->hrk/dot_general | solution.py:62
  60.9 1.3 copy.55
  62.2 6.7 %fusion.123 = f32[4,256,16,64]{1,3,2,0:T(8,128)} fusion(f32[4,256,16,64]{1,3,2,0:T(8,128)} %get-tuple-element.232, s32[]{:T(128)} %get-tuple-element.231, bf16[512,16,64]{0,2,1:T(8,128)(2,1)} %bitcast.78, f32[16,512,256]{2,1,0:T(8,128)} %get-tuple-element.218, f32[16,256]{1,0:T(8,128)S(1)} %compare_select_fusion.3, ...), kind=kOutput, calls=%fused_computation.6.clone.1 | convolution fusion | flops 276824064 | bytes 10633728 | tf_op jit(solution)/shard_map/while/body/eval_jaxpr/hrk,khd->rhd/dot_general | solution.py:75
  69.0 0.6 dynamic_slice.33
  69.5 0.6 broadcast_compare_fusion.3
  70.3 0.6 dynamic_slice.34
  70.8 0.6 iota_compare_fusion.10
  71.6 2.7 %constant_dynamic-slice_fusion.4 = (bf16[1,512,1024]{2,1,0:T(8,128)(2,1)}, bf16[1,512,1024]{2,1,0:T(8,128)(2,1)S(1)}) fusion(bf16[4,512,1024]{2,1,0:T(8,128)(2,1)} %get-tuple-element.249, s32[]{:T(128)} %get-tuple-element.231, bf16[4,512,1024]{2,1,0:T(8,128)(2,1)} %get-tuple-element.245), kind=kLoop, calls=%fused_computation.12.clone.1 | loop fusion | bytes 4194308 | tf_op jit(solution)/shard_map/while/body/jit(dynamic_index_in_dim)/dynamic_slice | solution.py:84
  74.3 2.3 copy.56
  76.6 6.5 %fusion.122 = (f32[16,256]{1,0:T(8,128)S(1)}, f32[16,512,256]{2,1,0:T(8,128)}) fusion(pred[256,512]{0,1:T(8,128)(4,1)S(1)} %broadcast_and_fusion.2, bf16[512,16,64]{0,2,1:T(8,128)(2,1)} %bitcast.79, bf16[256,16,64]{0,2,1:T(8,128)(2,1)} %get-tuple-element.250), kind=kOutput, calls=%fused_computation.3.clone.1 | convolution fusion | flops 274722816 | bytes 10108928 | tf_op jit(solution)/shard_map/while/body/eval_jaxpr/rhd,khd->hrk/dot_general | solution.py:62
  83.1 1.3 copy.55
  84.4 6.7 %fusion.123 = f32[4,256,16,64]{1,3,2,0:T(8,128)} fusion(f32[4,256,16,64]{1,3,2,0:T(8,128)} %get-tuple-element.232, s32[]{:T(128)} %get-tuple-element.231, bf16[512,16,64]{0,2,1:T(8,128)(2,1)} %bitcast.78, f32[16,512,256]{2,1,0:T(8,128)} %get-tuple-element.218, f32[16,256]{1,0:T(8,128)S(1)} %compare_select_fusion.3, ...), kind=kOutput, calls=%fused_computation.6.clone.1 | convolution fusion | flops 276824064 | bytes 10633728 | tf_op jit(solution)/shard_map/while/body/eval_jaxpr/hrk,khd->rhd/dot_general | solution.py:75
  91.1 0.6 dynamic_slice.33
  91.7 0.6 broadcast_compare_fusion.3
  92.4 0.6 dynamic_slice.34
  93.0 0.6 iota_compare_fusion.10
  93.7 2.7 %constant_dynamic-slice_fusion.4 = (bf16[1,512,1024]{2,1,0:T(8,128)(2,1)}, bf16[1,512,1024]{2,1,0:T(8,128)(2,1)S(1)}) fusion(bf16[4,512,1024]{2,1,0:T(8,128)(2,1)} %get-tuple-element.249, s32[]{:T(128)} %get-tuple-element.231, bf16[4,512,1024]{2,1,0:T(8,128)(2,1)} %get-tuple-element.245), kind=kLoop, calls=%fused_computation.12.clone.1 | loop fusion | bytes 4194308 | tf_op jit(solution)/shard_map/while/body/jit(dynamic_index_in_dim)/dynamic_slice | solution.py:84
  96.4 2.3 copy.56
  98.7 6.5 %fusion.122 = (f32[16,256]{1,0:T(8,128)S(1)}, f32[16,512,256]{2,1,0:T(8,128)}) fusion(pred[256,512]{0,1:T(8,128)(4,1)S(1)} %broadcast_and_fusion.2, bf16[512,16,64]{0,2,1:T(8,128)(2,1)} %bitcast.79, bf16[256,16,64]{0,2,1:T(8,128)(2,1)} %get-tuple-element.250), kind=kOutput, calls=%fused_computation.3.clone.1 | convolution fusion | flops 274722816 | bytes 10108928 | tf_op jit(solution)/shard_map/while/body/eval_jaxpr/rhd,khd->hrk/dot_general | solution.py:62
  105.2 1.3 copy.55
  106.5 6.7 %fusion.123 = f32[4,256,16,64]{1,3,2,0:T(8,128)} fusion(f32[4,256,16,64]{1,3,2,0:T(8,128)} %get-tuple-element.232, s32[]{:T(128)} %get-tuple-element.231, bf16[512,16,64]{0,2,1:T(8,128)(2,1)} %bitcast.78, f32[16,512,256]{2,1,0:T(8,128)} %get-tuple-element.218, f32[16,256]{1,0:T(8,128)S(1)} %compare_select_fusion.3, ...), kind=kOutput, calls=%fused_computation.6.clone.1 | convolution fusion | flops 276824064 | bytes 10633728 | tf_op jit(solution)/shard_map/while/body/eval_jaxpr/hrk,khd->rhd/dot_general | solution.py:75
  113.2 0.6 dynamic_slice.33
  113.8 0.6 broadcast_compare_fusion.3
  114.5 0.6 dynamic_slice.34
  115.1 0.6 iota_compare_fusion.10
  115.8 2.7 %constant_dynamic-slice_fusion.4 = (bf16[1,512,1024]{2,1,0:T(8,128)(2,1)}, bf16[1,512,1024]{2,1,0:T(8,128)(2,1)S(1)}) fusion(bf16[4,512,1024]{2,1,0:T(8,128)(2,1)} %get-tuple-element.249, s32[]{:T(128)} %get-tuple-element.231, bf16[4,512,1024]{2,1,0:T(8,128)(2,1)} %get-tuple-element.245), kind=kLoop, calls=%fused_computation.12.clone.1 | loop fusion | bytes 4194308 | tf_op jit(solution)/shard_map/while/body/jit(dynamic_index_in_dim)/dynamic_slice | solution.py:84
  118.5 2.3 copy.56
  120.8 6.5 %fusion.122 = (f32[16,256]{1,0:T(8,128)S(1)}, f32[16,512,256]{2,1,0:T(8,128)}) fusion(pred[256,512]{0,1:T(8,128)(4,1)S(1)} %broadcast_and_fusion.2, bf16[512,16,64]{0,2,1:T(8,128)(2,1)} %bitcast.79, bf16[256,16,64]{0,2,1:T(8,128)(2,1)} %get-tuple-element.250), kind=kOutput, calls=%fused_computation.3.clone.1 | convolution fusion | flops 274722816 | bytes 10108928 | tf_op jit(solution)/shard_map/while/body/eval_jaxpr/rhd,khd->hrk/dot_general | solution.py:62
  127.3 1.3 copy.55
  128.7 6.7 %fusion.123 = f32[4,256,16,64]{1,3,2,0:T(8,128)} fusion(f32[4,256,16,64]{1,3,2,0:T(8,128)} %get-tuple-element.232, s32[]{:T(128)} %get-tuple-element.231, bf16[512,16,64]{0,2,1:T(8,128)(2,1)} %bitcast.78, f32[16,512,256]{2,1,0:T(8,128)} %get-tuple-element.218, f32[16,256]{1,0:T(8,128)S(1)} %compare_select_fusion.3, ...), kind=kOutput, calls=%fused_computation.6.clone.1 | convolution fusion | flops 276824064 | bytes 10633728 | tf_op jit(solution)/shard_map/while/body/eval_jaxpr/hrk,khd->rhd/dot_general | solution.py:75
  135.4 3.7 %reduce_sum.116 = f32[256,16,64]{0,2,1:T(8,128)} reduce(f32[4,256,16,64]{1,3,2,0:T(8,128)} %get-tuple-element.63, f32[]{:T(128)} %constant.28.clone.1), dimensions={0}, to_apply=%region_10.11 | reduce | flops 786432 | bytes 5242884 | tf_op jit(solution)/shard_map/reduce_sum | solution.py:88
  139.1 0.2 copy.46
  139.3 4.4 %fusion.22 = bf16[256,16,64]{0,2,1:T(8,128)(2,1)} fusion(f32[256,16,64]{0,2,1:T(8,128)} %reduce_sum.116, bf16[256,16,64]{0,2,1:T(8,128)(2,1)S(1)} %bitcast.84, f32[16,256,256]{1,2,0:T(8,128)} %get-tuple-element.148, f32[16,256]{1,0:T(8,128)S(1)} %compare_select_fusion.1, pred[256,256]{0,1:T(8,128)(4,1)S(1)} %compare_and_fusion), kind=kOutput, calls=%fused_computation.43 | convolution fusion | flops 138936320 | bytes 6373376 | tf_op jit(solution)/shard_map/hrs,shd->rhd/dot_general | solution.py:89
  143.7 2.0 copy.48
  145.7 1.4 convert_element_type.69
  147.1 18.7 %all_to_all.10 = bf16[128,2,1024]{2,1,0:T(2,128)(2,1)S(1)} all-to-all(bf16[128,2,1024]{2,1,0:T(2,128)(2,1)} %convert_element_type.69), channel_id=1, replica_groups=mesh['req'=16,'mlp'=8] {'req','mlp'}, dimensions={0} | all-to-all | bytes 1048576 | tf_op jit(solution)/shard_map/all_to_all | solution.py:146
  166.0 0.7 fusion.97
  166.7 0.2 multiply_reduce_fusion.1
  167.0 0.9 add_convert_fusion.1
  167.9 21.2 %all-gather.2.cloned.1.call-done = bf16[1024,1024]{1,0:T(8,128)(2,1)} async-done(((bf16[128,1024]{1,0:T(8,128)(2,1)}), bf16[1024,1024]{1,0:T(8,128)(2,1)}) %all-gather.2.cloned.1.call-update) | async-done | bytes 2097168 | tf_op jit(solution)/shard_map/all_gather | solution.py:160
  189.2 9.7 %convolution_convert_fusion.1 = bf16[1024,1024]{1,0:T(8,128)(2,1)} fusion(bf16[512,1024]{1,0:T(8,128)(2,1)} %param.25, bf16[1024,1024]{1,0:T(8,128)(2,1)} %all-gather.2.cloned.1.call-done, bf16[1024,512]{1,0:T(8,128)(2,1)} %param.24), kind=kOutput, calls=%fused_computation.40 | convolution fusion | flops 2182610944 | bytes 6291456 | tf_op jit(solution)/shard_map/dot_general | solution.py:165
  198.9 34.3 %reduce-scatter.2.cloned.1.call-done = bf16[128,1024]{1,0:T(8,128)(2,1)} async-done(((bf16[1024,1024]{1,0:T(8,128)(2,1)}), bf16[128,1024]{1,0:T(8,128)(2,1)}) %reduce-scatter.2.cloned.1.call-update) | async-done | bytes 262160 | tf_op jit(solution)/shard_map/reduce_scatter | solution.py:164
  233.2 1.2 fusion.55
  234.4 1.3 multiply_reduce_fusion
  235.7 1.9 add_convert_fusion
  (70 shorter events, 3.6 us)
Async XLA Ops:
  6.5 159.5 %copy-start = (bf16[1024,1024]{1,0:T(8,128)(2,1)S(1)}, bf16[1024,1024]{1,0:T(8,128)(2,1)}, u32[]{:S(2)}) copy-start(bf16[1024,1024]{1,0:T(8,128)(2,1)} %param.23) | copy-start | bytes 6291460
  6.5 15.5 %copy-start.3 = (s32[16384,1]{0,1:T(1,128)S(1)}, s32[16384,1]{0,1:T(1,128)}, u32[]{:S(2)}) copy-start(s32[16384,1]{0,1:T(1,128)} %param.17) | copy-start | bytes 196612
  6.5 15.9 %copy-start.6 = (s32[16384]{0:T(1024)S(1)}, s32[16384]{0:T(1024)}, u32[]{:S(2)}) copy-start(s32[16384]{0:T(1024)} %param.18) | copy-start | bytes 196612
  10.8 24.9 %all-to-all-start = ((bf16[128,2,1024]{2,1,0:T(2,128)(2,1)}), bf16[128,2,1024]{2,1,0:T(2,128)(2,1)S(1)}, u32[]{:S(2)}, u32[]{:S(2)}) async-start(bf16[128,2,1024]{2,1,0:T(2,128)(2,1)} %reshape.262), calls=%async_computation | async-start | bytes 1048576 | tf_op jit(solution)/shard_map/all_to_all | solution.py:132
  21.9 167.2 %all-gather.2.cloned.1.call-start = ((), (), s32[]{:S(2)}) async-start(), calls=%async_computation.3 | async-start | bytes 2359296 | tf_op jit(solution)/shard_map/all_gather | solution.py:160
  42.6 4.1 %copy-start.9 = (s32[4]{0:T(128)S(1)}, s32[4]{0:T(128)}, u32[]{:S(2)}) copy-start(s32[4]{0:T(128)} %param.19) | copy-start | bytes 52
  135.4 3.7 %copy-start.1 = (bf16[256,1024]{1,0:T(8,128)(2,1)S(1)}, bf16[256,1024]{1,0:T(8,128)(2,1)}, u32[]{:S(2)}) copy-start(bf16[256,1024]{1,0:T(8,128)(2,1)} %get-tuple-element.144) | copy-start | bytes 1572868
  145.7 20.3 %copy-start.2 = (bf16[128,1024]{1,0:T(8,128)(2,1)S(1)}, bf16[128,1024]{1,0:T(8,128)(2,1)}, u32[]{:S(2)}) copy-start(bf16[128,1024]{1,0:T(8,128)(2,1)} %param.16) | copy-start | bytes 786436
  166.0 0.9 copy-start.4
  166.0 0.9 copy-start.5
  167.9 65.3 %reduce-scatter.2.cloned.1.call-start = ((), (), s32[]{:S(2)}) async-start(), calls=%async_computation.4 | async-start | bytes 2359296 | tf_op jit(solution)/shard_map/reduce_scatter | solution.py:164
  198.8 36.8 %copy-start.7 = (f32[1024]{0:T(1024)S(1)}, f32[1024]{0:T(1024)}, u32[]{:S(2)}) copy-start(f32[1024]{0:T(1024)} %param.29) | copy-start | bytes 12292
  198.8 36.8 %copy-start.8 = (f32[1024]{0:T(1024)S(1)}, f32[1024]{0:T(1024)}, u32[]{:S(2)}) copy-start(f32[1024]{0:T(1024)} %param.28) | copy-start | bytes 12292
Sparse Core Ops, SparseCore 0:
  168.0 21.1 all-gather.1
  199.0 34.1 reduce-scatter.1
where the time goes:
time: 245 us; the launch traced here: 244 us
  matrix products  77.6 us (32%)
  waiting for transfers between devices  67.5 us (28%)
  local copies, waits for them, and re-layouts  39.5 us (16%)
  blocking collectives  18.7 us (8%)
  other arithmetic  16 us (7%)
  between operations  13.7 us (6%)
  starting transfers between devices  11.2 us (5%)
    reduce_scatter x1, waiting for transfers between devices, per_device(): lax.psum_scatter(jnp.dot(hidden, w_fc2, preferred_element_type=jnp.float3...  34.3 us
    dynamic_slice x20, local copies, waits for them, and re-layouts, attend(): lax.map(one_request, (cache_keys, cache_values, lengths, request_ids))  30 us
    dot_general x4, matrix products, one_request(): jnp.einsum('hrk,khd->rhd', weight, values_here.reshape(context, HEADS, he...  26.8 us
    dot_general x4, matrix products, one_request(): jnp.einsum('rhd,khd->hrk', queries, keys_here.reshape(context, HEADS, hea...  26.1 us
    all_gather x1, waiting for transfers between devices, per_device(): gathered = lax.all_gather(normed, 'mlp', axis=0, tiled=True)  21.2 us
    all_to_all x1, blocking collectives, per_device(): lax.all_to_all(attended.reshape(devices, capacity, width), ('req', 'mlp')...  18.7 us
    all_to_all x1, waiting for transfers between devices, per_device(): lax.all_to_all(outgoing.reshape(devices, capacity, width), ('req', 'mlp')...  12 us
    all_to_all x1, starting transfers between devices, per_device(): lax.all_to_all(outgoing.reshape(devices, capacity, width), ('req', 'mlp')...  11.1 us
  transfers between devices with their start and end apart: 3, of which 3 were waited for; matrix products, arithmetic and copies ran while one was open for 1% of the time, Pallas kernels for 0%

commit v1 on v0

--- a/solution.py
+++ b/solution.py
@@ -2,6 +2,8 @@
 import jax.numpy as jnp
 from jax import lax
 from jax.sharding import PartitionSpec as P
+from jax.experimental import pallas as pl
+from jax.experimental.pallas import tpu as pltpu
 
 HEADS = 16
 
@@ -33,63 +35,98 @@
     return (global_row, slot_request, filled.reshape(-1))
 
 
+def attention_kernel(
+    q_ref, kn_ref, vn_ref, k_ref, v_ref, rreq_ref, rrow_ref, rfill_ref, ctag_ref, ntag_ref, nrow_ref, o_ref
+):
+    head_dim = q_ref.shape[1] // 2
+    score_scale = head_dim ** (-0.5)
+    q = q_ref[...]
+    keys = k_ref[...]
+    values = v_ref[...]
+    key_new = kn_ref[...]
+    value_new = vn_ref[...]
+    row_request = rreq_ref[...]
+    old_mask = ctag_ref[...] == row_request
+    new_mask = (ntag_ref[...] == row_request) & (nrow_ref[...] <= rrow_ref[...])
+    lane = lax.broadcasted_iota(jnp.int32, (1, q.shape[1]), 1)
+    contract = (((1,), (1,)), ((), ()))
+    result = None
+    for half in range(2):
+        in_head = (lane // head_dim) == half
+        q_head = jnp.where(in_head, q, jnp.zeros_like(q))
+        old_score = (
+            lax.dot_general(q_head, keys, contract, preferred_element_type=jnp.float32) * score_scale
+        )
+        new_score = (
+            lax.dot_general(q_head, key_new, contract, preferred_element_type=jnp.float32)
+            * score_scale
+        )
+        old_exp = jnp.where(old_mask, jnp.exp(old_score), jnp.float32(0.0))
+        new_exp = jnp.where(new_mask, jnp.exp(new_score), jnp.float32(0.0))
+        total = jnp.sum(old_exp, axis=1, keepdims=True) + jnp.sum(new_exp, axis=1, keepdims=True)
+        total = jnp.where(total > 0, total, jnp.float32(1.0))
+        inverse = 1.0 / total
+        old_weight = (old_exp * inverse).astype(jnp.bfloat16)
+        new_weight = (new_exp * inverse).astype(jnp.bfloat16)
+        part = jnp.dot(old_weight, values, preferred_element_type=jnp.float32) + jnp.dot(
+            new_weight, value_new, preferred_element_type=jnp.float32
+        )
+        result = part if result is None else jnp.where(in_head, part, result)
+    result = jnp.where(rfill_ref[...] > 0, result, jnp.float32(0.0))
+    o_ref[...] = result.astype(o_ref.dtype)
+
+
 def attend(projections, cache_keys, cache_values, lengths, global_row, slot_request, filled):
     slot_count = projections.shape[0]
     width = projections.shape[1] // 3
-    head_dim = width // HEADS
-    context = cache_keys.shape[1]
-    score_scale = head_dim ** (-0.5)
-    queries = projections[:, :width].reshape(slot_count, HEADS, head_dim)
-    key_new = projections[:, width : 2 * width].reshape(slot_count, HEADS, head_dim)
-    value_new = projections[:, 2 * width :].reshape(slot_count, HEADS, head_dim)
-    new_mask = (
-        (filled[None, :] > 0)
-        & (slot_request[None, :] == slot_request[:, None])
-        & (global_row[None, :] <= global_row[:, None])
-    )
-    new_score = (
-        jnp.einsum("rhd,shd->hrs", queries, key_new, preferred_element_type=jnp.float32)
-        * score_scale
-    )
-    new_exp = jnp.where(new_mask[None], jnp.exp(new_score), jnp.float32(0.0))
-    new_total = jnp.sum(new_exp, axis=-1)
-    key_place = jnp.arange(context, dtype=jnp.int32)
-
-    def one_request(items):
-        keys_here, values_here, length, request_index = items
-        mask = (slot_request[:, None] == request_index) & (key_place[None, :] < length)
-        score = (
-            jnp.einsum(
-                "rhd,khd->hrk",
-                queries,
-                keys_here.reshape(context, HEADS, head_dim),
-                preferred_element_type=jnp.float32,
-            )
-            * score_scale
-        )
-        old_exp = jnp.where(mask[None], jnp.exp(score), jnp.float32(0.0))
-        old_total = jnp.sum(old_exp, axis=-1)
-        total = old_total + new_total
-        total = jnp.where(total > 0, total, jnp.float32(1.0))
-        weight = (old_exp / total[:, :, None]).astype(jnp.bfloat16)
-        part = jnp.einsum(
-            "hrk,khd->rhd",
-            weight,
-            values_here.reshape(context, HEADS, head_dim),
-            preferred_element_type=jnp.float32,
-        )
-        return (part, old_total)
-
-    request_ids = jnp.arange(cache_keys.shape[0], dtype=jnp.int32)
-    parts, totals = lax.map(one_request, (cache_keys, cache_values, lengths, request_ids))
-    denominator = jnp.sum(totals, axis=0) + new_total
-    denominator = jnp.where(denominator > 0, denominator, jnp.float32(1.0))
-    new_weight = (new_exp / denominator[:, :, None]).astype(jnp.bfloat16)
-    result = jnp.sum(parts, axis=0)
-    result = result + jnp.einsum(
-        "hrs,shd->rhd", new_weight, value_new, preferred_element_type=jnp.float32
-    )
-    return result.reshape(slot_count, width).astype(jnp.bfloat16)
+    requests, context = cache_keys.shape[0], cache_keys.shape[1]
+    pair = 128
+    pairs = width // pair
+    keys = cache_keys.reshape(requests * context, width)
+    values = cache_values.reshape(requests * context, width)
+    key_owner = jnp.arange(requests * context, dtype=jnp.int32) // context
+    key_place = jnp.arange(requests * context, dtype=jnp.int32) % context
+    key_limit = jnp.repeat(lengths, context)
+    column_tag = jnp.where(key_place < key_limit, key_owner, -1).reshape(1, -1)
+    new_tag = jnp.where(filled > 0, slot_request, -1).reshape(1, -1)
+    new_row = global_row.reshape(1, -1)
+    row_request = slot_request.reshape(-1, 1)
+    row_index = global_row.reshape(-1, 1)
+    row_filled = filled.reshape(-1, 1)
+    keyed = requests * context
+    whole = lambda shape: pl.BlockSpec(shape, lambda p: (0, 0))
+    return pl.pallas_call(
+        attention_kernel,
+        grid=(pairs,),
+        in_specs=[
+            pl.BlockSpec((slot_count, pair), lambda p: (0, p)),
+            pl.BlockSpec((slot_count, pair), lambda p: (0, pairs + p)),
+            pl.BlockSpec((slot_count, pair), lambda p: (0, 2 * pairs + p)),
+            pl.BlockSpec((keyed, pair), lambda p: (0, p)),
+            pl.BlockSpec((keyed, pair), lambda p: (0, p)),
+            whole((slot_count, 1)),
+            whole((slot_count, 1)),
+            whole((slot_count, 1)),
+            whole((1, keyed)),
+            whole((1, slot_count)),
+            whole((1, slot_count)),
+        ],
+        out_specs=pl.BlockSpec((slot_count, pair), lambda p: (0, p)),
+        out_shape=jax.ShapeDtypeStruct((slot_count, width), jnp.bfloat16),
+        compiler_params=pltpu.CompilerParams(vmem_limit_bytes=48 * 1024 * 1024),
+    )(
+        projections,
+        projections,
+        projections,
+        keys,
+        values,
+        row_request,
+        row_index,
+        row_filled,
+        column_tag,
+        new_tag,
+        new_row,
+    )
 
 
 def per_device(

time: 245 us -> 157 us (0.64)
  matrix products: 77.6 us -> 16.3 us
  local copies, waits for them, and re-layouts: 39.5 us -> 3.79 us
  Pallas kernels: 0 us -> 19.6 us
  other arithmetic: 16 us -> 7.06 us
    dot_general x10 -> x0, matrix products: 61.3 us -> none  [the longest x4 26.8 us: one_request(): jnp.einsum('hrk,khd->rhd', weight, values_here.reshape(context, HEADS, he...]
    dynamic_slice x20 -> x0, local copies, waits for them, and re-layouts: 30 us -> none  [attend(): lax.map(one_request, (cache_keys, cache_values, lengths, request_ids))]
    pallas_call x0 -> x1, Pallas kernels: none -> 19.6 us  [attend(): pl.pallas_call(attention_kernel, grid=(pairs,), in_specs=[pl.BlockSpec((s...]
    reduce_sum x3 -> x1, other arithmetic: 3.84 us -> 0.18 us  [slot_table(): filled = jnp.sum(hit_table, axis=1)]
    convert_element_type x2 -> x0, local copies, waits for them, and re-layouts: 3.37 us -> none  [attend(): return result.reshape(slot_count, width).astype(jnp.bfloat16)]
where the time goes in v1:
time: 157 us
  waiting for transfers between devices  67.1 us (43%)
  Pallas kernels  19.6 us (12%)
  blocking collectives  18 us (11%)
  matrix products  16.3 us (10%)
  between operations  13.7 us (9%)
  starting transfers between devices  11.4 us (7%)
  other arithmetic  7.06 us (4%)
  local copies, waits for them, and re-layouts  3.79 us (2%)
    reduce_scatter x1, waiting for transfers between devices, per_device(): lax.psum_scatter(jnp.dot(hidden, w_fc2, preferred_element_type=jnp.float3...  34.3 us
    all_gather x1, waiting for transfers between devices, per_device(): gathered = lax.all_gather(normed, 'mlp', axis=0, tiled=True)  21 us
    pallas_call x1, Pallas kernels, attend(): pl.pallas_call(attention_kernel, grid=(pairs,), in_specs=[pl.BlockSpec((s...  19.6 us
    all_to_all x1, blocking collectives, per_device(): lax.all_to_all(attended.reshape(devices, capacity, width), ('req', 'mlp')...  18 us
    all_to_all x1, waiting for transfers between devices, per_device(): lax.all_to_all(outgoing.reshape(devices, capacity, width), ('req', 'mlp')...  11.7 us
    all_to_all x1, starting transfers between devices, per_device(): lax.all_to_all(outgoing.reshape(devices, capacity, width), ('req', 'mlp')...  11.1 us
    dot_general x1, matrix products, per_device(): jnp.dot(hidden, w_fc2, preferred_element_type=jnp.float32)  9.68 us
    dot_general x1, matrix products, per_device(): jnp.dot(arrived.reshape(slot_count, width), w_qkv, preferred_element_type...  4.58 us
  transfers between devices with their start and end apart: 3, of which 3 were waited for; matrix products, arithmetic and copies ran while one was open for 1% of the time, Pallas kernels for 0%

profile of v1, /device:TPU:0, one launch (start us, length us, event | category | flops | bytes accessed | tf_op | source)
XLA Modules:
  0.0 157.0 jit_solution(8335216962352885863)
XLA Ops:
  6.5 0.0 copy-start
  6.5 0.0 copy-start.2
  6.5 0.0 copy-start.5
  6.5 0.8 fusion.50
  7.3 0.1 fusion.48
  7.4 0.2 reduce_window_sum.22
  7.6 0.2 select_reduce_fusion.1
  7.8 0.7 fusion.49
  8.5 0.0 copy-start.6
  8.5 1.3 convolution_convert_fusion.2
  9.8 0.0 copy-start.10
  9.8 1.0 reshape.234
  10.8 11.1 %all-to-all-start = ((bf16[128,2,1024]{2,1,0:T(2,128)(2,1)}), bf16[128,2,1024]{2,1,0:T(2,128)(2,1)S(1)}, u32[]{:S(2)}, u32[]{:S(2)}) async-start(bf16[128,2,1024]{2,1,0:T(2,128)(2,1)} %reshape.234), calls=%async_computation | async-start | bytes 1048576 | tf_op jit(solution)/shard_map/all_to_all | solution.py:169
  22.0 0.0 all-gather.2.cloned.1.call-start
  22.0 0.0 copy-done.6
  22.0 0.0 copy-done.2
  22.0 0.1 compare_convert_fusion
  22.1 0.1 copy.23
  22.2 0.2 reduce_window_sum.23
  22.4 0.1 copy.24
  22.5 0.0 copy-done.5
  22.5 0.2 select_reduce_fusion
  22.7 0.1 copy.26
  22.8 0.1 reduce_sum.86.rfill_ref
  22.9 0.1 copy.28
  23.0 0.1 add.118
  23.1 0.0 copy-done.10
  23.1 0.1 broadcast_bitcast_fusion
  23.2 0.1 copy.25
  23.3 0.1 copy.31
  23.4 0.1 select_n.85.nrow_ref
  23.6 0.1 reshape_reshape.3.rreq_ref
  23.7 0.1 copy.30
  23.8 0.1 select_n.83.ntag_ref
  24.0 11.7 %all-to-all-done = bf16[128,2,1024]{2,1,0:T(2,128)(2,1)S(1)} async-done(((bf16[128,2,1024]{2,1,0:T(2,128)(2,1)}), bf16[128,2,1024]{2,1,0:T(2,128)(2,1)S(1)}, u32[]{:S(2)}, u32[]{:S(2)}) %all-to-all-start) | async-done | bytes 524320 | tf_op jit(solution)/shard_map/all_to_all | solution.py:169
  35.7 0.2 reshape.235
  35.9 4.6 %convolution_convert_fusion.q_ref.kn_ref.vn_ref = bf16[256,3072]{1,0:T(8,128)(2,1)S(1)} fusion(bf16[256,1024]{1,0:T(8,128)(2,1)S(1)} %reshape.235, bf16[1024,3072]{1,0:T(8,128)(2,1)} %param.20), kind=kOutput, calls=%fused_computation | convolution fusion | flops 1611399168 | bytes 8388608 | tf_op jit(solution)/shard_map/dot_general | solution.py:176
  40.5 19.6 %shard_map.136 = bf16[256,1024]{1,0:T(8,128)(2,1)S(1)} custom-call(bf16[256,3072]{1,0:T(8,128)(2,1)S(1)} %convolution_convert_fusion.q_ref.kn_ref.vn_ref, bf16[256,3072]{1,0:T(8,128)(2,1)S(1)} %convolution_convert_fusion.q_ref.kn_ref.vn_ref, bf16[256,3072]{1,0:T(8,128)(2,1)S(1)} %convolution_convert_fusion.q_ref.kn_ref.vn_ref, bf16[2048,1024]{1,0:T(8,128)(2,1)} %bitcast.24, ...), custom_call_target="tpu_custom_call" | custom-call | tf_op jit(solution)/shard_map/pallas_call | solution.py:98
  60.1 0.0 copy-start.1
  60.1 0.0 copy-start.7
  60.1 0.2 reshape.239
  60.4 18.0 %all_to_all.10 = bf16[128,2,1024]{2,1,0:T(2,128)(2,1)S(1)} all-to-all(bf16[128,2,1024]{2,1,0:T(2,128)(2,1)S(1)} %reshape.239), channel_id=1, replica_groups=mesh['req'=16,'mlp'=8] {'req','mlp'}, dimensions={0} | all-to-all | bytes 1048576 | tf_op jit(solution)/shard_map/all_to_all | solution.py:183
  78.3 0.2 reshape.240
  78.5 0.0 copy-done
  78.5 0.0 copy-done.1
  78.5 0.0 copy-done.7
  78.6 0.0 copy-start.3
  78.6 0.0 copy-start.4
  78.6 0.7 fusion.81
  79.3 0.2 multiply_reduce_fusion.1
  79.5 0.0 copy-done.3
  79.5 0.0 copy-done.4
  79.5 0.9 add_convert_fusion.1
  80.4 0.0 all-gather.2.cloned.1.call-update
  80.4 0.2 reduce-scatter.2.cloned.1.call-start
  80.6 21.0 %all-gather.2.cloned.1.call-done = bf16[1024,1024]{1,0:T(8,128)(2,1)} async-done(((bf16[128,1024]{1,0:T(8,128)(2,1)}), bf16[1024,1024]{1,0:T(8,128)(2,1)}) %all-gather.2.cloned.1.call-update) | async-done | bytes 2097168 | tf_op jit(solution)/shard_map/all_gather | solution.py:197
  101.7 9.7 %convolution_convert_fusion.1 = bf16[1024,1024]{1,0:T(8,128)(2,1)} fusion(bf16[512,1024]{1,0:T(8,128)(2,1)} %param.23, bf16[1024,1024]{1,0:T(8,128)(2,1)} %all-gather.2.cloned.1.call-done, bf16[1024,512]{1,0:T(8,128)(2,1)} %param.22), kind=kOutput, calls=%fused_computation.20 | convolution fusion | flops 2182610944 | bytes 6291456 | tf_op jit(solution)/shard_map/dot_general | solution.py:202
  111.4 0.0 reduce-scatter.2.cloned.1.call-update
  111.4 34.3 %reduce-scatter.2.cloned.1.call-done = bf16[128,1024]{1,0:T(8,128)(2,1)} async-done(((bf16[1024,1024]{1,0:T(8,128)(2,1)}), bf16[128,1024]{1,0:T(8,128)(2,1)}) %reduce-scatter.2.cloned.1.call-update) | async-done | bytes 262160 | tf_op jit(solution)/shard_map/reduce_scatter | solution.py:201
  145.7 1.2 fusion.42
  146.9 1.3 multiply_reduce_fusion
  148.2 0.0 copy-done.8
  148.2 0.0 copy-done.9
  148.2 1.9 %add_convert_fusion = bf16[128,1024]{1,0:T(8,128)(2,1)} fusion(bf16[128,1024]{1,0:T(8,128)(2,1)} %reduce-scatter.2.cloned.1.call-done, f32[1024]{0:T(1024)S(1)} %copy-done.8, f32[1024]{0:T(1024)S(1)} %copy-done.9, f32[128]{0:T(128)S(1)} %add_rsqrt_fusion, f32[128]{0:T(128)S(1)} %broadcast_multiply_fusion, f32[1024]{0:T(1024)S(1)} %copy-done.3, ...), kind=kLoop, calls=%fused_computation.54 | loop fusion | flops 1703936 | bytes 1067008 | tf_op jit(solution)/shard_map/convert_element_type | solution.py:207
  (12 shorter events, 0.1 us)
Async XLA Ops:
  6.5 72.0 %copy-start = (bf16[1024,1024]{1,0:T(8,128)(2,1)S(1)}, bf16[1024,1024]{1,0:T(8,128)(2,1)}, u32[]{:S(2)}) copy-start(bf16[1024,1024]{1,0:T(8,128)(2,1)} %param.21) | copy-start | bytes 6291460
  6.5 15.5 %copy-start.2 = (s32[16384,1]{0,1:T(1,128)S(1)}, s32[16384,1]{0,1:T(1,128)}, u32[]{:S(2)}) copy-start(s32[16384,1]{0,1:T(1,128)} %param.15) | copy-start | bytes 196612
  6.5 16.0 %copy-start.5 = (s32[16384]{0:T(1024)S(1)}, s32[16384]{0:T(1024)}, u32[]{:S(2)}) copy-start(s32[16384]{0:T(1024)} %param.16) | copy-start | bytes 196612
  8.5 13.6 %copy-start.6 = (s32[128]{0:T(128)}, s32[128]{0:T(128)S(1)}, u32[]{:S(2)}) copy-start(s32[128]{0:T(128)S(1)} %fusion.49) | copy-start | bytes 1540
  9.8 13.3 %copy-start.10 = (s32[4]{0:T(128)S(1)}, s32[4]{0:T(128)}, u32[]{:S(2)}) copy-start(s32[4]{0:T(128)} %param.17) | copy-start | bytes 52
  10.8 24.9 %all-to-all-start = ((bf16[128,2,1024]{2,1,0:T(2,128)(2,1)}), bf16[128,2,1024]{2,1,0:T(2,128)(2,1)S(1)}, u32[]{:S(2)}, u32[]{:S(2)}) async-start(bf16[128,2,1024]{2,1,0:T(2,128)(2,1)} %reshape.234), calls=%async_computation | async-start | bytes 1048576 | tf_op jit(solution)/shard_map/all_to_all | solution.py:169
  22.0 79.7 %all-gather.2.cloned.1.call-start = ((), (), s32[]{:S(2)}) async-start(), calls=%async_computation.3 | async-start | bytes 2359296 | tf_op jit(solution)/shard_map/all_gather | solution.py:197
  60.1 18.4 %copy-start.1 = (bf16[128,1024]{1,0:T(8,128)(2,1)S(1)}, bf16[128,1024]{1,0:T(8,128)(2,1)}, u32[]{:S(2)}) copy-start(bf16[128,1024]{1,0:T(8,128)(2,1)} %param.14) | copy-start | bytes 786436
  60.1 18.4 %copy-start.7 = (s32[128]{0:T(128)S(1)}, s32[128]{0:T(128)}, u32[]{:S(2)}) copy-start(s32[128]{0:T(128)} %copy-done.6) | copy-start | bytes 1540
  78.6 0.9 copy-start.3
  78.6 0.9 copy-start.4
  80.4 65.3 %reduce-scatter.2.cloned.1.call-start = ((), (), s32[]{:S(2)}) async-start(), calls=%async_computation.4 | async-start | bytes 2359296 | tf_op jit(solution)/shard_map/reduce_scatter | solution.py:201
  111.4 36.8 %copy-start.8 = (f32[1024]{0:T(1024)S(1)}, f32[1024]{0:T(1024)}, u32[]{:S(2)}) copy-start(f32[1024]{0:T(1024)} %param.27) | copy-start | bytes 12292
  111.4 36.8 %copy-start.9 = (f32[1024]{0:T(1024)S(1)}, f32[1024]{0:T(1024)}, u32[]{:S(2)}) copy-start(f32[1024]{0:T(1024)} %param.26) | copy-start | bytes 12292
Sparse Core Ops, SparseCore 0:
  80.5 21.1 all-gather.1
  111.5 34.1 reduce-scatter.1

commit v2 on v1

--- a/solution.py
+++ b/solution.py
@@ -1,3 +1,5 @@
+import functools
+
 import jax
 import jax.numpy as jnp
 from jax import lax
@@ -129,6 +131,56 @@
     )
 
 
+def exchange_kernel(groups, x_ref, o_ref, send_sem, recv_sem, local_sem):
+    n = x_ref.shape[0]
+    me = lax.axis_index("req") * groups + lax.axis_index("mlp")
+
+    def remote(k):
+        peer = lax.rem(me + k, n)
+        return pltpu.make_async_remote_copy(
+            src_ref=x_ref.at[peer],
+            dst_ref=o_ref.at[me],
+            send_sem=send_sem.at[k],
+            recv_sem=recv_sem.at[k],
+            device_id=(peer // groups, lax.rem(peer, groups)),
+            device_id_type=pl.DeviceIdType.MESH,
+        )
+
+    own = pltpu.make_async_copy(x_ref.at[me], o_ref.at[me], local_sem)
+    own.start()
+
+    def start(k, carry):
+        remote(k).start()
+        return carry
+
+    def finish(k, carry):
+        copy = remote(k)
+        copy.wait_send()
+        copy.wait_recv()
+        return carry
+
+    lax.fori_loop(1, n, start, 0)
+    own.wait()
+    lax.fori_loop(1, n, finish, 0)
+
+
+def exchange(blocks):
+    n = blocks.shape[0]
+    groups = lax.axis_size("mlp")
+    return pl.pallas_call(
+        functools.partial(exchange_kernel, groups),
+        in_specs=[pl.BlockSpec(memory_space=pl.ANY)],
+        out_specs=pl.BlockSpec(memory_space=pl.ANY),
+        out_shape=jax.ShapeDtypeStruct(blocks.shape, blocks.dtype),
+        scratch_shapes=[
+            pltpu.SemaphoreType.DMA((n,)),
+            pltpu.SemaphoreType.DMA((n,)),
+            pltpu.SemaphoreType.DMA(()),
+        ],
+        compiler_params=pltpu.CompilerParams(has_side_effects=True),
+    )(blocks)
+
+
 def per_device(
     tokens,
     token_owner,
@@ -166,13 +218,7 @@
     outgoing = jnp.einsum("tr,td->rd", dispatch, tokens, preferred_element_type=jnp.float32).astype(
         jnp.bfloat16
     )
-    arrived = lax.all_to_all(
-        outgoing.reshape(devices, capacity, width),
-        ("req", "mlp"),
-        split_axis=0,
-        concat_axis=0,
-        tiled=True,
-    )
+    arrived = exchange(outgoing.reshape(devices, capacity, width))
     projections = jnp.dot(
         arrived.reshape(slot_count, width), w_qkv, preferred_element_type=jnp.float32
     ).astype(jnp.bfloat16)
@@ -180,13 +226,7 @@
         owners_flat, token_request, owner_index, devices, tok_dev, capacity
     )
     attended = attend(projections, cache_k, cache_v, cache_len, global_row, slot_request, filled)
-    returned = lax.all_to_all(
-        attended.reshape(devices, capacity, width),
-        ("req", "mlp"),
-        split_axis=0,
-        concat_axis=0,
-        tiled=True,
-    )
+    returned = exchange(attended.reshape(devices, capacity, width))
     attn_rows = jnp.dot(
         dispatch, returned.reshape(slot_count, width), preferred_element_type=jnp.float32
     ).astype(jnp.bfloat16)

time: 157 us -> 170 us (1.083)
  Pallas kernels: 19.6 us -> 66.5 us
  blocking collectives: 18 us -> 0 us
  starting transfers between devices: 11.4 us -> 0.22 us
  waiting for transfers between devices: 67.1 us -> 57.5 us
  local copies, waits for them, and re-layouts: 3.79 us -> 7.15 us
  other arithmetic: 7.06 us -> 8.91 us
    pallas_call x0 -> x2, Pallas kernels: none -> 47 us  [exchange(): pl.pallas_call(functools.partial(exchange_kernel, groups), in_specs=[pl.B...]
    all_to_all x1 -> x0, blocking collectives: 18 us -> none  [per_device(): lax.all_to_all(attended.reshape(devices, capacity, width), ('req', 'mlp')...]
    all_to_all x1 -> x0, waiting for transfers between devices: 11.7 us -> none  [per_device(): lax.all_to_all(outgoing.reshape(devices, capacity, width), ('req', 'mlp')...]
    all_to_all x1 -> x0, starting transfers between devices: 11.1 us -> none  [per_device(): lax.all_to_all(outgoing.reshape(devices, capacity, width), ('req', 'mlp')...]
    all_gather x1, waiting for transfers between devices: 21 us -> 23.2 us  [per_device(): gathered = lax.all_gather(normed, 'mlp', axis=0, tiled=True)]
  transfers between devices with their start and end apart: 3 -> 2, of which waited for: 3 -> 2; matrix products, arithmetic and copies ran while one was open for 1% -> 0% of each run, Pallas kernels for 0% -> 0%
where the time goes in v2:
time: 170 us; the launch traced here: 169 us
  Pallas kernels  66.5 us (39%)
  waiting for transfers between devices  57.5 us (34%)
  matrix products  15.4 us (9%)
  between operations  13.6 us (8%)
  other arithmetic  8.91 us (5%)
  local copies, waits for them, and re-layouts  7.15 us (4%)
    pallas_call x2, Pallas kernels, exchange(): pl.pallas_call(functools.partial(exchange_kernel, groups), in_specs=[pl.B...  47 us
    reduce_scatter x1, waiting for transfers between devices, per_device(): lax.psum_scatter(jnp.dot(hidden, w_fc2, preferred_element_type=jnp.float3...  34.3 us
    all_gather x1, waiting for transfers between devices, per_device(): gathered = lax.all_gather(normed, 'mlp', axis=0, tiled=True)  23.2 us
    pallas_call x1, Pallas kernels, attend(): pl.pallas_call(attention_kernel, grid=(pairs,), in_specs=[pl.BlockSpec((s...  19.5 us
    dot_general x1, matrix products, per_device(): jnp.dot(hidden, w_fc2, preferred_element_type=jnp.float32)  9.68 us
    dot_general x1, matrix products, per_device(): jnp.dot(arrived.reshape(slot_count, width), w_qkv, preferred_element_type...  4.6 us
  transfers between devices with their start and end apart: 2, of which 2 were waited for; matrix products, arithmetic and copies ran while one was open for 0% of the time, Pallas kernels for 0%

profile of v2, /device:TPU:0, one launch (start us, length us, event | category | flops | bytes accessed | tf_op | source)
XLA Modules:
  0.0 169.3 jit_solution(5165002575610033107)
XLA Ops:
  6.5 0.0 copy-start
  6.5 0.0 copy-start.1
  6.5 0.0 all-gather.2.cloned.1.call-start
  6.6 1.1 compare_convert_fusion
  7.6 0.7 fusion.50
  8.3 0.7 broadcast_bitcast_fusion
  9.0 0.1 copy.23
  9.1 0.2 reduce_window_sum.23
  9.3 0.1 copy.24
  9.4 1.0 select_reduce_fusion
  10.4 0.1 copy.25
  10.6 0.1 copy.26
  10.7 0.1 copy.31
  10.8 0.1 select_n.85.nrow_ref
  10.9 0.1 reduce_sum.86.rfill_ref
  11.0 0.1 reshape_reshape.3.rreq_ref
  11.1 0.1 copy.28
  11.2 0.1 add.118
  11.3 0.1 copy.30
  11.4 0.1 select_n.83.ntag_ref
  11.6 0.1 fusion.48
  11.7 0.2 reduce_window_sum.22
  11.8 0.2 select_reduce_fusion.1
  12.0 0.7 fusion.49
  12.7 0.0 copy-done.1
  12.7 0.4 convolution_convert_fusion.2
  13.1 1.0 reshape.234.x_ref
  14.1 25.8 %shard_map.136 = bf16[128,2,1024]{2,1,0:T(2,128)(2,1)} custom-call(bf16[128,2,1024]{2,1,0:T(2,128)(2,1)} %reshape.234.x_ref), custom_call_target="tpu_custom_call" | custom-call | tf_op jit(solution)/shard_map/pallas_call | solution.py:170
  39.9 1.2 reshape.235
  41.1 4.6 %convolution_convert_fusion.q_ref.kn_ref.vn_ref = bf16[256,3072]{1,0:T(8,128)(2,1)S(1)} fusion(bf16[256,1024]{1,0:T(8,128)(2,1)S(1)} %reshape.235, bf16[1024,3072]{1,0:T(8,128)(2,1)} %param.20), kind=kOutput, calls=%fused_computation | convolution fusion | flops 1611399168 | bytes 8388608 | tf_op jit(solution)/shard_map/dot_general | solution.py:222
  45.7 19.5 %shard_map.137 = bf16[256,1024]{1,0:T(8,128)(2,1)S(1)} custom-call(bf16[256,3072]{1,0:T(8,128)(2,1)S(1)} %convolution_convert_fusion.q_ref.kn_ref.vn_ref, bf16[256,3072]{1,0:T(8,128)(2,1)S(1)} %convolution_convert_fusion.q_ref.kn_ref.vn_ref, bf16[256,3072]{1,0:T(8,128)(2,1)S(1)} %convolution_convert_fusion.q_ref.kn_ref.vn_ref, bf16[2048,1024]{1,0:T(8,128)(2,1)} %bitcast.24, ...), custom_call_target="tpu_custom_call" | custom-call | tf_op jit(solution)/shard_map/pallas_call | solution.py:100
  65.2 1.0 reshape.239.x_ref
  66.2 21.3 %shard_map.138 = bf16[128,2,1024]{2,1,0:T(2,128)(2,1)} custom-call(bf16[128,2,1024]{2,1,0:T(2,128)(2,1)} %reshape.239.x_ref), custom_call_target="tpu_custom_call" | custom-call | tf_op jit(solution)/shard_map/pallas_call | solution.py:170
  87.5 1.2 reshape.240
  88.7 0.0 copy-done
  88.7 0.0 copy-start.2
  88.8 0.0 copy-start.3
  88.8 0.7 fusion.81
  89.5 0.2 multiply_reduce_fusion.1
  89.7 0.0 copy-done.2
  89.7 0.0 copy-done.3
  89.7 0.9 add_convert_fusion.1
  90.6 0.0 all-gather.2.cloned.1.call-update
  90.6 0.2 reduce-scatter.2.cloned.1.call-start
  90.8 23.2 %all-gather.2.cloned.1.call-done = bf16[1024,1024]{1,0:T(8,128)(2,1)} async-done(((bf16[128,1024]{1,0:T(8,128)(2,1)}), bf16[1024,1024]{1,0:T(8,128)(2,1)}) %all-gather.2.cloned.1.call-update) | async-done | bytes 2097168 | tf_op jit(solution)/shard_map/all_gather | solution.py:237
  114.0 9.7 %convolution_convert_fusion.1 = bf16[1024,1024]{1,0:T(8,128)(2,1)} fusion(bf16[512,1024]{1,0:T(8,128)(2,1)} %param.23, bf16[1024,1024]{1,0:T(8,128)(2,1)} %all-gather.2.cloned.1.call-done, bf16[1024,512]{1,0:T(8,128)(2,1)} %param.22), kind=kOutput, calls=%fused_computation.20 | convolution fusion | flops 2182610944 | bytes 6291456 | tf_op jit(solution)/shard_map/dot_general | solution.py:242
  123.7 0.0 copy-start.4
  123.7 0.0 copy-start.5
  123.7 0.0 reduce-scatter.2.cloned.1.call-update
  123.7 34.3 %reduce-scatter.2.cloned.1.call-done = bf16[128,1024]{1,0:T(8,128)(2,1)} async-done(((bf16[1024,1024]{1,0:T(8,128)(2,1)}), bf16[128,1024]{1,0:T(8,128)(2,1)}) %reduce-scatter.2.cloned.1.call-update) | async-done | bytes 262160 | tf_op jit(solution)/shard_map/reduce_scatter | solution.py:241
  158.0 1.2 fusion.42
  159.3 1.3 multiply_reduce_fusion
  160.5 0.0 copy-done.4
  160.5 0.0 copy-done.5
  160.6 1.9 %add_convert_fusion = bf16[128,1024]{1,0:T(8,128)(2,1)} fusion(bf16[128,1024]{1,0:T(8,128)(2,1)} %reduce-scatter.2.cloned.1.call-done, f32[1024]{0:T(1024)S(1)} %copy-done.4, f32[1024]{0:T(1024)S(1)} %copy-done.5, f32[128]{0:T(128)S(1)} %add_rsqrt_fusion, f32[128]{0:T(128)S(1)} %broadcast_multiply_fusion, f32[1024]{0:T(1024)S(1)} %copy-done.2, ...), kind=kLoop, calls=%fused_computation.54 | loop fusion | flops 1703936 | bytes 1067008 | tf_op jit(solution)/shard_map/convert_element_type | solution.py:247
  (10 shorter events, 0.1 us)
Async XLA Ops:
  6.5 82.2 %copy-start = (bf16[1024,1024]{1,0:T(8,128)(2,1)S(1)}, bf16[1024,1024]{1,0:T(8,128)(2,1)}, u32[]{:S(2)}) copy-start(bf16[1024,1024]{1,0:T(8,128)(2,1)} %param.21) | copy-start | bytes 6291460
  6.5 6.2 %copy-start.1 = (bf16[128,1024]{1,0:T(8,128)(2,1)S(1)}, bf16[128,1024]{1,0:T(8,128)(2,1)}, u32[]{:S(2)}) copy-start(bf16[128,1024]{1,0:T(8,128)(2,1)} %param.14) | copy-start | bytes 786436
  6.5 107.5 %all-gather.2.cloned.1.call-start = ((), (), s32[]{:S(2)}) async-start(), calls=%async_computation.1 | async-start | bytes 2359296 | tf_op jit(solution)/shard_map/all_gather | solution.py:237
  88.7 0.9 copy-start.2
  88.8 0.9 copy-start.3
  90.6 67.4 %reduce-scatter.2.cloned.1.call-start = ((), (), s32[]{:S(2)}) async-start(), calls=%async_computation.2 | async-start | bytes 2359296 | tf_op jit(solution)/shard_map/reduce_scatter | solution.py:241
  123.7 36.8 %copy-start.4 = (f32[1024]{0:T(1024)S(1)}, f32[1024]{0:T(1024)}, u32[]{:S(2)}) copy-start(f32[1024]{0:T(1024)} %param.27) | copy-start | bytes 12292
  123.7 36.8 %copy-start.5 = (f32[1024]{0:T(1024)S(1)}, f32[1024]{0:T(1024)}, u32[]{:S(2)}) copy-start(f32[1024]{0:T(1024)} %param.26) | copy-start | bytes 12292
Sparse Core Ops, SparseCore 0:
  90.7 23.2 all-gather.1
  123.8 34.1 reduce-scatter.1

commit v3 on v1

--- a/solution.py
+++ b/solution.py
@@ -129,6 +129,17 @@
     )
 
 
+def exchange(blocks):
+    n_req = lax.axis_size("req")
+    n_mlp = lax.axis_size("mlp")
+    rest = blocks.shape[1:]
+    staged = blocks.reshape((n_req, n_mlp) + rest).swapaxes(0, 1)
+    staged = lax.all_to_all(staged, "mlp", split_axis=0, concat_axis=0, tiled=True)
+    staged = staged.swapaxes(0, 1)
+    staged = lax.all_to_all(staged, "req", split_axis=0, concat_axis=0, tiled=True)
+    return staged.reshape(blocks.shape)
+
+
 def per_device(
     tokens,
     token_owner,
@@ -166,13 +177,7 @@
     outgoing = jnp.einsum("tr,td->rd", dispatch, tokens, preferred_element_type=jnp.float32).astype(
         jnp.bfloat16
     )
-    arrived = lax.all_to_all(
-        outgoing.reshape(devices, capacity, width),
-        ("req", "mlp"),
-        split_axis=0,
-        concat_axis=0,
-        tiled=True,
-    )
+    arrived = exchange(outgoing.reshape(devices, capacity, width))
     projections = jnp.dot(
         arrived.reshape(slot_count, width), w_qkv, preferred_element_type=jnp.float32
     ).astype(jnp.bfloat16)
@@ -180,13 +185,7 @@
         owners_flat, token_request, owner_index, devices, tok_dev, capacity
     )
     attended = attend(projections, cache_k, cache_v, cache_len, global_row, slot_request, filled)
-    returned = lax.all_to_all(
-        attended.reshape(devices, capacity, width),
-        ("req", "mlp"),
-        split_axis=0,
-        concat_axis=0,
-        tiled=True,
-    )
+    returned = exchange(attended.reshape(devices, capacity, width))
     attn_rows = jnp.dot(
         dispatch, returned.reshape(slot_count, width), preferred_element_type=jnp.float32
     ).astype(jnp.bfloat16)

time: 157 us -> 179 us (1.14)
  blocking collectives: 18 us -> 27 us
  waiting for transfers between devices: 67.1 us -> 75 us
  local copies, waits for them, and re-layouts: 3.79 us -> 6.83 us
    all_to_all x1 -> x2, blocking collectives: 18 us -> 27 us  [the longest x1 14.1 us: exchange(): lax.all_to_all(staged, 'req', split_axis=0, concat_axis=0, tiled=True)]
    all_to_all x1 -> x2, waiting for transfers between devices: 11.7 us -> 19.7 us  [the longest x1 10.5 us: exchange(): lax.all_to_all(staged, 'req', split_axis=0, concat_axis=0, tiled=True)]
    another operation x0 -> x6, local copies, waits for them, and re-layouts: none -> 2.35 us  [the longest x4 1.95 us: exchange(): staged = blocks.reshape((n_req, n_mlp) + rest).swapaxes(0, 1)]
    all_to_all x1 -> x2, starting transfers between devices: 11.1 us -> 12.4 us  [the longest x1 7.03 us: exchange(): lax.all_to_all(staged, 'req', split_axis=0, concat_axis=0, tiled=True)]
  transfers between devices with their start and end apart: 3 -> 4, of which waited for: 3 -> 4; matrix products, arithmetic and copies ran while one was open for 1% -> 1% of each run, Pallas kernels for 0% -> 0%
where the time goes in v3:
time: 179 us; the launch traced here: 178 us
  waiting for transfers between devices  75 us (42%)
  blocking collectives  27 us (15%)
  Pallas kernels  19.7 us (11%)
  matrix products  16.3 us (9%)
  between operations  13.7 us (8%)
  starting transfers between devices  12.7 us (7%)
  other arithmetic  7.06 us (4%)
  local copies, waits for them, and re-layouts  6.83 us (4%)
    reduce_scatter x1, waiting for transfers between devices, per_device(): lax.psum_scatter(jnp.dot(hidden, w_fc2, preferred_element_type=jnp.float3...  34.3 us
    all_gather x1, waiting for transfers between devices, per_device(): gathered = lax.all_gather(normed, 'mlp', axis=0, tiled=True)  20.9 us
    pallas_call x1, Pallas kernels, attend(): pl.pallas_call(attention_kernel, grid=(pairs,), in_specs=[pl.BlockSpec((s...  19.7 us
    all_to_all x1, blocking collectives, exchange(): lax.all_to_all(staged, 'req', split_axis=0, concat_axis=0, tiled=True)  14.1 us
    all_to_all x1, blocking collectives, exchange(): lax.all_to_all(staged, 'mlp', split_axis=0, concat_axis=0, tiled=True)  12.9 us
    all_to_all x1, waiting for transfers between devices, exchange(): lax.all_to_all(staged, 'req', split_axis=0, concat_axis=0, tiled=True)  10.5 us
    dot_general x1, matrix products, per_device(): jnp.dot(hidden, w_fc2, preferred_element_type=jnp.float32)  9.68 us
    all_to_all x1, waiting for transfers between devices, exchange(): lax.all_to_all(staged, 'mlp', split_axis=0, concat_axis=0, tiled=True)  9.24 us
  transfers between devices with their start and end apart: 4, of which 4 were waited for; matrix products, arithmetic and copies ran while one was open for 1% of the time, Pallas kernels for 0%

profile of v3, /device:TPU:0, one launch (start us, length us, event | category | flops | bytes accessed | tf_op | source)
XLA Modules:
  0.0 178.3 jit_solution(17415937202963111384)
XLA Ops:
  6.5 0.0 copy-start
  6.5 0.8 fusion.50
  7.3 0.1 fusion.48
  7.4 0.2 reduce_window_sum.22
  7.6 0.2 select_reduce_fusion.1
  7.8 0.7 fusion.49
  8.5 0.5 copy-done.6
  9.0 1.3 convolution_convert_fusion.2
  10.3 0.0 copy-start.5
  10.3 0.2 reshape_reshape.19
  10.5 1.2 copy.70
  11.7 5.4 %all-to-all-start = ((bf16[8,16,2,1024]{3,2,1,0:T(2,128)(2,1)}), bf16[8,16,2,1024]{3,2,1,0:T(2,128)(2,1)S(1)}, u32[]{:S(2)}, u32[]{:S(2)}) async-start(bf16[8,16,2,1024]{3,2,1,0:T(2,128)(2,1)} %bitcast.31), calls=%async_computation | async-start | bytes 1048576 | tf_op jit(solution)/shard_map/all_to_all | solution.py:137
  17.1 0.0 copy-done.2
  17.1 0.0 copy-start.10
  17.1 0.1 compare_convert_fusion
  17.2 0.1 copy.53
  17.3 0.2 reduce_window_sum.23
  17.5 0.1 copy.54
  17.6 0.0 copy-done.5
  17.6 0.2 select_reduce_fusion
  17.8 0.1 copy.56
  17.9 0.1 reduce_sum.86.rfill_ref
  18.0 0.1 copy.58
  18.1 0.1 add.118
  18.2 9.2 %all-to-all-done = bf16[8,16,2,1024]{3,2,1,0:T(2,128)(2,1)S(1)} async-done(((bf16[8,16,2,1024]{3,2,1,0:T(2,128)(2,1)}), bf16[8,16,2,1024]{3,2,1,0:T(2,128)(2,1)S(1)}, u32[]{:S(2)}, u32[]{:S(2)}) %all-to-all-start) | async-done | bytes 524320 | tf_op jit(solution)/shard_map/all_to_all | solution.py:137
  27.5 1.3 copy.52
  28.8 7.0 %all-to-all-start.1 = ((bf16[16,8,2,1024]{3,2,1,0:T(2,128)(2,1)}), bf16[16,8,2,1024]{3,2,1,0:T(2,128)(2,1)S(1)}, u32[]{:S(2)}, u32[]{:S(2)}) async-start(bf16[16,8,2,1024]{3,2,1,0:T(2,128)(2,1)} %copy.52), calls=%async_computation.1 | async-start | bytes 1048576 | tf_op jit(solution)/shard_map/all_to_all | solution.py:139
  35.8 0.0 all-gather.2.cloned.1.call-start
  35.9 0.1 broadcast_bitcast_fusion
  35.9 0.1 copy.55
  36.1 0.1 copy.61
  36.2 0.1 select_n.85.nrow_ref
  36.3 0.1 reshape_reshape.24.rreq_ref
  36.4 0.1 copy.60
  36.5 0.1 select_n.83.ntag_ref
  36.7 10.5 %all-to-all-done.1 = bf16[16,8,2,1024]{3,2,1,0:T(2,128)(2,1)S(1)} async-done(((bf16[16,8,2,1024]{3,2,1,0:T(2,128)(2,1)}), bf16[16,8,2,1024]{3,2,1,0:T(2,128)(2,1)S(1)}, u32[]{:S(2)}, u32[]{:S(2)}) %all-to-all-start.1) | async-done | bytes 524320 | tf_op jit(solution)/shard_map/all_to_all | solution.py:139
  47.1 0.2 reshape_reshape.20
  47.4 4.6 %convolution_convert_fusion.q_ref.kn_ref.vn_ref = bf16[256,3072]{1,0:T(8,128)(2,1)S(1)} fusion(bf16[256,1024]{1,0:T(8,128)(2,1)S(1)} %reshape_reshape.20, bf16[1024,3072]{1,0:T(8,128)(2,1)} %param.20), kind=kOutput, calls=%fused_computation | convolution fusion | flops 1611399168 | bytes 8388608 | tf_op jit(solution)/shard_map/dot_general | solution.py:181
  51.9 19.7 %shard_map.136 = bf16[256,1024]{1,0:T(8,128)(2,1)S(1)} custom-call(bf16[256,3072]{1,0:T(8,128)(2,1)S(1)} %convolution_convert_fusion.q_ref.kn_ref.vn_ref, bf16[256,3072]{1,0:T(8,128)(2,1)S(1)} %convolution_convert_fusion.q_ref.kn_ref.vn_ref, bf16[256,3072]{1,0:T(8,128)(2,1)S(1)} %convolution_convert_fusion.q_ref.kn_ref.vn_ref, bf16[2048,1024]{1,0:T(8,128)(2,1)} %bitcast.32, ...), custom_call_target="tpu_custom_call" | custom-call | tf_op jit(solution)/shard_map/pallas_call | solution.py:98
  71.6 0.2 reshape_reshape.22
  71.8 0.4 copy.69
  72.2 0.0 copy-start.1
  72.2 0.0 copy-start.7
  72.2 12.9 %all_to_all.20 = bf16[8,16,2,1024]{3,2,1,0:T(2,128)(2,1)S(1)} all-to-all(bf16[8,16,2,1024]{3,2,1,0:T(2,128)(2,1)S(1)} %bitcast.35), channel_id=1, replica_groups=mesh['req'=16,'mlp'=8] {'mlp'}, dimensions={0} | all-to-all | bytes 1048576 | tf_op jit(solution)/shard_map/all_to_all | solution.py:137
  85.2 0.5 copy.65
  85.6 14.1 %all_to_all.21 = bf16[16,8,2,1024]{3,2,1,0:T(2,128)(2,1)S(1)} all-to-all(bf16[16,8,2,1024]{3,2,1,0:T(2,128)(2,1)S(1)} %copy.65), channel_id=1, replica_groups=mesh['req'=16,'mlp'=8] {'req'}, dimensions={0} | all-to-all | bytes 1048576 | tf_op jit(solution)/shard_map/all_to_all | solution.py:139
  99.7 0.2 reshape_reshape.23
  100.0 0.0 copy-start.3
  100.0 0.0 copy-start.4
  100.0 0.7 fusion.81
  100.7 0.2 multiply_reduce_fusion.1
  100.9 0.0 copy-done.3
  100.9 0.9 add_convert_fusion.1
  101.8 0.0 all-gather.2.cloned.1.call-update
  101.8 0.2 reduce-scatter.2.cloned.1.call-start
  102.0 20.9 %all-gather.2.cloned.1.call-done = bf16[1024,1024]{1,0:T(8,128)(2,1)} async-done(((bf16[128,1024]{1,0:T(8,128)(2,1)}), bf16[1024,1024]{1,0:T(8,128)(2,1)}) %all-gather.2.cloned.1.call-update) | async-done | bytes 2097168 | tf_op jit(solution)/shard_map/all_gather | solution.py:196
  123.0 9.7 %convolution_convert_fusion.1 = bf16[1024,1024]{1,0:T(8,128)(2,1)} fusion(bf16[512,1024]{1,0:T(8,128)(2,1)} %param.23, bf16[1024,1024]{1,0:T(8,128)(2,1)} %all-gather.2.cloned.1.call-done, bf16[1024,512]{1,0:T(8,128)(2,1)} %param.22), kind=kOutput, calls=%fused_computation.20 | convolution fusion | flops 2182610944 | bytes 6291456 | tf_op jit(solution)/shard_map/dot_general | solution.py:201
  132.7 0.0 reduce-scatter.2.cloned.1.call-update
  132.7 34.3 %reduce-scatter.2.cloned.1.call-done = bf16[128,1024]{1,0:T(8,128)(2,1)} async-done(((bf16[1024,1024]{1,0:T(8,128)(2,1)}), bf16[128,1024]{1,0:T(8,128)(2,1)}) %reduce-scatter.2.cloned.1.call-update) | async-done | bytes 262160 | tf_op jit(solution)/shard_map/reduce_scatter | solution.py:200
  167.0 1.2 fusion.42
  168.2 1.3 multiply_reduce_fusion
  169.5 0.0 copy-done.8
  169.5 0.0 copy-done.9
  169.5 1.9 %add_convert_fusion = bf16[128,1024]{1,0:T(8,128)(2,1)} fusion(bf16[128,1024]{1,0:T(8,128)(2,1)} %reduce-scatter.2.cloned.1.call-done, f32[1024]{0:T(1024)S(1)} %copy-done.8, f32[1024]{0:T(1024)S(1)} %copy-done.9, f32[128]{0:T(128)S(1)} %add_rsqrt_fusion, f32[128]{0:T(128)S(1)} %broadcast_multiply_fusion, f32[1024]{0:T(1024)S(1)} %copy-done.3, ...), kind=kLoop, calls=%fused_computation.56 | loop fusion | flops 1703936 | bytes 1067008 | tf_op jit(solution)/shard_map/convert_element_type | solution.py:206
  (19 shorter events, 0.1 us)
Async XLA Ops:
  6.5 93.4 %copy-start = (bf16[1024,1024]{1,0:T(8,128)(2,1)S(1)}, bf16[1024,1024]{1,0:T(8,128)(2,1)}, u32[]{:S(2)}) copy-start(bf16[1024,1024]{1,0:T(8,128)(2,1)} %param.21) | copy-start | bytes 6291460
  7.3 9.8 %copy-start.2 = (s32[16384,1]{0,1:T(1,128)S(1)}, s32[16384,1]{0,1:T(1,128)}, u32[]{:S(2)}) copy-start(s32[16384,1]{0,1:T(1,128)} %param.15) | copy-start | bytes 196612
  8.4 0.5 copy-start.6
  10.3 7.3 %copy-start.5 = (s32[16384]{0:T(1024)S(1)}, s32[16384]{0:T(1024)}, u32[]{:S(2)}) copy-start(s32[16384]{0:T(1024)} %param.16) | copy-start | bytes 196612
  11.7 15.7 %all-to-all-start = ((bf16[8,16,2,1024]{3,2,1,0:T(2,128)(2,1)}), bf16[8,16,2,1024]{3,2,1,0:T(2,128)(2,1)S(1)}, u32[]{:S(2)}, u32[]{:S(2)}) async-start(bf16[8,16,2,1024]{3,2,1,0:T(2,128)(2,1)} %bitcast.31), calls=%async_computation | async-start | bytes 1048576 | tf_op jit(solution)/shard_map/all_to_all | solution.py:137
  17.1 18.7 %copy-start.10 = (s32[4]{0:T(128)S(1)}, s32[4]{0:T(128)}, u32[]{:S(2)}) copy-start(s32[4]{0:T(128)} %param.17) | copy-start | bytes 52
  28.8 18.4 %all-to-all-start.1 = ((bf16[16,8,2,1024]{3,2,1,0:T(2,128)(2,1)}), bf16[16,8,2,1024]{3,2,1,0:T(2,128)(2,1)S(1)}, u32[]{:S(2)}, u32[]{:S(2)}) async-start(bf16[16,8,2,1024]{3,2,1,0:T(2,128)(2,1)} %copy.52), calls=%async_computation.1 | async-start | bytes 1048576 | tf_op jit(solution)/shard_map/all_to_all | solution.py:139
  35.8 87.2 %all-gather.2.cloned.1.call-start = ((), (), s32[]{:S(2)}) async-start(), calls=%async_computation.5 | async-start | bytes 2359296 | tf_op jit(solution)/shard_map/all_gather | solution.py:196
  72.2 27.8 %copy-start.1 = (bf16[128,1024]{1,0:T(8,128)(2,1)S(1)}, bf16[128,1024]{1,0:T(8,128)(2,1)}, u32[]{:S(2)}) copy-start(bf16[128,1024]{1,0:T(8,128)(2,1)} %param.14) | copy-start | bytes 786436
  72.2 27.8 %copy-start.7 = (s32[128]{0:T(128)S(1)}, s32[128]{0:T(128)}, u32[]{:S(2)}) copy-start(s32[128]{0:T(128)} %copy-done.6) | copy-start | bytes 1540
  100.0 0.9 copy-start.3
  100.0 0.9 copy-start.4
  101.8 65.2 %reduce-scatter.2.cloned.1.call-start = ((), (), s32[]{:S(2)}) async-start(), calls=%async_computation.6 | async-start | bytes 2359296 | tf_op jit(solution)/shard_map/reduce_scatter | solution.py:200
  132.7 36.8 %copy-start.8 = (f32[1024]{0:T(1024)S(1)}, f32[1024]{0:T(1024)}, u32[]{:S(2)}) copy-start(f32[1024]{0:T(1024)} %param.27) | copy-start | bytes 12292
  132.7 36.8 %copy-start.9 = (f32[1024]{0:T(1024)S(1)}, f32[1024]{0:T(1024)}, u32[]{:S(2)}) copy-start(f32[1024]{0:T(1024)} %param.26) | copy-start | bytes 12292
Sparse Core Ops, SparseCore 0:
  101.9 20.9 all-gather.1
  132.8 34.1 reduce-scatter.1

commit v4 on v1

--- a/solution.py
+++ b/solution.py
@@ -129,6 +129,87 @@
     )
 
 
+def scatter_kernel(part_ref, o_ref, pair_buf, send_buf, ring_buf, pair_send, pair_recv, ring_send, ring_recv):
+    req = lax.axis_index("req")
+    me = lax.axis_index("mlp")
+    chips = lax.axis_size("mlp") // 2
+    chip, core = me // 2, lax.rem(me, 2)
+    partner = chip * 2 + 1 - core
+    rows = o_ref.shape[0]
+    barrier = pltpu.get_barrier_semaphore()
+    pl.semaphore_signal(barrier, 1, device_id=(req, partner), device_id_type=pl.DeviceIdType.MESH)
+    for k in range(1, chips):
+        other = lax.rem(chip + k, chips) * 2 + core
+        pl.semaphore_signal(barrier, 1, device_id=(req, other), device_id_type=pl.DeviceIdType.MESH)
+    pl.semaphore_wait(barrier, chips)
+
+    def pair_copy(z):
+        block = z * 2 + 1 - core
+        return pltpu.make_async_remote_copy(
+            src_ref=part_ref.at[pl.ds(pl.multiple_of(block * rows, rows), rows)],
+            dst_ref=pair_buf.at[z],
+            send_sem=pair_send.at[z],
+            recv_sem=pair_recv.at[z],
+            device_id=(req, partner),
+            device_id_type=pl.DeviceIdType.MESH,
+        )
+
+    for z in range(chips):
+        pair_copy(z).start()
+    for z in range(chips):
+        pair_copy(z).wait()
+
+    def ring_copy(k):
+        target = lax.rem(chip + k, chips)
+        return pltpu.make_async_remote_copy(
+            src_ref=send_buf.at[k],
+            dst_ref=ring_buf.at[k],
+            send_sem=ring_send.at[k],
+            recv_sem=ring_recv.at[k],
+            device_id=(req, target * 2 + core),
+            device_id_type=pl.DeviceIdType.MESH,
+        )
+
+    for k in range(1, chips):
+        target = lax.rem(chip + k, chips)
+        mine = part_ref[pl.ds(pl.multiple_of((target * 2 + core) * rows, rows), rows), :]
+        send_buf[k] = (mine.astype(jnp.float32) + pair_buf[target].astype(jnp.float32)).astype(
+            send_buf.dtype
+        )
+        ring_copy(k).start()
+    own = part_ref[pl.ds(pl.multiple_of(me * rows, rows), rows), :]
+    total = own.astype(jnp.float32) + pair_buf[chip].astype(jnp.float32)
+    for k in range(1, chips):
+        ring_copy(k).wait()
+        total = total + ring_buf[k].astype(jnp.float32)
+    o_ref[...] = total
+
+
+def scatter_sum(partial):
+    groups = lax.axis_size("mlp")
+    chips = groups // 2
+    rows = partial.shape[0] // groups
+    width = partial.shape[1]
+    return pl.pallas_call(
+        scatter_kernel,
+        in_specs=[pl.BlockSpec(memory_space=pltpu.VMEM)],
+        out_specs=pl.BlockSpec(memory_space=pltpu.VMEM),
+        out_shape=jax.ShapeDtypeStruct((rows, width), jnp.float32),
+        scratch_shapes=[
+            pltpu.VMEM((chips, rows, width), partial.dtype),
+            pltpu.VMEM((chips, rows, width), partial.dtype),
+            pltpu.VMEM((chips, rows, width), partial.dtype),
+            pltpu.SemaphoreType.DMA((chips,)),
+            pltpu.SemaphoreType.DMA((chips,)),
+            pltpu.SemaphoreType.DMA((chips,)),
+            pltpu.SemaphoreType.DMA((chips,)),
+        ],
+        compiler_params=pltpu.CompilerParams(
+            collective_id=1, has_side_effects=True, vmem_limit_bytes=48 * 1024 * 1024
+        ),
+    )(partial)
+
+
 def per_device(
     tokens,
     token_owner,
@@ -198,12 +279,9 @@
     hidden = jax.nn.gelu(
         jnp.dot(gathered, w_fc1, preferred_element_type=jnp.float32), approximate=False
     ).astype(jnp.bfloat16)
-    summed = lax.psum_scatter(
-        jnp.dot(hidden, w_fc2, preferred_element_type=jnp.float32).astype(jnp.bfloat16),
-        "mlp",
-        scatter_dimension=0,
-        tiled=True,
-    ).astype(jnp.float32)
+    summed = scatter_sum(
+        jnp.dot(hidden, w_fc2, preferred_element_type=jnp.float32).astype(jnp.bfloat16)
+    )
     return layer_norm(normed.astype(jnp.float32) + summed, ln2_gain, ln2_bias).astype(jnp.bfloat16)
 
 

time: 157 us -> 141 us (0.90)
  waiting for transfers between devices: 67.1 us -> 33 us
  Pallas kernels: 19.6 us -> 38.1 us
  other arithmetic: 7.06 us -> 4.16 us
  local copies, waits for them, and re-layouts: 3.79 us -> 5.38 us
    reduce_scatter x1 -> x0, waiting for transfers between devices: 34.3 us -> none  [per_device(): lax.psum_scatter(jnp.dot(hidden, w_fc2, preferred_element_type=jnp.float3...]
    pallas_call x0 -> x1, Pallas kernels: none -> 18.6 us  [scatter_sum(): pl.pallas_call(scatter_kernel, in_specs=[pl.BlockSpec(memory_space=pltpu....]
    unnamed x24 -> x26, local copies, waits for them, and re-layouts: 0.13 us -> 1.72 us
  transfers between devices with their start and end apart: 3 -> 2, of which waited for: 3 -> 2; matrix products, arithmetic and copies ran while one was open for 1% -> 1% of each run, Pallas kernels for 0% -> 0%
where the time goes in v4:
time: 141 us; the launch traced here: 140 us
  Pallas kernels  38.1 us (27%)
  waiting for transfers between devices  33 us (23%)
  blocking collectives  18 us (13%)
  matrix products  16.2 us (11%)
  between operations  13.7 us (10%)
  starting transfers between devices  11.2 us (8%)
  local copies, waits for them, and re-layouts  5.38 us (4%)
  other arithmetic  4.16 us (3%)
    all_gather x1, waiting for transfers between devices, per_device(): gathered = lax.all_gather(normed, 'mlp', axis=0, tiled=True)  21.3 us
    pallas_call x1, Pallas kernels, attend(): pl.pallas_call(attention_kernel, grid=(pairs,), in_specs=[pl.BlockSpec((s...  19.5 us
    pallas_call x1, Pallas kernels, scatter_sum(): pl.pallas_call(scatter_kernel, in_specs=[pl.BlockSpec(memory_space=pltpu....  18.6 us
    all_to_all x1, blocking collectives, per_device(): lax.all_to_all(attended.reshape(devices, capacity, width), ('req', 'mlp')...  18 us
    all_to_all x1, waiting for transfers between devices, per_device(): lax.all_to_all(outgoing.reshape(devices, capacity, width), ('req', 'mlp')...  11.7 us
    all_to_all x1, starting transfers between devices, per_device(): lax.all_to_all(outgoing.reshape(devices, capacity, width), ('req', 'mlp')...  11.1 us
    dot_general x1, matrix products, per_device(): jnp.dot(hidden, w_fc2, preferred_element_type=jnp.float32)  9.63 us
    dot_general x1, matrix products, per_device(): jnp.dot(arrived.reshape(slot_count, width), w_qkv, preferred_element_type...  4.58 us
  transfers between devices with their start and end apart: 2, of which 2 were waited for; matrix products, arithmetic and copies ran while one was open for 1% of the time, Pallas kernels for 0%

profile of v4, /device:TPU:0, one launch (start us, length us, event | category | flops | bytes accessed | tf_op | source)
XLA Modules:
  0.0 139.8 jit_solution(1056482518326541266)
XLA Ops:
  6.5 0.0 copy-start
  6.5 0.0 copy-start.3
  6.5 0.0 copy-start.6
  6.5 0.8 fusion.49
  7.3 0.1 fusion.47
  7.4 0.2 reduce_window_sum.22
  7.6 0.2 select_reduce_fusion.1
  7.8 0.7 fusion.48
  8.5 0.0 copy-start.7
  8.5 1.3 convolution_convert_fusion.2
  9.8 0.0 copy-start.11
  9.8 1.0 reshape.234
  10.8 11.1 %all-to-all-start = ((bf16[128,2,1024]{2,1,0:T(2,128)(2,1)}), bf16[128,2,1024]{2,1,0:T(2,128)(2,1)S(1)}, u32[]{:S(2)}, u32[]{:S(2)}) async-start(bf16[128,2,1024]{2,1,0:T(2,128)(2,1)} %reshape.234), calls=%async_computation | async-start | bytes 1048576 | tf_op jit(solution)/shard_map/all_to_all | solution.py:250
  22.0 0.0 all-gather.2.cloned.1.call-start
  22.0 0.0 copy-done.7
  22.0 0.0 copy-done.3
  22.0 0.1 compare_convert_fusion
  22.1 0.1 copy.23
  22.2 0.2 reduce_window_sum.23
  22.4 0.1 copy.24
  22.5 0.0 copy-done.6
  22.5 0.2 select_reduce_fusion
  22.7 0.1 copy.26
  22.8 0.1 reduce_sum.86.rfill_ref
  22.9 0.1 copy.28
  23.0 0.1 add.116
  23.1 0.0 copy-done.11
  23.1 0.1 broadcast_bitcast_fusion
  23.2 0.1 copy.25
  23.3 0.1 copy.31
  23.4 0.1 select_n.85.nrow_ref
  23.6 0.1 reshape_reshape.3.rreq_ref
  23.7 0.1 copy.30
  23.8 0.1 select_n.83.ntag_ref
  24.0 11.7 %all-to-all-done = bf16[128,2,1024]{2,1,0:T(2,128)(2,1)S(1)} async-done(((bf16[128,2,1024]{2,1,0:T(2,128)(2,1)}), bf16[128,2,1024]{2,1,0:T(2,128)(2,1)S(1)}, u32[]{:S(2)}, u32[]{:S(2)}) %all-to-all-start) | async-done | bytes 524320 | tf_op jit(solution)/shard_map/all_to_all | solution.py:250
  35.7 0.2 reshape.235
  35.9 4.6 %convolution_convert_fusion.q_ref.kn_ref.vn_ref = bf16[256,3072]{1,0:T(8,128)(2,1)S(1)} fusion(bf16[256,1024]{1,0:T(8,128)(2,1)S(1)} %reshape.235, bf16[1024,3072]{1,0:T(8,128)(2,1)} %param.20), kind=kOutput, calls=%fused_computation | convolution fusion | flops 1611399168 | bytes 8388608 | tf_op jit(solution)/shard_map/dot_general | solution.py:257
  40.5 19.5 %shard_map.136 = bf16[256,1024]{1,0:T(8,128)(2,1)S(1)} custom-call(bf16[256,3072]{1,0:T(8,128)(2,1)S(1)} %convolution_convert_fusion.q_ref.kn_ref.vn_ref, bf16[256,3072]{1,0:T(8,128)(2,1)S(1)} %convolution_convert_fusion.q_ref.kn_ref.vn_ref, bf16[256,3072]{1,0:T(8,128)(2,1)S(1)} %convolution_convert_fusion.q_ref.kn_ref.vn_ref, bf16[2048,1024]{1,0:T(8,128)(2,1)} %bitcast.24, ...), custom_call_target="tpu_custom_call" | custom-call | tf_op jit(solution)/shard_map/pallas_call | solution.py:98
  60.0 0.0 copy-start.2
  60.0 0.0 copy-start.8
  60.0 0.2 reshape.239
  60.2 18.0 %all_to_all.10 = bf16[128,2,1024]{2,1,0:T(2,128)(2,1)S(1)} all-to-all(bf16[128,2,1024]{2,1,0:T(2,128)(2,1)S(1)} %reshape.239), channel_id=1, replica_groups=mesh['req'=16,'mlp'=8] {'req','mlp'}, dimensions={0} | all-to-all | bytes 1048576 | tf_op jit(solution)/shard_map/all_to_all | solution.py:264
  78.2 0.2 reshape.240
  78.4 0.0 copy-done
  78.4 0.0 copy-done.2
  78.4 0.0 copy-done.8
  78.4 0.0 copy-start.4
  78.4 0.0 copy-start.5
  78.4 0.7 fusion.80
  79.1 0.2 multiply_reduce_fusion.1
  79.4 0.0 copy-done.4
  79.4 0.0 copy-done.5
  79.4 0.9 add_convert_fusion.1
  80.2 0.0 all-gather.2.cloned.1.call-update
  80.3 21.3 %all-gather.2.cloned.1.call-done = bf16[1024,1024]{1,0:T(8,128)(2,1)} async-done(((bf16[128,1024]{1,0:T(8,128)(2,1)}), bf16[1024,1024]{1,0:T(8,128)(2,1)}) %all-gather.2.cloned.1.call-update) | async-done | bytes 2097168 | tf_op jit(solution)/shard_map/all_gather | solution.py:278
  101.5 9.6 %convolution_convert_fusion.1.part_ref = bf16[1024,1024]{1,0:T(8,128)(2,1)} fusion(bf16[512,1024]{1,0:T(8,128)(2,1)} %param.23, bf16[1024,1024]{1,0:T(8,128)(2,1)} %all-gather.2.cloned.1.call-done, bf16[1024,512]{1,0:T(8,128)(2,1)} %param.22), kind=kOutput, calls=%fused_computation.20 | convolution fusion | flops 2182610944 | bytes 6291456 | tf_op jit(solution)/shard_map/dot_general | solution.py:283
  111.2 0.0 copy-start.1
  111.2 1.6 %copy-done.1 = bf16[1024,1024]{1,0:T(8,128)(2,1)S(1)} copy-done((bf16[1024,1024]{1,0:T(8,128)(2,1)S(1)}, bf16[1024,1024]{1,0:T(8,128)(2,1)}, u32[]{:S(2)}) %copy-start.1) | copy-done | bytes 2097176
  112.8 18.6 %shard_map.137 = f32[128,1024]{1,0:T(8,128)S(1)} custom-call(bf16[1024,1024]{1,0:T(8,128)(2,1)S(1)} %copy-done.1), custom_call_target="tpu_custom_call" | custom-call | tf_op jit(solution)/shard_map/pallas_call | solution.py:193
  131.4 0.3 fusion.41
  131.6 0.3 multiply_reduce_fusion
  131.9 0.0 copy-done.9
  131.9 0.0 copy-done.10
  132.0 1.0 add_convert_fusion
  (12 shorter events, 0.1 us)
Async XLA Ops:
  6.5 71.9 %copy-start = (bf16[1024,1024]{1,0:T(8,128)(2,1)S(1)}, bf16[1024,1024]{1,0:T(8,128)(2,1)}, u32[]{:S(2)}) copy-start(bf16[1024,1024]{1,0:T(8,128)(2,1)} %param.21) | copy-start | bytes 6291460
  6.5 15.5 %copy-start.3 = (s32[16384,1]{0,1:T(1,128)S(1)}, s32[16384,1]{0,1:T(1,128)}, u32[]{:S(2)}) copy-start(s32[16384,1]{0,1:T(1,128)} %param.15) | copy-start | bytes 196612
  6.5 16.0 %copy-start.6 = (s32[16384]{0:T(1024)S(1)}, s32[16384]{0:T(1024)}, u32[]{:S(2)}) copy-start(s32[16384]{0:T(1024)} %param.16) | copy-start | bytes 196612
  8.5 13.6 %copy-start.7 = (s32[128]{0:T(128)}, s32[128]{0:T(128)S(1)}, u32[]{:S(2)}) copy-start(s32[128]{0:T(128)S(1)} %fusion.48) | copy-start | bytes 1540
  9.8 13.3 %copy-start.11 = (s32[4]{0:T(128)S(1)}, s32[4]{0:T(128)}, u32[]{:S(2)}) copy-start(s32[4]{0:T(128)} %param.17) | copy-start | bytes 52
  10.8 24.9 %all-to-all-start = ((bf16[128,2,1024]{2,1,0:T(2,128)(2,1)}), bf16[128,2,1024]{2,1,0:T(2,128)(2,1)S(1)}, u32[]{:S(2)}, u32[]{:S(2)}) async-start(bf16[128,2,1024]{2,1,0:T(2,128)(2,1)} %reshape.234), calls=%async_computation | async-start | bytes 1048576 | tf_op jit(solution)/shard_map/all_to_all | solution.py:250
  22.0 79.6 %all-gather.2.cloned.1.call-start = ((), (), s32[]{:S(2)}) async-start(), calls=%async_computation.2 | async-start | bytes 2359296 | tf_op jit(solution)/shard_map/all_gather | solution.py:278
  60.0 18.4 %copy-start.2 = (bf16[128,1024]{1,0:T(8,128)(2,1)S(1)}, bf16[128,1024]{1,0:T(8,128)(2,1)}, u32[]{:S(2)}) copy-start(bf16[128,1024]{1,0:T(8,128)(2,1)} %param.14) | copy-start | bytes 786436
  60.0 18.4 %copy-start.8 = (s32[128]{0:T(128)S(1)}, s32[128]{0:T(128)}, u32[]{:S(2)}) copy-start(s32[128]{0:T(128)} %copy-done.7) | copy-start | bytes 1540
  78.4 0.9 copy-start.4
  78.4 0.9 copy-start.5
  111.2 1.6 %copy-start.1 = (bf16[1024,1024]{1,0:T(8,128)(2,1)S(1)}, bf16[1024,1024]{1,0:T(8,128)(2,1)}, u32[]{:S(2)}) copy-start(bf16[1024,1024]{1,0:T(8,128)(2,1)} %convolution_convert_fusion.1.part_ref) | copy-start | bytes 6291460
  112.8 19.2 %copy-start.9 = (f32[1024]{0:T(1024)S(1)}, f32[1024]{0:T(1024)}, u32[]{:S(2)}) copy-start(f32[1024]{0:T(1024)} %param.27) | copy-start | bytes 12292
  112.8 19.2 %copy-start.10 = (f32[1024]{0:T(1024)S(1)}, f32[1024]{0:T(1024)}, u32[]{:S(2)}) copy-start(f32[1024]{0:T(1024)} %param.26) | copy-start | bytes 12292
Sparse Core Ops, SparseCore 0:
  80.4 21.1 all-gather.1

commit v5 on v4

--- a/solution.py
+++ b/solution.py
@@ -210,6 +210,78 @@
     )(partial)
 
 
+def gather_kernel(x_ref, o_ref, ring_send, ring_recv, pair_send, pair_recv):
+    req = lax.axis_index("req")
+    me = lax.axis_index("mlp")
+    chips = lax.axis_size("mlp") // 2
+    chip, core = me // 2, lax.rem(me, 2)
+    partner = chip * 2 + 1 - core
+    rows = x_ref.shape[0]
+    barrier = pltpu.get_barrier_semaphore()
+    pl.semaphore_signal(barrier, 1, device_id=(req, partner), device_id_type=pl.DeviceIdType.MESH)
+    for k in range(1, chips):
+        other = lax.rem(chip + k, chips) * 2 + core
+        pl.semaphore_signal(barrier, 1, device_id=(req, other), device_id_type=pl.DeviceIdType.MESH)
+    pl.semaphore_wait(barrier, chips)
+
+    def block_rows(block):
+        return pl.ds(pl.multiple_of(block * rows, rows), rows)
+
+    def ring_copy(k):
+        target = lax.rem(chip + k, chips)
+        return pltpu.make_async_remote_copy(
+            src_ref=x_ref,
+            dst_ref=o_ref.at[block_rows(me)],
+            send_sem=ring_send.at[k],
+            recv_sem=ring_recv.at[k],
+            device_id=(req, target * 2 + core),
+            device_id_type=pl.DeviceIdType.MESH,
+        )
+
+    def pair_copy(k):
+        source = lax.rem(chip + chips - k, chips) * 2 + core
+        return pltpu.make_async_remote_copy(
+            src_ref=x_ref if k == 0 else o_ref.at[block_rows(source)],
+            dst_ref=o_ref.at[block_rows(source)],
+            send_sem=pair_send.at[k],
+            recv_sem=pair_recv.at[k],
+            device_id=(req, partner),
+            device_id_type=pl.DeviceIdType.MESH,
+        )
+
+    for k in range(1, chips):
+        ring_copy(k).start()
+    pair_copy(0).start()
+    o_ref[block_rows(me), :] = x_ref[...]
+    for k in range(1, chips):
+        ring_copy(k).wait_recv()
+        pair_copy(k).start()
+    for k in range(1, chips):
+        ring_copy(k).wait_send()
+    for k in range(chips):
+        pair_copy(k).wait()
+
+
+def gather_rows(block):
+    groups = lax.axis_size("mlp")
+    chips = groups // 2
+    return pl.pallas_call(
+        gather_kernel,
+        in_specs=[pl.BlockSpec(memory_space=pltpu.VMEM)],
+        out_specs=pl.BlockSpec(memory_space=pltpu.VMEM),
+        out_shape=jax.ShapeDtypeStruct((groups * block.shape[0], block.shape[1]), block.dtype),
+        scratch_shapes=[
+            pltpu.SemaphoreType.DMA((chips,)),
+            pltpu.SemaphoreType.DMA((chips,)),
+            pltpu.SemaphoreType.DMA((chips,)),
+            pltpu.SemaphoreType.DMA((chips,)),
+        ],
+        compiler_params=pltpu.CompilerParams(
+            collective_id=2, has_side_effects=True, vmem_limit_bytes=48 * 1024 * 1024
+        ),
+    )(block)
+
+
 def per_device(
     tokens,
     token_owner,
@@ -275,7 +347,7 @@
     normed = layer_norm(projected_out + tokens.astype(jnp.float32), ln1_gain, ln1_bias).astype(
         jnp.bfloat16
     )
-    gathered = lax.all_gather(normed, "mlp", axis=0, tiled=True)
+    gathered = gather_rows(normed)
     hidden = jax.nn.gelu(
         jnp.dot(gathered, w_fc1, preferred_element_type=jnp.float32), approximate=False
     ).astype(jnp.bfloat16)

time: 141 us -> 123 us (0.87)
  waiting for transfers between devices: 33 us -> 11.8 us
  Pallas kernels: 38.1 us -> 54.7 us
  between operations: 13.7 us -> 0.34 us
    all_gather x1 -> x0, waiting for transfers between devices: 21.3 us -> none  [per_device(): gathered = lax.all_gather(normed, 'mlp', axis=0, tiled=True)]
    pallas_call x0 -> x1, Pallas kernels: none -> 16.4 us  [gather_rows(): pl.pallas_call(gather_kernel, in_specs=[pl.BlockSpec(memory_space=pltpu.V...]
    unnamed x26 -> x28, local copies, waits for them, and re-layouts: 1.72 us -> 3.07 us
  transfers between devices with their start and end apart: 2 -> 1, of which waited for: 2 -> 1; matrix products, arithmetic and copies ran while one was open for 1% -> 1% of each run, Pallas kernels for 0% -> 0%
where the time goes in v5:
time: 123 us; the launch traced here: 122 us
  Pallas kernels  54.7 us (44%)
  blocking collectives  17.8 us (14%)
  matrix products  16.2 us (13%)
  waiting for transfers between devices  11.8 us (10%)
  starting transfers between devices  11.2 us (9%)
  local copies, waits for them, and re-layouts  6.72 us (5%)
  other arithmetic  3.46 us (3%)
    pallas_call x1, Pallas kernels, attend(): pl.pallas_call(attention_kernel, grid=(pairs,), in_specs=[pl.BlockSpec((s...  19.6 us
    pallas_call x1, Pallas kernels, scatter_sum(): pl.pallas_call(scatter_kernel, in_specs=[pl.BlockSpec(memory_space=pltpu....  18.6 us
    all_to_all x1, blocking collectives, per_device(): lax.all_to_all(attended.reshape(devices, capacity, width), ('req', 'mlp')...  17.8 us
    pallas_call x1, Pallas kernels, gather_rows(): pl.pallas_call(gather_kernel, in_specs=[pl.BlockSpec(memory_space=pltpu.V...  16.4 us
    all_to_all x1, waiting for transfers between devices, per_device(): lax.all_to_all(outgoing.reshape(devices, capacity, width), ('req', 'mlp')...  11.8 us
    all_to_all x1, starting transfers between devices, per_device(): lax.all_to_all(outgoing.reshape(devices, capacity, width), ('req', 'mlp')...  11.2 us
    dot_general x1, matrix products, per_device(): jnp.dot(hidden, w_fc2, preferred_element_type=jnp.float32)  9.63 us
    dot_general x1, matrix products, per_device(): jnp.dot(arrived.reshape(slot_count, width), w_qkv, preferred_element_type...  4.58 us
  transfers between devices with their start and end apart: 1, of which 1 were waited for; matrix products, arithmetic and copies ran while one was open for 1% of the time, Pallas kernels for 0%

profile of v5, /device:TPU:0, one launch (start us, length us, event | category | flops | bytes accessed | tf_op | source)
XLA Modules:
  0.0 122.2 jit_solution(3048403111571873590)
XLA Ops:
  0.0 0.0 copy-start
  0.0 0.0 copy-start.4
  0.0 0.0 copy-start.7
  0.0 0.8 fusion.49
  0.8 0.1 fusion.47
  0.9 0.2 reduce_window_sum.22
  1.1 0.2 select_reduce_fusion.1
  1.3 0.7 fusion.48
  1.9 0.0 copy-start.8
  1.9 1.3 %convolution_convert_fusion.2 = bf16[256,1024]{1,0:T(8,128)(2,1)S(1)} fusion(bf16[128,1024]{1,0:T(8,128)(2,1)} %param.14, s32[128]{0:T(128)S(1)} %fusion.48), kind=kOutput, calls=%fused_computation.21 | convolution fusion | flops 67403776 | bytes 786944 | tf_op jit(solution)/shard_map/tr,td->rd/dot_general | solution.py:319
  3.3 0.0 copy-start.12
  3.3 1.0 reshape.234
  4.3 11.2 %all-to-all-start = ((bf16[128,2,1024]{2,1,0:T(2,128)(2,1)}), bf16[128,2,1024]{2,1,0:T(2,128)(2,1)S(1)}, u32[]{:S(2)}, u32[]{:S(2)}) async-start(bf16[128,2,1024]{2,1,0:T(2,128)(2,1)} %reshape.234), calls=%async_computation | async-start | bytes 1048576 | tf_op jit(solution)/shard_map/all_to_all | solution.py:322
  15.4 0.0 copy-done.8
  15.5 0.0 copy-done.4
  15.5 0.1 compare_convert_fusion
  15.5 0.1 copy.23
  15.6 0.2 reduce_window_sum.23
  15.8 0.1 copy.24
  15.9 0.0 copy-done.7
  15.9 0.2 select_reduce_fusion
  16.1 0.1 copy.26
  16.2 0.1 reduce_sum.86.rfill_ref
  16.3 0.1 copy.28
  16.4 0.1 add.116
  16.6 0.0 copy-done.12
  16.6 0.1 broadcast_bitcast_fusion
  16.6 0.1 copy.25
  16.8 0.1 copy.31
  16.9 0.1 select_n.85.nrow_ref
  17.0 0.1 reshape_reshape.3.rreq_ref
  17.1 0.1 copy.30
  17.2 0.1 select_n.83.ntag_ref
  17.4 11.8 %all-to-all-done = bf16[128,2,1024]{2,1,0:T(2,128)(2,1)S(1)} async-done(((bf16[128,2,1024]{2,1,0:T(2,128)(2,1)}), bf16[128,2,1024]{2,1,0:T(2,128)(2,1)S(1)}, u32[]{:S(2)}, u32[]{:S(2)}) %all-to-all-start) | async-done | bytes 524320 | tf_op jit(solution)/shard_map/all_to_all | solution.py:322
  29.2 0.2 reshape.235
  29.4 4.6 %convolution_convert_fusion.q_ref.kn_ref.vn_ref = bf16[256,3072]{1,0:T(8,128)(2,1)S(1)} fusion(bf16[256,1024]{1,0:T(8,128)(2,1)S(1)} %reshape.235, bf16[1024,3072]{1,0:T(8,128)(2,1)} %param.20), kind=kOutput, calls=%fused_computation | convolution fusion | flops 1611399168 | bytes 8388608 | tf_op jit(solution)/shard_map/dot_general | solution.py:329
  33.9 19.6 %shard_map.136 = bf16[256,1024]{1,0:T(8,128)(2,1)S(1)} custom-call(bf16[256,3072]{1,0:T(8,128)(2,1)S(1)} %convolution_convert_fusion.q_ref.kn_ref.vn_ref, bf16[256,3072]{1,0:T(8,128)(2,1)S(1)} %convolution_convert_fusion.q_ref.kn_ref.vn_ref, bf16[256,3072]{1,0:T(8,128)(2,1)S(1)} %convolution_convert_fusion.q_ref.kn_ref.vn_ref, bf16[2048,1024]{1,0:T(8,128)(2,1)} %bitcast.24, ...), custom_call_target="tpu_custom_call" | custom-call | tf_op jit(solution)/shard_map/pallas_call | solution.py:98
  53.6 0.0 copy-start.3
  53.6 0.0 copy-start.9
  53.6 0.2 reshape.239
  53.8 17.8 %all_to_all.10 = bf16[128,2,1024]{2,1,0:T(2,128)(2,1)S(1)} all-to-all(bf16[128,2,1024]{2,1,0:T(2,128)(2,1)S(1)} %reshape.239), channel_id=1, replica_groups=mesh['req'=16,'mlp'=8] {'req','mlp'}, dimensions={0} | all-to-all | bytes 1048576 | tf_op jit(solution)/shard_map/all_to_all | solution.py:336
  71.7 0.2 reshape.240
  71.9 0.0 copy-done
  71.9 0.0 copy-done.3
  71.9 0.0 copy-done.9
  71.9 0.0 copy-start.5
  71.9 0.0 copy-start.6
  71.9 0.7 fusion.80
  72.6 0.2 multiply_reduce_fusion.1
  72.8 0.0 copy-done.5
  72.8 0.0 copy-done.6
  72.8 0.2 add_convert_fusion.1.x_ref
  73.0 16.4 %shard_map.137 = bf16[1024,1024]{1,0:T(8,128)(2,1)S(1)} custom-call(bf16[128,1024]{1,0:T(8,128)(2,1)S(1)} %add_convert_fusion.1.x_ref), custom_call_target="tpu_custom_call" | custom-call | tf_op jit(solution)/shard_map/pallas_call | solution.py:268
  89.5 0.0 copy-start.2
  89.5 1.3 %copy-done.2 = bf16[1024,1024]{1,0:T(8,128)(2,1)} copy-done((bf16[1024,1024]{1,0:T(8,128)(2,1)}, bf16[1024,1024]{1,0:T(8,128)(2,1)S(1)}, u32[]{:S(2)}) %copy-start.2) | copy-done | bytes 2097176
  90.8 9.6 %convolution_convert_fusion.1.part_ref = bf16[1024,1024]{1,0:T(8,128)(2,1)} fusion(bf16[512,1024]{1,0:T(8,128)(2,1)} %param.23, bf16[1024,1024]{1,0:T(8,128)(2,1)} %copy-done.2, bf16[1024,512]{1,0:T(8,128)(2,1)} %param.22), kind=kOutput, calls=%fused_computation.20 | convolution fusion | flops 2182610944 | bytes 6291456 | tf_op jit(solution)/shard_map/dot_general | solution.py:355
  100.4 0.0 copy-start.1
  100.4 1.6 %copy-done.1 = bf16[1024,1024]{1,0:T(8,128)(2,1)S(1)} copy-done((bf16[1024,1024]{1,0:T(8,128)(2,1)S(1)}, bf16[1024,1024]{1,0:T(8,128)(2,1)}, u32[]{:S(2)}) %copy-start.1) | copy-done | bytes 2097176
  102.0 18.6 %shard_map.138 = f32[128,1024]{1,0:T(8,128)S(1)} custom-call(bf16[1024,1024]{1,0:T(8,128)(2,1)S(1)} %copy-done.1), custom_call_target="tpu_custom_call" | custom-call | tf_op jit(solution)/shard_map/pallas_call | solution.py:193
  120.6 0.3 fusion.41
  120.9 0.3 multiply_reduce_fusion
  121.2 0.0 copy-done.10
  121.2 0.0 copy-done.11
  121.2 1.0 add_convert_fusion
  (12 shorter events, 0.1 us)
Async XLA Ops:
  0.0 71.9 %copy-start = (bf16[1024,1024]{1,0:T(8,128)(2,1)S(1)}, bf16[1024,1024]{1,0:T(8,128)(2,1)}, u32[]{:S(2)}) copy-start(bf16[1024,1024]{1,0:T(8,128)(2,1)} %param.21) | copy-start | bytes 6291460
  0.0 15.5 %copy-start.4 = (s32[16384,1]{0,1:T(1,128)S(1)}, s32[16384,1]{0,1:T(1,128)}, u32[]{:S(2)}) copy-start(s32[16384,1]{0,1:T(1,128)} %param.15) | copy-start | bytes 196612
  0.0 15.9 %copy-start.7 = (s32[16384]{0:T(1024)S(1)}, s32[16384]{0:T(1024)}, u32[]{:S(2)}) copy-start(s32[16384]{0:T(1024)} %param.16) | copy-start | bytes 196612
  1.9 13.5 %copy-start.8 = (s32[128]{0:T(128)}, s32[128]{0:T(128)S(1)}, u32[]{:S(2)}) copy-start(s32[128]{0:T(128)S(1)} %fusion.48) | copy-start | bytes 1540
  3.3 13.3 %copy-start.12 = (s32[4]{0:T(128)S(1)}, s32[4]{0:T(128)}, u32[]{:S(2)}) copy-start(s32[4]{0:T(128)} %param.17) | copy-start | bytes 52
  4.3 24.9 %all-to-all-start = ((bf16[128,2,1024]{2,1,0:T(2,128)(2,1)}), bf16[128,2,1024]{2,1,0:T(2,128)(2,1)S(1)}, u32[]{:S(2)}, u32[]{:S(2)}) async-start(bf16[128,2,1024]{2,1,0:T(2,128)(2,1)} %reshape.234), calls=%async_computation | async-start | bytes 1048576 | tf_op jit(solution)/shard_map/all_to_all | solution.py:322
  53.6 18.3 %copy-start.3 = (bf16[128,1024]{1,0:T(8,128)(2,1)S(1)}, bf16[128,1024]{1,0:T(8,128)(2,1)}, u32[]{:S(2)}) copy-start(bf16[128,1024]{1,0:T(8,128)(2,1)} %param.14) | copy-start | bytes 786436
  53.6 18.3 %copy-start.9 = (s32[128]{0:T(128)S(1)}, s32[128]{0:T(128)}, u32[]{:S(2)}) copy-start(s32[128]{0:T(128)} %copy-done.8) | copy-start | bytes 1540
  71.9 0.9 copy-start.5
  71.9 0.9 copy-start.6
  89.5 1.4 %copy-start.2 = (bf16[1024,1024]{1,0:T(8,128)(2,1)}, bf16[1024,1024]{1,0:T(8,128)(2,1)S(1)}, u32[]{:S(2)}) copy-start(bf16[1024,1024]{1,0:T(8,128)(2,1)S(1)} %shard_map.137) | copy-start | bytes 6291460
  100.4 1.6 %copy-start.1 = (bf16[1024,1024]{1,0:T(8,128)(2,1)S(1)}, bf16[1024,1024]{1,0:T(8,128)(2,1)}, u32[]{:S(2)}) copy-start(bf16[1024,1024]{1,0:T(8,128)(2,1)} %convolution_convert_fusion.1.part_ref) | copy-start | bytes 6291460
  102.0 19.2 %copy-start.10 = (f32[1024]{0:T(1024)S(1)}, f32[1024]{0:T(1024)}, u32[]{:S(2)}) copy-start(f32[1024]{0:T(1024)} %param.27) | copy-start | bytes 12292
  102.0 19.2 %copy-start.11 = (f32[1024]{0:T(1024)S(1)}, f32[1024]{0:T(1024)}, u32[]{:S(2)}) copy-start(f32[1024]{0:T(1024)} %param.26) | copy-start | bytes 12292

commit v6 on v5

--- a/solution.py
+++ b/solution.py
@@ -1,3 +1,5 @@
+import functools
+
 import jax
 import jax.numpy as jnp
 from jax import lax
@@ -282,6 +284,87 @@
     )(block)
 
 
+def staged_kernel(first, second, strided_out, x_ref, o_ref, mid, sends, recvs, locals_):
+    axes = {"req": lax.axis_index("req"), "mlp": lax.axis_index("mlp")}
+    n1, n2 = x_ref.shape[0], x_ref.shape[1]
+    me1, me2 = axes[first], axes[second]
+
+    def device(one, two):
+        coords = {first: one, second: two}
+        return (coords["req"], coords["mlp"])
+
+    barrier = pltpu.get_barrier_semaphore()
+    for k in range(1, n1):
+        pl.semaphore_signal(
+            barrier, 1, device_id=device(lax.rem(me1 + k, n1), me2), device_id_type=pl.DeviceIdType.MESH
+        )
+    for k in range(1, n2):
+        pl.semaphore_signal(
+            barrier, 1, device_id=device(me1, lax.rem(me2 + k, n2)), device_id_type=pl.DeviceIdType.MESH
+        )
+    pl.semaphore_wait(barrier, n1 + n2 - 2)
+
+    def out_view(index):
+        return o_ref.at[:, index] if strided_out else o_ref.at[index]
+
+    def stage_one(k):
+        target = lax.rem(me1 + k, n1)
+        return pltpu.make_async_remote_copy(
+            src_ref=x_ref.at[target],
+            dst_ref=mid.at[:, me1],
+            send_sem=sends.at[0, k],
+            recv_sem=recvs.at[0, k],
+            device_id=device(target, me2),
+            device_id_type=pl.DeviceIdType.MESH,
+        )
+
+    def stage_two(k):
+        target = lax.rem(me2 + k, n2)
+        return pltpu.make_async_remote_copy(
+            src_ref=mid.at[target],
+            dst_ref=out_view(me2),
+            send_sem=sends.at[1, k],
+            recv_sem=recvs.at[1, k],
+            device_id=device(me1, target),
+            device_id_type=pl.DeviceIdType.MESH,
+        )
+
+    own_one = pltpu.make_async_copy(x_ref.at[me1], mid.at[:, me1], locals_.at[0])
+    own_one.start()
+    for k in range(1, n1):
+        stage_one(k).start()
+    own_one.wait()
+    for k in range(1, n1):
+        stage_one(k).wait()
+    own_two = pltpu.make_async_copy(mid.at[me2], out_view(me2), locals_.at[1])
+    own_two.start()
+    for k in range(1, n2):
+        stage_two(k).start()
+    own_two.wait()
+    for k in range(1, n2):
+        stage_two(k).wait()
+
+
+def staged_exchange(blocks, first, second, strided_out, ident):
+    n1, n2 = blocks.shape[0], blocks.shape[1]
+    rest = blocks.shape[2:]
+    out_shape = (n2, n1) + rest if not strided_out else (n1, n2) + rest
+    most = max(n1, n2)
+    return pl.pallas_call(
+        functools.partial(staged_kernel, first, second, strided_out),
+        in_specs=[pl.BlockSpec(memory_space=pl.ANY)],
+        out_specs=pl.BlockSpec(memory_space=pl.ANY),
+        out_shape=jax.ShapeDtypeStruct(out_shape, blocks.dtype),
+        scratch_shapes=[
+            pltpu.VMEM((n2, n1) + rest, blocks.dtype),
+            pltpu.SemaphoreType.DMA((2, most)),
+            pltpu.SemaphoreType.DMA((2, most)),
+            pltpu.SemaphoreType.DMA((2,)),
+        ],
+        compiler_params=pltpu.CompilerParams(collective_id=ident, has_side_effects=True),
+    )(blocks)
+
+
 def per_device(
     tokens,
     token_owner,
@@ -316,15 +399,15 @@
     dispatch = (column[:, None] == jnp.arange(slot_count, dtype=jnp.int32)[None, :]).astype(
         jnp.bfloat16
     )
-    outgoing = jnp.einsum("tr,td->rd", dispatch, tokens, preferred_element_type=jnp.float32).astype(
-        jnp.bfloat16
-    )
-    arrived = lax.all_to_all(
-        outgoing.reshape(devices, capacity, width),
-        ("req", "mlp"),
-        split_axis=0,
-        concat_axis=0,
-        tiled=True,
+    send_column = ((my_owners % n_mlp) * n_req + my_owners // n_mlp) * capacity + my_rank
+    send_dispatch = (
+        send_column[:, None] == jnp.arange(slot_count, dtype=jnp.int32)[None, :]
+    ).astype(jnp.bfloat16)
+    outgoing = jnp.einsum(
+        "tr,td->rd", send_dispatch, tokens, preferred_element_type=jnp.float32
+    ).astype(jnp.bfloat16)
+    arrived = staged_exchange(
+        outgoing.reshape(n_mlp, n_req, capacity, width), "mlp", "req", False, 3
     )
     projections = jnp.dot(
         arrived.reshape(slot_count, width), w_qkv, preferred_element_type=jnp.float32
@@ -333,12 +416,8 @@
         owners_flat, token_request, owner_index, devices, tok_dev, capacity
     )
     attended = attend(projections, cache_k, cache_v, cache_len, global_row, slot_request, filled)
-    returned = lax.all_to_all(
-        attended.reshape(devices, capacity, width),
-        ("req", "mlp"),
-        split_axis=0,
-        concat_axis=0,
-        tiled=True,
+    returned = staged_exchange(
+        attended.reshape(n_req, n_mlp, capacity, width), "req", "mlp", True, 4
     )
     attn_rows = jnp.dot(
         dispatch, returned.reshape(slot_count, width), preferred_element_type=jnp.float32

time: 123 us -> 132 us (1.073)
  Pallas kernels: 54.7 us -> 99.6 us
  blocking collectives: 17.8 us -> 0 us
  waiting for transfers between devices: 11.8 us -> 0 us
  starting transfers between devices: 11.2 us -> 0 us
  local copies, waits for them, and re-layouts: 6.72 us -> 10.2 us
  other arithmetic: 3.46 us -> 5.15 us
    pallas_call x0 -> x2, Pallas kernels: none -> 43.3 us  [staged_exchange(): pl.pallas_call(functools.partial(staged_kernel, first, second, strided_ou...]
    all_to_all x1 -> x0, blocking collectives: 17.8 us -> none  [per_device(): lax.all_to_all(attended.reshape(devices, capacity, width), ('req', 'mlp')...]
    all_to_all x1 -> x0, waiting for transfers between devices: 11.8 us -> none  [per_device(): lax.all_to_all(outgoing.reshape(devices, capacity, width), ('req', 'mlp')...]
    all_to_all x1 -> x0, starting transfers between devices: 11.2 us -> none  [per_device(): lax.all_to_all(outgoing.reshape(devices, capacity, width), ('req', 'mlp')...]
    pallas_call x1, Pallas kernels: 16.4 us -> 17.9 us  [gather_rows(): pl.pallas_call(gather_kernel, in_specs=[pl.BlockSpec(memory_space=pltpu.V...]
    unnamed x28 -> x18, local copies, waits for them, and re-layouts: 3.07 us -> 3.7 us
  transfers between devices with their start and end apart: 1 -> 0, of which waited for: 1 -> 0; matrix products, arithmetic and copies ran while one was open for 1% -> 0% of each run, Pallas kernels for 0% -> 0%
where the time goes in v6:
time: 132 us; the launch traced here: 131 us
  Pallas kernels  99.6 us (75%)
  matrix products  15.3 us (12%)
  local copies, waits for them, and re-layouts  10.2 us (8%)
  other arithmetic  5.15 us (4%)
    pallas_call x2, Pallas kernels, staged_exchange(): pl.pallas_call(functools.partial(staged_kernel, first, second, strided_ou...  43.3 us
    pallas_call x1, Pallas kernels, attend(): pl.pallas_call(attention_kernel, grid=(pairs,), in_specs=[pl.BlockSpec((s...  19.7 us
    pallas_call x1, Pallas kernels, scatter_sum(): pl.pallas_call(scatter_kernel, in_specs=[pl.BlockSpec(memory_space=pltpu....  18.6 us
    pallas_call x1, Pallas kernels, gather_rows(): pl.pallas_call(gather_kernel, in_specs=[pl.BlockSpec(memory_space=pltpu.V...  17.9 us
    dot_general x1, matrix products, per_device(): jnp.dot(hidden, w_fc2, preferred_element_type=jnp.float32)  9.63 us
    dot_general x1, matrix products, per_device(): jnp.dot(arrived.reshape(slot_count, width), w_qkv, preferred_element_type...  4.6 us
    unnamed x18, local copies, waits for them, and re-layouts  3.7 us

profile of v6, /device:TPU:0, one launch (start us, length us, event | category | flops | bytes accessed | tf_op | source)
XLA Modules:
  0.0 130.5 jit_solution(15561419208324913339)
XLA Ops:
  0.0 0.0 copy-start
  0.0 0.0 copy-start.3
  0.0 0.8 fusion.82
  0.8 0.7 broadcast_bitcast_fusion
  1.6 0.9 compare_convert_fusion
  2.5 0.1 copy.23
  2.6 0.2 reduce_window_sum.23
  2.8 0.1 copy.24
  2.9 1.0 select_reduce_fusion
  3.9 0.1 copy.31
  4.0 0.1 select_n.100.nrow_ref
  4.2 0.1 copy.25
  4.3 0.1 copy.26
  4.4 0.1 reduce_sum.86.rfill_ref
  4.5 0.1 reshape_reshape.3.rreq_ref
  4.6 0.1 copy.28
  4.7 0.1 add.136
  4.8 0.1 copy.30
  4.9 0.1 select_n.98.ntag_ref
  5.0 0.1 fusion.47
  5.1 0.2 reduce_window_sum.22
  5.3 0.2 select_reduce_fusion.1
  5.5 0.7 fusion.50
  6.2 0.0 copy-done.3
  6.2 0.4 convolution_convert_fusion.2
  6.6 1.0 reshape.235.x_ref
  7.6 24.6 %shard_map.136 = bf16[16,8,2,1024]{3,2,1,0:T(2,128)(2,1)} custom-call(bf16[8,16,2,1024]{3,2,1,0:T(2,128)(2,1)} %reshape.235.x_ref), custom_call_target="tpu_custom_call" | custom-call | tf_op jit(solution)/shard_map/pallas_call | solution.py:353
  32.2 1.2 reshape.236
  33.4 4.6 %convolution_convert_fusion.q_ref.kn_ref.vn_ref = bf16[256,3072]{1,0:T(8,128)(2,1)S(1)} fusion(bf16[256,1024]{1,0:T(8,128)(2,1)S(1)} %reshape.236, bf16[1024,3072]{1,0:T(8,128)(2,1)} %param.20), kind=kOutput, calls=%fused_computation | convolution fusion | flops 1611399168 | bytes 8388608 | tf_op jit(solution)/shard_map/dot_general | solution.py:412
  38.0 19.7 %shard_map.137 = bf16[256,1024]{1,0:T(8,128)(2,1)S(1)} custom-call(bf16[256,3072]{1,0:T(8,128)(2,1)S(1)} %convolution_convert_fusion.q_ref.kn_ref.vn_ref, bf16[256,3072]{1,0:T(8,128)(2,1)S(1)} %convolution_convert_fusion.q_ref.kn_ref.vn_ref, bf16[256,3072]{1,0:T(8,128)(2,1)S(1)} %convolution_convert_fusion.q_ref.kn_ref.vn_ref, bf16[2048,1024]{1,0:T(8,128)(2,1)} %bitcast.29, ...), custom_call_target="tpu_custom_call" | custom-call | tf_op jit(solution)/shard_map/pallas_call | solution.py:100
  57.8 1.0 reshape.240.x_ref
  58.8 18.6 %shard_map.138 = bf16[16,8,2,1024]{3,2,1,0:T(2,128)(2,1)} custom-call(bf16[16,8,2,1024]{3,2,1,0:T(2,128)(2,1)} %reshape.240.x_ref), custom_call_target="tpu_custom_call" | custom-call | tf_op jit(solution)/shard_map/pallas_call | solution.py:353
  77.4 1.2 reshape.241
  78.7 0.0 copy-done
  78.7 0.0 copy-start.4
  78.7 0.0 copy-start.5
  78.7 0.7 fusion.83
  79.4 0.2 multiply_reduce_fusion.1
  79.6 0.0 copy-done.4
  79.6 0.0 copy-done.5
  79.6 0.2 add_convert_fusion.1.x_ref
  79.8 17.9 %shard_map.139 = bf16[1024,1024]{1,0:T(8,128)(2,1)S(1)} custom-call(bf16[128,1024]{1,0:T(8,128)(2,1)S(1)} %add_convert_fusion.1.x_ref), custom_call_target="tpu_custom_call" | custom-call | tf_op jit(solution)/shard_map/pallas_call | solution.py:270
  97.8 0.0 copy-start.2
  97.8 1.3 %copy-done.2 = bf16[1024,1024]{1,0:T(8,128)(2,1)} copy-done((bf16[1024,1024]{1,0:T(8,128)(2,1)}, bf16[1024,1024]{1,0:T(8,128)(2,1)S(1)}, u32[]{:S(2)}) %copy-start.2) | copy-done | bytes 2097176
  99.1 9.6 %convolution_convert_fusion.1.part_ref = bf16[1024,1024]{1,0:T(8,128)(2,1)} fusion(bf16[512,1024]{1,0:T(8,128)(2,1)} %param.23, bf16[1024,1024]{1,0:T(8,128)(2,1)} %copy-done.2, bf16[1024,512]{1,0:T(8,128)(2,1)} %param.22), kind=kOutput, calls=%fused_computation.20 | convolution fusion | flops 2182610944 | bytes 6291456 | tf_op jit(solution)/shard_map/dot_general | solution.py:434
  108.7 0.0 copy-start.1
  108.7 1.6 %copy-done.1 = bf16[1024,1024]{1,0:T(8,128)(2,1)S(1)} copy-done((bf16[1024,1024]{1,0:T(8,128)(2,1)S(1)}, bf16[1024,1024]{1,0:T(8,128)(2,1)}, u32[]{:S(2)}) %copy-start.1) | copy-done | bytes 2097176
  110.3 0.0 copy-start.6
  110.3 0.0 copy-start.7
  110.3 18.6 %shard_map.140 = f32[128,1024]{1,0:T(8,128)S(1)} custom-call(bf16[1024,1024]{1,0:T(8,128)(2,1)S(1)} %copy-done.1), custom_call_target="tpu_custom_call" | custom-call | tf_op jit(solution)/shard_map/pallas_call | solution.py:195
  129.0 0.3 fusion.41
  129.2 0.3 multiply_reduce_fusion
  129.5 0.0 copy-done.6
  129.5 0.0 copy-done.7
  129.5 1.0 add_convert_fusion
  (10 shorter events, 0.1 us)
Async XLA Ops:
  0.0 78.7 %copy-start = (bf16[1024,1024]{1,0:T(8,128)(2,1)S(1)}, bf16[1024,1024]{1,0:T(8,128)(2,1)}, u32[]{:S(2)}) copy-start(bf16[1024,1024]{1,0:T(8,128)(2,1)} %param.21) | copy-start | bytes 6291460
  0.0 6.2 %copy-start.3 = (bf16[128,1024]{1,0:T(8,128)(2,1)S(1)}, bf16[128,1024]{1,0:T(8,128)(2,1)}, u32[]{:S(2)}) copy-start(bf16[128,1024]{1,0:T(8,128)(2,1)} %param.14) | copy-start | bytes 786436
  78.7 0.9 copy-start.4
  78.7 0.9 copy-start.5
  97.8 1.4 %copy-start.2 = (bf16[1024,1024]{1,0:T(8,128)(2,1)}, bf16[1024,1024]{1,0:T(8,128)(2,1)S(1)}, u32[]{:S(2)}) copy-start(bf16[1024,1024]{1,0:T(8,128)(2,1)S(1)} %shard_map.139) | copy-start | bytes 6291460
  108.7 1.6 %copy-start.1 = (bf16[1024,1024]{1,0:T(8,128)(2,1)S(1)}, bf16[1024,1024]{1,0:T(8,128)(2,1)}, u32[]{:S(2)}) copy-start(bf16[1024,1024]{1,0:T(8,128)(2,1)} %convolution_convert_fusion.1.part_ref) | copy-start | bytes 6291460
  110.3 19.2 %copy-start.6 = (f32[1024]{0:T(1024)S(1)}, f32[1024]{0:T(1024)}, u32[]{:S(2)}) copy-start(f32[1024]{0:T(1024)} %param.27) | copy-start | bytes 12292
  110.3 19.2 %copy-start.7 = (f32[1024]{0:T(1024)S(1)}, f32[1024]{0:T(1024)}, u32[]{:S(2)}) copy-start(f32[1024]{0:T(1024)} %param.26) | copy-start | bytes 12292

commit v7 on v5

--- a/solution.py
+++ b/solution.py
@@ -36,44 +36,53 @@
 
 
 def attention_kernel(
-    q_ref, kn_ref, vn_ref, k_ref, v_ref, rreq_ref, rrow_ref, rfill_ref, ctag_ref, ntag_ref, nrow_ref, o_ref
+    tiles_ref, q_ref, kn_ref, vn_ref, k_ref, v_ref, rreq_ref, rrow_ref, ctag_ref, ntag_ref, nrow_ref, o_ref
 ):
     head_dim = q_ref.shape[1] // 2
     score_scale = head_dim ** (-0.5)
-    q = q_ref[...]
-    keys = k_ref[...]
-    values = v_ref[...]
+    requests = tiles_ref.shape[0] // 2
+    context = k_ref.shape[0] // requests
+    tile = 64
+    lane = lax.broadcasted_iota(jnp.int32, (1, q_ref.shape[1]), 1)
+    contract = (((1,), (1,)), ((), ()))
     key_new = kn_ref[...]
     value_new = vn_ref[...]
-    row_request = rreq_ref[...]
-    old_mask = ctag_ref[...] == row_request
-    new_mask = (ntag_ref[...] == row_request) & (nrow_ref[...] <= rrow_ref[...])
-    lane = lax.broadcasted_iota(jnp.int32, (1, q.shape[1]), 1)
-    contract = (((1,), (1,)), ((), ()))
-    result = None
-    for half in range(2):
-        in_head = (lane // head_dim) == half
-        q_head = jnp.where(in_head, q, jnp.zeros_like(q))
-        old_score = (
-            lax.dot_general(q_head, keys, contract, preferred_element_type=jnp.float32) * score_scale
-        )
-        new_score = (
-            lax.dot_general(q_head, key_new, contract, preferred_element_type=jnp.float32)
-            * score_scale
-        )
-        old_exp = jnp.where(old_mask, jnp.exp(old_score), jnp.float32(0.0))
-        new_exp = jnp.where(new_mask, jnp.exp(new_score), jnp.float32(0.0))
-        total = jnp.sum(old_exp, axis=1, keepdims=True) + jnp.sum(new_exp, axis=1, keepdims=True)
-        total = jnp.where(total > 0, total, jnp.float32(1.0))
-        inverse = 1.0 / total
-        old_weight = (old_exp * inverse).astype(jnp.bfloat16)
-        new_weight = (new_exp * inverse).astype(jnp.bfloat16)
-        part = jnp.dot(old_weight, values, preferred_element_type=jnp.float32) + jnp.dot(
-            new_weight, value_new, preferred_element_type=jnp.float32
-        )
-        result = part if result is None else jnp.where(in_head, part, result)
-    result = jnp.where(rfill_ref[...] > 0, result, jnp.float32(0.0))
-    o_ref[...] = result.astype(o_ref.dtype)
+    new_tag = ntag_ref[...]
+    new_row = nrow_ref[...]
+    o_ref[...] = jnp.zeros(o_ref.shape, o_ref.dtype)
+    for request in range(requests):
+        keys = k_ref[request * context : (request + 1) * context, :]
+        values = v_ref[request * context : (request + 1) * context, :]
+        column_tag = ctag_ref[:, request * context : (request + 1) * context]
+
+        def body(t, carry):
+            rows = pl.ds(pl.multiple_of(t * tile, tile), tile)
+            q = q_ref[rows, :] * jnp.asarray(score_scale, q_ref.dtype)
+            row_request = rreq_ref[rows, :]
+            old_mask = column_tag == row_request
+            new_mask = (new_tag == row_request) & (new_row <= rrow_ref[rows, :])
+            result = None
+            for half in range(2):
+                in_head = (lane // head_dim) == half
+                q_head = jnp.where(in_head, q, jnp.zeros_like(q))
+                old_score = lax.dot_general(q_head, keys, contract, preferred_element_type=jnp.float32)
+                new_score = lax.dot_general(q_head, key_new, contract, preferred_element_type=jnp.float32)
+                old_exp = jnp.where(old_mask, jnp.exp(old_score), jnp.float32(0.0))
+                new_exp = jnp.where(new_mask, jnp.exp(new_score), jnp.float32(0.0))
+                total = jnp.sum(old_exp, axis=1, keepdims=True) + jnp.sum(new_exp, axis=1, keepdims=True)
+                total = jnp.where(total > 0, total, jnp.float32(1.0))
+                inverse = 1.0 / total
+                old_weight = (old_exp * inverse).astype(jnp.bfloat16)
+                new_weight = (new_exp * inverse).astype(jnp.bfloat16)
+                part = jnp.dot(old_weight, values, preferred_element_type=jnp.float32) + jnp.dot(
+                    new_weight, value_new, preferred_element_type=jnp.float32
+                )
+                result = part if result is None else jnp.where(in_head, part, result)
+            previous = o_ref[rows, :]
+            o_ref[rows, :] = jnp.where(row_request == request, result.astype(o_ref.dtype), previous)
+            return carry
+
+        lax.fori_loop(tiles_ref[request], tiles_ref[requests + request], body, 0)
 
 
 def attend(projections, cache_keys, cache_values, lengths, global_row, slot_request, filled):
@@ -82,51 +91,70 @@
     requests, context = cache_keys.shape[0], cache_keys.shape[1]
     pair = 128
     pairs = width // pair
+    tile = 64
     keys = cache_keys.reshape(requests * context, width)
     values = cache_values.reshape(requests * context, width)
     key_owner = jnp.arange(requests * context, dtype=jnp.int32) // context
     key_place = jnp.arange(requests * context, dtype=jnp.int32) % context
     key_limit = jnp.repeat(lengths, context)
     column_tag = jnp.where(key_place < key_limit, key_owner, -1).reshape(1, -1)
-    new_tag = jnp.where(filled > 0, slot_request, -1).reshape(1, -1)
-    new_row = global_row.reshape(1, -1)
-    row_request = slot_request.reshape(-1, 1)
-    row_index = global_row.reshape(-1, 1)
-    row_filled = filled.reshape(-1, 1)
+    sort_key = jnp.where(filled > 0, slot_request, requests)
+    key_hot = (sort_key[:, None] == jnp.arange(requests + 1, dtype=jnp.int32)[None, :]).astype(jnp.int32)
+    counts = jnp.sum(key_hot, axis=0)
+    starts = jnp.cumsum(counts) - counts
+    before = jnp.cumsum(key_hot, axis=0) - key_hot
+    position = jnp.sum(key_hot * (starts[None, :] + before), axis=1)
+    order = position[None, :] == jnp.arange(slot_count, dtype=jnp.int32)[:, None]
+    order_int = order.astype(jnp.int32)
+    sorted_projections = jnp.dot(
+        order.astype(projections.dtype), projections, preferred_element_type=jnp.float32
+    ).astype(projections.dtype)
+    sorted_key = jnp.sum(order_int * sort_key[None, :], axis=1)
+    sorted_row = jnp.sum(order_int * global_row[None, :], axis=1)
+    first = starts[:requests] // tile
+    last = jnp.where(
+        counts[:requests] > 0, (starts[:requests] + counts[:requests] + tile - 1) // tile, first
+    )
+    tiles = jnp.concatenate([first, last]).astype(jnp.int32)
+    whole = lambda shape: pl.BlockSpec(shape, lambda p, t: (0, 0))
     keyed = requests * context
-    whole = lambda shape: pl.BlockSpec(shape, lambda p: (0, 0))
-    return pl.pallas_call(
+    sorted_out = pl.pallas_call(
         attention_kernel,
-        grid=(pairs,),
-        in_specs=[
-            pl.BlockSpec((slot_count, pair), lambda p: (0, p)),
-            pl.BlockSpec((slot_count, pair), lambda p: (0, pairs + p)),
-            pl.BlockSpec((slot_count, pair), lambda p: (0, 2 * pairs + p)),
-            pl.BlockSpec((keyed, pair), lambda p: (0, p)),
-            pl.BlockSpec((keyed, pair), lambda p: (0, p)),
-            whole((slot_count, 1)),
-            whole((slot_count, 1)),
-            whole((slot_count, 1)),
-            whole((1, keyed)),
-            whole((1, slot_count)),
-            whole((1, slot_count)),
-        ],
-        out_specs=pl.BlockSpec((slot_count, pair), lambda p: (0, p)),
+        grid_spec=pltpu.PrefetchScalarGridSpec(
+            num_scalar_prefetch=1,
+            grid=(pairs,),
+            in_specs=[
+                pl.BlockSpec((slot_count, pair), lambda p, t: (0, p)),
+                pl.BlockSpec((slot_count, pair), lambda p, t: (0, pairs + p)),
+                pl.BlockSpec((slot_count, pair), lambda p, t: (0, 2 * pairs + p)),
+                pl.BlockSpec((keyed, pair), lambda p, t: (0, p)),
+                pl.BlockSpec((keyed, pair), lambda p, t: (0, p)),
+                whole((slot_count, 1)),
+                whole((slot_count, 1)),
+                whole((1, keyed)),
+                whole((1, slot_count)),
+                whole((1, slot_count)),
+            ],
+            out_specs=pl.BlockSpec((slot_count, pair), lambda p, t: (0, p)),
+        ),
         out_shape=jax.ShapeDtypeStruct((slot_count, width), jnp.bfloat16),
         compiler_params=pltpu.CompilerParams(vmem_limit_bytes=48 * 1024 * 1024),
     )(
-        projections,
-        projections,
-        projections,
+        tiles,
+        sorted_projections,
+        sorted_projections,
+        sorted_projections,
         keys,
         values,
-        row_request,
-        row_index,
-        row_filled,
+        sorted_key.reshape(-1, 1),
+        sorted_row.reshape(-1, 1),
         column_tag,
-        new_tag,
-        new_row,
-    )
+        sorted_key.reshape(1, -1),
+        sorted_row.reshape(1, -1),
+    )
+    return jnp.dot(
+        order.T.astype(sorted_out.dtype), sorted_out, preferred_element_type=jnp.float32
+    ).astype(sorted_out.dtype)
 
 
 def scatter_kernel(part_ref, o_ref, pair_buf, send_buf, ring_buf, pair_send, pair_recv, ring_send, ring_recv):

time: 123 us -> 152 us (1.24)
  Pallas kernels: 54.7 us -> 69.7 us
  blocking collectives: 17.8 us -> 28.4 us
  waiting for transfers between devices: 11.8 us -> 9.38 us
  other arithmetic: 3.46 us -> 5.75 us
  matrix products: 16.2 us -> 18.2 us
  local copies, waits for them, and re-layouts: 6.72 us -> 8.24 us
    pallas_call x1, Pallas kernels: 19.6 us -> 34.6 us  [attend(): pl.pallas_call(attention_kernel, grid_spec=pltpu.PrefetchScalarGridSpec(n...]
    all_to_all x1, blocking collectives: 17.8 us -> 28.4 us  [per_device(): lax.all_to_all(attended.reshape(devices, capacity, width), ('req', 'mlp')...]
    all_to_all x1, waiting for transfers between devices: 11.8 us -> 9.38 us  [per_device(): lax.all_to_all(outgoing.reshape(devices, capacity, width), ('req', 'mlp')...]
    dot_general x1 -> x2, matrix products: 4.58 us -> 6.53 us  [the longest x1 6.18 us: attend(): jnp.dot(order.astype(projections.dtype), projections, preferred_element_t...]
    another operation x0 -> x3, other arithmetic: none -> 1.75 us
    unnamed x28 -> x26, local copies, waits for them, and re-layouts: 3.07 us -> 4.47 us
  transfers between devices with their start and end apart: 1 -> 1, of which waited for: 1 -> 1; matrix products, arithmetic and copies ran while one was open for 1% -> 3% of each run, Pallas kernels for 0% -> 0%
where the time goes in v7:
time: 152 us; the launch traced here: 151 us
  Pallas kernels  69.7 us (46%)
  blocking collectives  28.4 us (19%)
  matrix products  18.2 us (12%)
  starting transfers between devices  11.2 us (7%)
  waiting for transfers between devices  9.38 us (6%)
  local copies, waits for them, and re-layouts  8.24 us (5%)
  other arithmetic  5.75 us (4%)
    pallas_call x1, Pallas kernels, attend(): pl.pallas_call(attention_kernel, grid_spec=pltpu.PrefetchScalarGridSpec(n...  34.6 us
    all_to_all x1, blocking collectives, per_device(): lax.all_to_all(attended.reshape(devices, capacity, width), ('req', 'mlp')...  28.4 us
    pallas_call x1, Pallas kernels, scatter_sum(): pl.pallas_call(scatter_kernel, in_specs=[pl.BlockSpec(memory_space=pltpu....  18.6 us
    pallas_call x1, Pallas kernels, gather_rows(): pl.pallas_call(gather_kernel, in_specs=[pl.BlockSpec(memory_space=pltpu.V...  16.4 us
    all_to_all x1, starting transfers between devices, per_device(): lax.all_to_all(outgoing.reshape(devices, capacity, width), ('req', 'mlp')...  11.2 us
    dot_general x1, matrix products, per_device(): jnp.dot(hidden, w_fc2, preferred_element_type=jnp.float32)  9.63 us
    all_to_all x1, waiting for transfers between devices, per_device(): lax.all_to_all(outgoing.reshape(devices, capacity, width), ('req', 'mlp')...  9.38 us
    dot_general x1, matrix products, attend(): jnp.dot(order.astype(projections.dtype), projections, preferred_element_t...  6.18 us
  transfers between devices with their start and end apart: 1, of which 1 were waited for; matrix products, arithmetic and copies ran while one was open for 3% of the time, Pallas kernels for 0%

profile of v7, /device:TPU:0, one launch (start us, length us, event | category | flops | bytes accessed | tf_op | source)
XLA Modules:
  0.0 151.1 jit_solution(6937748645748432546)
XLA Ops:
  0.0 0.0 copy-start
  0.0 0.8 fusion.54
  0.8 0.1 fusion.49
  0.9 0.2 reduce_window_sum.44
  1.1 0.2 select_reduce_fusion.3
  1.3 0.7 fusion.53
  1.9 1.3 convolution_convert_fusion.4
  3.3 1.0 reshape.250
  4.3 11.2 %all-to-all-start = ((bf16[128,2,1024]{2,1,0:T(2,128)(2,1)}), bf16[128,2,1024]{2,1,0:T(2,128)(2,1)S(1)}, u32[]{:S(2)}, u32[]{:S(2)}) async-start(bf16[128,2,1024]{2,1,0:T(2,128)(2,1)} %reshape.250), calls=%async_computation | async-start | bytes 1048576 | tf_op jit(solution)/shard_map/all_to_all | solution.py:350
  15.4 0.0 copy-done.5
  15.5 0.1 compare_convert_fusion
  15.5 0.1 copy.25
  15.6 0.2 reduce_window_sum.45
  15.8 0.1 copy.26
  15.9 0.0 copy-done.8
  15.9 0.2 fusion.43
  16.1 0.1 copy.27
  16.2 0.1 select_n.83
  16.4 0.1 select_n.84
  16.5 0.0 copy-done.11
  16.5 0.1 broadcast_bitcast_fusion
  16.6 0.1 copy.31
  16.7 0.1 select_n.89
  16.9 0.1 convert_reduce_fusion
  17.0 0.2 reduce-window.14
  17.2 1.5 %reduce-window.18 = s32[5,2,128]{2,1,0:T(2,128)S(1)} reduce-window(s32[5,2,128]{2,1,0:T(2,128)S(1)} %compare_convert_fusion.1, s32[]{:T(128)} %constant.127.clone.1), window={size=1x1x128 pad=0_0x0_0x127_0}, to_apply=%region_7.8 | reduce-window | flops 162560 | bytes 10244 | tf_op jit(solution)/shard_map/reduce-window.1
  18.7 0.1 slice.18
  18.8 0.1 copy.29
  19.0 0.1 copy.30
  19.0 0.1 add_bitcast_fusion
  19.1 0.1 fusion.52
  19.2 0.2 select_reduce_fusion
  19.4 0.1 copy.32.rreq_ref
  19.5 0.1 copy.33.rrow_ref
  19.7 0.1 pad_add_fusion.tiles_ref
  19.8 9.4 %all-to-all-done = bf16[128,2,1024]{2,1,0:T(2,128)(2,1)S(1)} async-done(((bf16[128,2,1024]{2,1,0:T(2,128)(2,1)}), bf16[128,2,1024]{2,1,0:T(2,128)(2,1)S(1)}, u32[]{:S(2)}, u32[]{:S(2)}) %all-to-all-start) | async-done | bytes 524320 | tf_op jit(solution)/shard_map/all_to_all | solution.py:350
  29.1 0.2 reshape.251
  29.3 6.2 %convolution_convert_fusion.1.q_ref.kn_ref.vn_ref = bf16[256,3072]{1,0:T(8,128)(2,1)} fusion(bf16[256,1024]{1,0:T(8,128)(2,1)S(1)} %reshape.251, bf16[1024,3072]{1,0:T(8,128)(2,1)} %param.20, s32[256]{0:T(256)S(1)} %fusion.52), kind=kOutput, calls=%fused_computation.1 | convolution fusion | flops 2014904320 | bytes 8389632 | tf_op jit(solution)/shard_map/dot_general | solution.py:109
  35.5 1.4 copy-done.1
  36.9 34.6 %shard_map.136 = bf16[256,1024]{1,0:T(8,128)(2,1)S(1)} custom-call(s32[8]{0:T(128)S(1)} %pad_add_fusion.tiles_ref, bf16[256,3072]{1,0:T(8,128)(2,1)S(1)} %copy-done.1, bf16[256,3072]{1,0:T(8,128)(2,1)S(1)} %copy-done.1, bf16[256,3072]{1,0:T(8,128)(2,1)S(1)} %copy-done.1, bf16[2048,1024]{1,0:T(8,128)(2,1)} %bitcast.47, bf16[2048,1024]{1,0:T(8,128)(2,1)} %bitcast.48, ...), custom_call_target="tpu_custom_call" | custom-call | tf_op jit(solution)/shard_map/pallas_call | solution.py:121
  71.6 0.0 copy-start.4
  71.6 0.3 convolution_convert_fusion.3
  72.0 0.2 reshape.259
  72.2 28.4 %all_to_all.10 = bf16[128,2,1024]{2,1,0:T(2,128)(2,1)S(1)} all-to-all(bf16[128,2,1024]{2,1,0:T(2,128)(2,1)S(1)} %reshape.259), channel_id=1, replica_groups=mesh['req'=16,'mlp'=8] {'req','mlp'}, dimensions={0} | all-to-all | bytes 1048576 | tf_op jit(solution)/shard_map/all_to_all | solution.py:364
  100.6 0.2 reshape.260
  100.8 0.0 copy-done
  100.8 0.0 copy-done.4
  100.8 0.0 copy-start.6
  100.8 0.0 copy-start.7
  100.9 0.7 fusion.85
  101.6 0.2 multiply_reduce_fusion.1
  101.8 0.0 copy-done.6
  101.8 0.0 copy-done.7
  101.8 0.2 add_convert_fusion.1.x_ref
  102.0 16.4 %shard_map.137 = bf16[1024,1024]{1,0:T(8,128)(2,1)S(1)} custom-call(bf16[128,1024]{1,0:T(8,128)(2,1)S(1)} %add_convert_fusion.1.x_ref), custom_call_target="tpu_custom_call" | custom-call | tf_op jit(solution)/shard_map/pallas_call | solution.py:296
  118.4 1.3 copy-done.3
  119.7 9.6 %convolution_convert_fusion.2.part_ref = bf16[1024,1024]{1,0:T(8,128)(2,1)} fusion(bf16[512,1024]{1,0:T(8,128)(2,1)} %param.23, bf16[1024,1024]{1,0:T(8,128)(2,1)} %copy-done.3, bf16[1024,512]{1,0:T(8,128)(2,1)} %param.22), kind=kOutput, calls=%fused_computation.21 | convolution fusion | flops 2182610944 | bytes 6291456 | tf_op jit(solution)/shard_map/dot_general | solution.py:383
  129.4 1.6 %copy-done.2 = bf16[1024,1024]{1,0:T(8,128)(2,1)S(1)} copy-done((bf16[1024,1024]{1,0:T(8,128)(2,1)S(1)}, bf16[1024,1024]{1,0:T(8,128)(2,1)}, u32[]{:S(2)}) %copy-start.2) | copy-done | bytes 2097176
  131.0 18.6 %shard_map.138 = f32[128,1024]{1,0:T(8,128)S(1)} custom-call(bf16[1024,1024]{1,0:T(8,128)(2,1)S(1)} %copy-done.2), custom_call_target="tpu_custom_call" | custom-call | tf_op jit(solution)/shard_map/pallas_call | solution.py:221
  149.6 0.3 fusion.41
  149.8 0.3 multiply_reduce_fusion
  150.2 0.0 copy-done.9
  150.2 0.0 copy-done.10
  150.2 1.0 add_convert_fusion
  (22 shorter events, 0.2 us)
Async XLA Ops:
  0.0 100.8 %copy-start = (bf16[1024,1024]{1,0:T(8,128)(2,1)S(1)}, bf16[1024,1024]{1,0:T(8,128)(2,1)}, u32[]{:S(2)}) copy-start(bf16[1024,1024]{1,0:T(8,128)(2,1)} %param.21) | copy-start | bytes 6291460
  0.0 15.4 %copy-start.5 = (s32[16384,1]{0,1:T(1,128)S(1)}, s32[16384,1]{0,1:T(1,128)}, u32[]{:S(2)}) copy-start(s32[16384,1]{0,1:T(1,128)} %param.15) | copy-start | bytes 196612
  0.0 15.9 %copy-start.8 = (s32[16384]{0:T(1024)S(1)}, s32[16384]{0:T(1024)}, u32[]{:S(2)}) copy-start(s32[16384]{0:T(1024)} %param.16) | copy-start | bytes 196612
  0.8 15.7 %copy-start.11 = (s32[4]{0:T(128)S(1)}, s32[4]{0:T(128)}, u32[]{:S(2)}) copy-start(s32[4]{0:T(128)} %param.17) | copy-start | bytes 52
  4.3 24.9 %all-to-all-start = ((bf16[128,2,1024]{2,1,0:T(2,128)(2,1)}), bf16[128,2,1024]{2,1,0:T(2,128)(2,1)S(1)}, u32[]{:S(2)}, u32[]{:S(2)}) async-start(bf16[128,2,1024]{2,1,0:T(2,128)(2,1)} %reshape.250), calls=%async_computation | async-start | bytes 1048576 | tf_op jit(solution)/shard_map/all_to_all | solution.py:350
  35.5 1.4 copy-start.1
  71.6 29.2 %copy-start.4 = (bf16[128,1024]{1,0:T(8,128)(2,1)S(1)}, bf16[128,1024]{1,0:T(8,128)(2,1)}, u32[]{:S(2)}) copy-start(bf16[128,1024]{1,0:T(8,128)(2,1)} %param.14) | copy-start | bytes 786436
  100.8 0.9 copy-start.6
  100.8 0.9 copy-start.7
  118.4 1.4 copy-start.3
  129.4 1.6 %copy-start.2 = (bf16[1024,1024]{1,0:T(8,128)(2,1)S(1)}, bf16[1024,1024]{1,0:T(8,128)(2,1)}, u32[]{:S(2)}) copy-start(bf16[1024,1024]{1,0:T(8,128)(2,1)} %convolution_convert_fusion.2.part_ref) | copy-start | bytes 6291460
  131.0 19.2 %copy-start.9 = (f32[1024]{0:T(1024)S(1)}, f32[1024]{0:T(1024)}, u32[]{:S(2)}) copy-start(f32[1024]{0:T(1024)} %param.27) | copy-start | bytes 12292
  131.0 19.2 %copy-start.10 = (f32[1024]{0:T(1024)S(1)}, f32[1024]{0:T(1024)}, u32[]{:S(2)}) copy-start(f32[1024]{0:T(1024)} %param.26) | copy-start | bytes 12292

commit v8 on v5

--- a/solution.py
+++ b/solution.py
@@ -135,13 +135,16 @@
     chips = lax.axis_size("mlp") // 2
     chip, core = me // 2, lax.rem(me, 2)
     partner = chip * 2 + 1 - core
+    step = 1 - 2 * core
+    ahead = lax.rem(chip + step + chips, chips)
+    behind = lax.rem(chip - step + chips, chips)
+    across = lax.rem(chip + 2, chips)
     rows = o_ref.shape[0]
     barrier = pltpu.get_barrier_semaphore()
     pl.semaphore_signal(barrier, 1, device_id=(req, partner), device_id_type=pl.DeviceIdType.MESH)
-    for k in range(1, chips):
-        other = lax.rem(chip + k, chips) * 2 + core
-        pl.semaphore_signal(barrier, 1, device_id=(req, other), device_id_type=pl.DeviceIdType.MESH)
-    pl.semaphore_wait(barrier, chips)
+    pl.semaphore_signal(barrier, 1, device_id=(req, ahead * 2 + core), device_id_type=pl.DeviceIdType.MESH)
+    pl.semaphore_signal(barrier, 1, device_id=(req, behind * 2 + core), device_id_type=pl.DeviceIdType.MESH)
+    pl.semaphore_wait(barrier, 3)
 
     def pair_copy(z):
         block = z * 2 + 1 - core
@@ -159,30 +162,33 @@
     for z in range(chips):
         pair_copy(z).wait()
 
-    def ring_copy(k):
-        target = lax.rem(chip + k, chips)
+    def summed(z):
+        mine = part_ref[pl.ds(pl.multiple_of((z * 2 + core) * rows, rows), rows), :]
+        return mine.astype(jnp.float32) + pair_buf[z].astype(jnp.float32)
+
+    def ring_copy(kind, target):
         return pltpu.make_async_remote_copy(
-            src_ref=send_buf.at[k],
-            dst_ref=ring_buf.at[k],
-            send_sem=ring_send.at[k],
-            recv_sem=ring_recv.at[k],
+            src_ref=send_buf.at[kind],
+            dst_ref=ring_buf.at[kind],
+            send_sem=ring_send.at[kind],
+            recv_sem=ring_recv.at[kind],
             device_id=(req, target * 2 + core),
             device_id_type=pl.DeviceIdType.MESH,
         )
 
-    for k in range(1, chips):
-        target = lax.rem(chip + k, chips)
-        mine = part_ref[pl.ds(pl.multiple_of((target * 2 + core) * rows, rows), rows), :]
-        send_buf[k] = (mine.astype(jnp.float32) + pair_buf[target].astype(jnp.float32)).astype(
-            send_buf.dtype
-        )
-        ring_copy(k).start()
-    own = part_ref[pl.ds(pl.multiple_of(me * rows, rows), rows), :]
-    total = own.astype(jnp.float32) + pair_buf[chip].astype(jnp.float32)
-    for k in range(1, chips):
-        ring_copy(k).wait()
-        total = total + ring_buf[k].astype(jnp.float32)
-    o_ref[...] = total
+    send_buf[1] = summed(across).astype(send_buf.dtype)
+    ring_copy(1, ahead).start()
+    send_buf[0] = summed(behind).astype(send_buf.dtype)
+    ring_copy(0, behind).start()
+    ring_copy(1, ahead).wait_recv()
+    send_buf[2] = (summed(ahead) + ring_buf[1].astype(jnp.float32)).astype(send_buf.dtype)
+    ring_copy(2, ahead).start()
+    total = summed(chip)
+    ring_copy(0, behind).wait()
+    total = total + ring_buf[0].astype(jnp.float32)
+    ring_copy(1, ahead).wait_send()
+    ring_copy(2, ahead).wait()
+    o_ref[...] = total + ring_buf[2].astype(jnp.float32)
 
 
 def scatter_sum(partial):
@@ -197,12 +203,12 @@
         out_shape=jax.ShapeDtypeStruct((rows, width), jnp.float32),
         scratch_shapes=[
             pltpu.VMEM((chips, rows, width), partial.dtype),
-            pltpu.VMEM((chips, rows, width), partial.dtype),
-            pltpu.VMEM((chips, rows, width), partial.dtype),
-            pltpu.SemaphoreType.DMA((chips,)),
-            pltpu.SemaphoreType.DMA((chips,)),
-            pltpu.SemaphoreType.DMA((chips,)),
-            pltpu.SemaphoreType.DMA((chips,)),
+            pltpu.VMEM((3, rows, width), partial.dtype),
+            pltpu.VMEM((3, rows, width), partial.dtype),
+            pltpu.SemaphoreType.DMA((chips,)),
+            pltpu.SemaphoreType.DMA((chips,)),
+            pltpu.SemaphoreType.DMA((3,)),
+            pltpu.SemaphoreType.DMA((3,)),
         ],
         compiler_params=pltpu.CompilerParams(
             collective_id=1, has_side_effects=True, vmem_limit_bytes=48 * 1024 * 1024
@@ -216,50 +222,61 @@
     chips = lax.axis_size("mlp") // 2
     chip, core = me // 2, lax.rem(me, 2)
     partner = chip * 2 + 1 - core
+    step = 1 - 2 * core
+    ahead = lax.rem(chip + step + chips, chips)
+    behind = lax.rem(chip - step + chips, chips)
+    across = lax.rem(chip + 2, chips)
     rows = x_ref.shape[0]
     barrier = pltpu.get_barrier_semaphore()
     pl.semaphore_signal(barrier, 1, device_id=(req, partner), device_id_type=pl.DeviceIdType.MESH)
-    for k in range(1, chips):
-        other = lax.rem(chip + k, chips) * 2 + core
-        pl.semaphore_signal(barrier, 1, device_id=(req, other), device_id_type=pl.DeviceIdType.MESH)
-    pl.semaphore_wait(barrier, chips)
-
-    def block_rows(block):
-        return pl.ds(pl.multiple_of(block * rows, rows), rows)
-
-    def ring_copy(k):
-        target = lax.rem(chip + k, chips)
+    pl.semaphore_signal(barrier, 1, device_id=(req, ahead * 2 + core), device_id_type=pl.DeviceIdType.MESH)
+    pl.semaphore_signal(barrier, 1, device_id=(req, behind * 2 + core), device_id_type=pl.DeviceIdType.MESH)
+    pl.semaphore_wait(barrier, 3)
+
+    def block_rows(z):
+        return pl.ds(pl.multiple_of((z * 2 + core) * rows, rows), rows)
+
+    origins = (me // 2, behind, ahead, across)
+
+    def ring_copy(kind):
+        source = x_ref if kind < 2 else o_ref.at[block_rows(behind)]
+        origin = chip if kind < 2 else behind
+        target = ahead if kind != 1 else behind
         return pltpu.make_async_remote_copy(
-            src_ref=x_ref,
-            dst_ref=o_ref.at[block_rows(me)],
-            send_sem=ring_send.at[k],
-            recv_sem=ring_recv.at[k],
+            src_ref=source,
+            dst_ref=o_ref.at[block_rows(origin)],
+            send_sem=ring_send.at[kind],
+            recv_sem=ring_recv.at[kind],
             device_id=(req, target * 2 + core),
             device_id_type=pl.DeviceIdType.MESH,
         )
 
-    def pair_copy(k):
-        source = lax.rem(chip + chips - k, chips) * 2 + core
+    def pair_copy(kind):
+        source = x_ref if kind == 0 else o_ref.at[block_rows(origins[kind])]
         return pltpu.make_async_remote_copy(
-            src_ref=x_ref if k == 0 else o_ref.at[block_rows(source)],
-            dst_ref=o_ref.at[block_rows(source)],
-            send_sem=pair_send.at[k],
-            recv_sem=pair_recv.at[k],
+            src_ref=source,
+            dst_ref=o_ref.at[block_rows(origins[kind])],
+            send_sem=pair_send.at[kind],
+            recv_sem=pair_recv.at[kind],
             device_id=(req, partner),
             device_id_type=pl.DeviceIdType.MESH,
         )
 
-    for k in range(1, chips):
-        ring_copy(k).start()
+    ring_copy(0).start()
+    ring_copy(1).start()
     pair_copy(0).start()
-    o_ref[block_rows(me), :] = x_ref[...]
-    for k in range(1, chips):
-        ring_copy(k).wait_recv()
-        pair_copy(k).start()
-    for k in range(1, chips):
-        ring_copy(k).wait_send()
-    for k in range(chips):
-        pair_copy(k).wait()
+    o_ref[block_rows(chip), :] = x_ref[...]
+    ring_copy(0).wait_recv()
+    ring_copy(2).start()
+    pair_copy(1).start()
+    ring_copy(1).wait_recv()
+    pair_copy(2).start()
+    ring_copy(2).wait_recv()
+    pair_copy(3).start()
+    for kind in range(3):
+        ring_copy(kind).wait_send()
+    for kind in range(4):
+        pair_copy(kind).wait()
 
 
 def gather_rows(block):

time: 123 us -> 120 us (0.976)
  Pallas kernels: 54.7 us -> 52.6 us
    pallas_call x1, Pallas kernels: 16.4 us -> 14.4 us  [gather_rows(): pl.pallas_call(gather_kernel, in_specs=[pl.BlockSpec(memory_space=pltpu.V...]
  transfers between devices with their start and end apart: 1 -> 1, of which waited for: 1 -> 1; matrix products, arithmetic and copies ran while one was open for 1% -> 2% of each run, Pallas kernels for 0% -> 0%
where the time goes in v8:
time: 120 us
  Pallas kernels  52.6 us (44%)
  blocking collectives  17.8 us (15%)
  matrix products  16.2 us (14%)
  waiting for transfers between devices  11.8 us (10%)
  starting transfers between devices  11.2 us (9%)
  local copies, waits for them, and re-layouts  6.72 us (6%)
  other arithmetic  3.46 us (3%)
    pallas_call x1, Pallas kernels, attend(): pl.pallas_call(attention_kernel, grid=(pairs,), in_specs=[pl.BlockSpec((s...  19.6 us
    pallas_call x1, Pallas kernels, scatter_sum(): pl.pallas_call(scatter_kernel, in_specs=[pl.BlockSpec(memory_space=pltpu....  18.6 us
    all_to_all x1, blocking collectives, per_device(): lax.all_to_all(attended.reshape(devices, capacity, width), ('req', 'mlp')...  17.8 us
    pallas_call x1, Pallas kernels, gather_rows(): pl.pallas_call(gather_kernel, in_specs=[pl.BlockSpec(memory_space=pltpu.V...  14.4 us
    all_to_all x1, waiting for transfers between devices, per_device(): lax.all_to_all(outgoing.reshape(devices, capacity, width), ('req', 'mlp')...  11.8 us
    all_to_all x1, starting transfers between devices, per_device(): lax.all_to_all(outgoing.reshape(devices, capacity, width), ('req', 'mlp')...  11.2 us
    dot_general x1, matrix products, per_device(): jnp.dot(hidden, w_fc2, preferred_element_type=jnp.float32)  9.63 us
    dot_general x1, matrix products, per_device(): jnp.dot(arrived.reshape(slot_count, width), w_qkv, preferred_element_type...  4.58 us
  transfers between devices with their start and end apart: 1, of which 1 were waited for; matrix products, arithmetic and copies ran while one was open for 2% of the time, Pallas kernels for 0%

profile of v8, /device:TPU:0, one launch (start us, length us, event | category | flops | bytes accessed | tf_op | source)
XLA Modules:
  0.0 120.2 jit_solution(17184585518471662987)
XLA Ops:
  0.0 0.0 copy-start
  0.0 0.0 copy-start.4
  0.0 0.0 copy-start.7
  0.0 0.8 fusion.49
  0.8 0.1 fusion.47
  0.9 0.2 reduce_window_sum.22
  1.1 0.2 select_reduce_fusion.1
  1.3 0.7 fusion.48
  1.9 0.0 copy-start.8
  1.9 1.3 %convolution_convert_fusion.2 = bf16[256,1024]{1,0:T(8,128)(2,1)S(1)} fusion(bf16[128,1024]{1,0:T(8,128)(2,1)} %param.14, s32[128]{0:T(128)S(1)} %fusion.48), kind=kOutput, calls=%fused_computation.21 | convolution fusion | flops 67403776 | bytes 786944 | tf_op jit(solution)/shard_map/tr,td->rd/dot_general | solution.py:336
  3.3 0.0 copy-start.12
  3.3 1.0 reshape.234
  4.3 11.2 %all-to-all-start = ((bf16[128,2,1024]{2,1,0:T(2,128)(2,1)}), bf16[128,2,1024]{2,1,0:T(2,128)(2,1)S(1)}, u32[]{:S(2)}, u32[]{:S(2)}) async-start(bf16[128,2,1024]{2,1,0:T(2,128)(2,1)} %reshape.234), calls=%async_computation | async-start | bytes 1048576 | tf_op jit(solution)/shard_map/all_to_all | solution.py:339
  15.4 0.0 copy-done.8
  15.5 0.0 copy-done.4
  15.5 0.1 compare_convert_fusion
  15.5 0.1 copy.23
  15.6 0.2 reduce_window_sum.23
  15.8 0.1 copy.24
  15.9 0.0 copy-done.7
  15.9 0.2 select_reduce_fusion
  16.1 0.1 copy.26
  16.2 0.1 reduce_sum.86.rfill_ref
  16.3 0.1 copy.28
  16.4 0.1 add.116
  16.6 0.0 copy-done.12
  16.6 0.1 broadcast_bitcast_fusion
  16.6 0.1 copy.25
  16.8 0.1 copy.31
  16.9 0.1 select_n.85.nrow_ref
  17.0 0.1 reshape_reshape.3.rreq_ref
  17.1 0.1 copy.30
  17.2 0.1 select_n.83.ntag_ref
  17.4 11.8 %all-to-all-done = bf16[128,2,1024]{2,1,0:T(2,128)(2,1)S(1)} async-done(((bf16[128,2,1024]{2,1,0:T(2,128)(2,1)}), bf16[128,2,1024]{2,1,0:T(2,128)(2,1)S(1)}, u32[]{:S(2)}, u32[]{:S(2)}) %all-to-all-start) | async-done | bytes 524320 | tf_op jit(solution)/shard_map/all_to_all | solution.py:339
  29.2 0.2 reshape.235
  29.4 4.6 %convolution_convert_fusion.q_ref.kn_ref.vn_ref = bf16[256,3072]{1,0:T(8,128)(2,1)S(1)} fusion(bf16[256,1024]{1,0:T(8,128)(2,1)S(1)} %reshape.235, bf16[1024,3072]{1,0:T(8,128)(2,1)} %param.20), kind=kOutput, calls=%fused_computation | convolution fusion | flops 1611399168 | bytes 8388608 | tf_op jit(solution)/shard_map/dot_general | solution.py:346
  33.9 19.6 %shard_map.136 = bf16[256,1024]{1,0:T(8,128)(2,1)S(1)} custom-call(bf16[256,3072]{1,0:T(8,128)(2,1)S(1)} %convolution_convert_fusion.q_ref.kn_ref.vn_ref, bf16[256,3072]{1,0:T(8,128)(2,1)S(1)} %convolution_convert_fusion.q_ref.kn_ref.vn_ref, bf16[256,3072]{1,0:T(8,128)(2,1)S(1)} %convolution_convert_fusion.q_ref.kn_ref.vn_ref, bf16[2048,1024]{1,0:T(8,128)(2,1)} %bitcast.24, ...), custom_call_target="tpu_custom_call" | custom-call | tf_op jit(solution)/shard_map/pallas_call | solution.py:98
  53.6 0.0 copy-start.3
  53.6 0.0 copy-start.9
  53.6 0.2 reshape.239
  53.8 17.8 %all_to_all.10 = bf16[128,2,1024]{2,1,0:T(2,128)(2,1)S(1)} all-to-all(bf16[128,2,1024]{2,1,0:T(2,128)(2,1)S(1)} %reshape.239), channel_id=1, replica_groups=mesh['req'=16,'mlp'=8] {'req','mlp'}, dimensions={0} | all-to-all | bytes 1048576 | tf_op jit(solution)/shard_map/all_to_all | solution.py:353
  71.7 0.2 reshape.240
  71.9 0.0 copy-done
  71.9 0.0 copy-done.3
  71.9 0.0 copy-done.9
  71.9 0.0 copy-start.5
  71.9 0.0 copy-start.6
  71.9 0.7 fusion.80
  72.6 0.2 multiply_reduce_fusion.1
  72.8 0.0 copy-done.5
  72.8 0.0 copy-done.6
  72.8 0.2 add_convert_fusion.1.x_ref
  73.0 14.4 %shard_map.137 = bf16[1024,1024]{1,0:T(8,128)(2,1)S(1)} custom-call(bf16[128,1024]{1,0:T(8,128)(2,1)S(1)} %add_convert_fusion.1.x_ref), custom_call_target="tpu_custom_call" | custom-call | tf_op jit(solution)/shard_map/pallas_call | solution.py:285
  87.4 0.0 copy-start.2
  87.4 1.3 %copy-done.2 = bf16[1024,1024]{1,0:T(8,128)(2,1)} copy-done((bf16[1024,1024]{1,0:T(8,128)(2,1)}, bf16[1024,1024]{1,0:T(8,128)(2,1)S(1)}, u32[]{:S(2)}) %copy-start.2) | copy-done | bytes 2097176
  88.7 9.6 %convolution_convert_fusion.1.part_ref = bf16[1024,1024]{1,0:T(8,128)(2,1)} fusion(bf16[512,1024]{1,0:T(8,128)(2,1)} %param.23, bf16[1024,1024]{1,0:T(8,128)(2,1)} %copy-done.2, bf16[1024,512]{1,0:T(8,128)(2,1)} %param.22), kind=kOutput, calls=%fused_computation.20 | convolution fusion | flops 2182610944 | bytes 6291456 | tf_op jit(solution)/shard_map/dot_general | solution.py:372
  98.4 1.6 %copy-done.1 = bf16[1024,1024]{1,0:T(8,128)(2,1)S(1)} copy-done((bf16[1024,1024]{1,0:T(8,128)(2,1)S(1)}, bf16[1024,1024]{1,0:T(8,128)(2,1)}, u32[]{:S(2)}) %copy-start.1) | copy-done | bytes 2097176
  100.0 0.0 copy-start.10
  100.0 18.6 %shard_map.138 = f32[128,1024]{1,0:T(8,128)S(1)} custom-call(bf16[1024,1024]{1,0:T(8,128)(2,1)S(1)} %copy-done.1), custom_call_target="tpu_custom_call" | custom-call | tf_op jit(solution)/shard_map/pallas_call | solution.py:199
  118.6 0.3 fusion.41
  118.9 0.3 multiply_reduce_fusion
  119.2 0.0 copy-done.10
  119.2 0.0 copy-done.11
  119.2 1.0 add_convert_fusion
  (12 shorter events, 0.1 us)
Async XLA Ops:
  0.0 71.9 %copy-start = (bf16[1024,1024]{1,0:T(8,128)(2,1)S(1)}, bf16[1024,1024]{1,0:T(8,128)(2,1)}, u32[]{:S(2)}) copy-start(bf16[1024,1024]{1,0:T(8,128)(2,1)} %param.21) | copy-start | bytes 6291460
  0.0 15.5 %copy-start.4 = (s32[16384,1]{0,1:T(1,128)S(1)}, s32[16384,1]{0,1:T(1,128)}, u32[]{:S(2)}) copy-start(s32[16384,1]{0,1:T(1,128)} %param.15) | copy-start | bytes 196612
  0.0 15.9 %copy-start.7 = (s32[16384]{0:T(1024)S(1)}, s32[16384]{0:T(1024)}, u32[]{:S(2)}) copy-start(s32[16384]{0:T(1024)} %param.16) | copy-start | bytes 196612
  1.9 13.5 %copy-start.8 = (s32[128]{0:T(128)}, s32[128]{0:T(128)S(1)}, u32[]{:S(2)}) copy-start(s32[128]{0:T(128)S(1)} %fusion.48) | copy-start | bytes 1540
  3.3 13.3 %copy-start.12 = (s32[4]{0:T(128)S(1)}, s32[4]{0:T(128)}, u32[]{:S(2)}) copy-start(s32[4]{0:T(128)} %param.17) | copy-start | bytes 52
  4.3 24.9 %all-to-all-start = ((bf16[128,2,1024]{2,1,0:T(2,128)(2,1)}), bf16[128,2,1024]{2,1,0:T(2,128)(2,1)S(1)}, u32[]{:S(2)}, u32[]{:S(2)}) async-start(bf16[128,2,1024]{2,1,0:T(2,128)(2,1)} %reshape.234), calls=%async_computation | async-start | bytes 1048576 | tf_op jit(solution)/shard_map/all_to_all | solution.py:339
  53.6 18.3 %copy-start.3 = (bf16[128,1024]{1,0:T(8,128)(2,1)S(1)}, bf16[128,1024]{1,0:T(8,128)(2,1)}, u32[]{:S(2)}) copy-start(bf16[128,1024]{1,0:T(8,128)(2,1)} %param.14) | copy-start | bytes 786436
  53.6 18.3 %copy-start.9 = (s32[128]{0:T(128)S(1)}, s32[128]{0:T(128)}, u32[]{:S(2)}) copy-start(s32[128]{0:T(128)} %copy-done.8) | copy-start | bytes 1540
  71.9 0.9 copy-start.5
  71.9 0.9 copy-start.6
  87.4 1.4 %copy-start.2 = (bf16[1024,1024]{1,0:T(8,128)(2,1)}, bf16[1024,1024]{1,0:T(8,128)(2,1)S(1)}, u32[]{:S(2)}) copy-start(bf16[1024,1024]{1,0:T(8,128)(2,1)S(1)} %shard_map.137) | copy-start | bytes 6291460
  98.4 1.6 %copy-start.1 = (bf16[1024,1024]{1,0:T(8,128)(2,1)S(1)}, bf16[1024,1024]{1,0:T(8,128)(2,1)}, u32[]{:S(2)}) copy-start(bf16[1024,1024]{1,0:T(8,128)(2,1)} %convolution_convert_fusion.1.part_ref) | copy-start | bytes 6291460
  100.0 19.2 %copy-start.10 = (f32[1024]{0:T(1024)S(1)}, f32[1024]{0:T(1024)}, u32[]{:S(2)}) copy-start(f32[1024]{0:T(1024)} %param.27) | copy-start | bytes 12292
  100.0 19.2 %copy-start.11 = (f32[1024]{0:T(1024)S(1)}, f32[1024]{0:T(1024)}, u32[]{:S(2)}) copy-start(f32[1024]{0:T(1024)} %param.26) | copy-start | bytes 12292

commit v9 on v8

--- a/solution.py
+++ b/solution.py
@@ -76,7 +76,7 @@
     o_ref[...] = result.astype(o_ref.dtype)
 
 
-def attend(projections, cache_keys, cache_values, lengths, global_row, slot_request, filled):
+def attend(projections, cache_keys, cache_values, lengths, global_row, slot_request, filled, first, count):
     slot_count = projections.shape[0]
     width = projections.shape[1] // 3
     requests, context = cache_keys.shape[0], cache_keys.shape[1]
@@ -97,13 +97,13 @@
     whole = lambda shape: pl.BlockSpec(shape, lambda p: (0, 0))
     return pl.pallas_call(
         attention_kernel,
-        grid=(pairs,),
+        grid=(count,),
         in_specs=[
-            pl.BlockSpec((slot_count, pair), lambda p: (0, p)),
-            pl.BlockSpec((slot_count, pair), lambda p: (0, pairs + p)),
-            pl.BlockSpec((slot_count, pair), lambda p: (0, 2 * pairs + p)),
-            pl.BlockSpec((keyed, pair), lambda p: (0, p)),
-            pl.BlockSpec((keyed, pair), lambda p: (0, p)),
+            pl.BlockSpec((slot_count, pair), lambda p: (0, first + p)),
+            pl.BlockSpec((slot_count, pair), lambda p: (0, pairs + first + p)),
+            pl.BlockSpec((slot_count, pair), lambda p: (0, 2 * pairs + first + p)),
+            pl.BlockSpec((keyed, pair), lambda p: (0, first + p)),
+            pl.BlockSpec((keyed, pair), lambda p: (0, first + p)),
             whole((slot_count, 1)),
             whole((slot_count, 1)),
             whole((slot_count, 1)),
@@ -112,7 +112,7 @@
             whole((1, slot_count)),
         ],
         out_specs=pl.BlockSpec((slot_count, pair), lambda p: (0, p)),
-        out_shape=jax.ShapeDtypeStruct((slot_count, width), jnp.bfloat16),
+        out_shape=jax.ShapeDtypeStruct((slot_count, count * pair), jnp.bfloat16),
         compiler_params=pltpu.CompilerParams(vmem_limit_bytes=48 * 1024 * 1024),
     )(
         projections,
@@ -349,18 +349,27 @@
     global_row, slot_request, filled = slot_table(
         owners_flat, token_request, owner_index, devices, tok_dev, capacity
     )
-    attended = attend(projections, cache_k, cache_v, cache_len, global_row, slot_request, filled)
-    returned = lax.all_to_all(
-        attended.reshape(devices, capacity, width),
-        ("req", "mlp"),
-        split_axis=0,
-        concat_axis=0,
-        tiled=True,
-    )
-    attn_rows = jnp.dot(
-        dispatch, returned.reshape(slot_count, width), preferred_element_type=jnp.float32
-    ).astype(jnp.bfloat16)
-    projected_out = jnp.dot(attn_rows, w_out, preferred_element_type=jnp.float32)
+    halves = 2
+    per_half = width // 128 // halves
+    projected_out = None
+    for half in range(halves):
+        attended = attend(
+            projections, cache_k, cache_v, cache_len, global_row, slot_request, filled,
+            half * per_half, per_half,
+        )
+        returned = lax.all_to_all(
+            attended.reshape(devices, capacity, per_half * 128),
+            ("req", "mlp"),
+            split_axis=0,
+            concat_axis=0,
+            tiled=True,
+        )
+        attn_rows = jnp.dot(
+            dispatch, returned.reshape(slot_count, per_half * 128), preferred_element_type=jnp.float32
+        ).astype(jnp.bfloat16)
+        columns = slice(half * per_half * 128, (half + 1) * per_half * 128)
+        product = jnp.dot(attn_rows, w_out[columns, :], preferred_element_type=jnp.float32)
+        projected_out = product if projected_out is None else projected_out + product
     normed = layer_norm(projected_out + tokens.astype(jnp.float32), ln1_gain, ln1_bias).astype(
         jnp.bfloat16
     )

time: 120 us -> 129 us (1.075)
  blocking collectives: 17.8 us -> 0 us
  starting transfers between devices: 11.2 us -> 25.7 us
  waiting for transfers between devices: 11.8 us -> 20.7 us
  matrix products: 16.2 us -> 17.7 us
  Pallas kernels: 52.6 us -> 53.9 us
    all_to_all x1 -> x0, blocking collectives: 17.8 us -> none  [per_device(): lax.all_to_all(attended.reshape(devices, capacity, width), ('req', 'mlp')...]
    all_to_all x0 -> x2, starting transfers between devices: none -> 14.6 us  [per_device(): lax.all_to_all(attended.reshape(devices, capacity, per_half * 128), ('req...]
    all_to_all x0 -> x2, waiting for transfers between devices: none -> 8.91 us  [per_device(): lax.all_to_all(attended.reshape(devices, capacity, per_half * 128), ('req...]
    dot_general x1 -> x2, matrix products: 0.69 us -> 3.48 us  [per_device(): jnp.dot(attn_rows, w_out[columns, :], preferred_element_type=jnp.float32)]
    reshape x2 -> x4, local copies, waits for them, and re-layouts: 0.4 us -> 1.8 us  [the longest x2 1.6 us: per_device(): attended.reshape(devices, capacity, per_half * 128)]
    unnamed x28 -> x30, local copies, waits for them, and re-layouts: 3.07 us -> 1.88 us
    pallas_call x1 -> x2, Pallas kernels: 19.6 us -> 20.8 us  [attend(): pl.pallas_call(attention_kernel, grid=(count,), in_specs=[pl.BlockSpec((s...]
  transfers between devices with their start and end apart: 1 -> 3, of which waited for: 1 -> 2; matrix products, arithmetic and copies ran while one was open for 2% -> 3% of each run, Pallas kernels for 0% -> 8%
where the time goes in v9:
time: 129 us
  Pallas kernels  53.9 us (42%)
  starting transfers between devices  25.7 us (20%)
  waiting for transfers between devices  20.7 us (16%)
  matrix products  17.7 us (14%)
  local copies, waits for them, and re-layouts  6.88 us (5%)
  other arithmetic  3.45 us (3%)
    pallas_call x2, Pallas kernels, attend(): pl.pallas_call(attention_kernel, grid=(count,), in_specs=[pl.BlockSpec((s...  20.8 us
    pallas_call x1, Pallas kernels, scatter_sum(): pl.pallas_call(scatter_kernel, in_specs=[pl.BlockSpec(memory_space=pltpu....  18.4 us
    pallas_call x1, Pallas kernels, gather_rows(): pl.pallas_call(gather_kernel, in_specs=[pl.BlockSpec(memory_space=pltpu.V...  14.7 us
    all_to_all x2, starting transfers between devices, per_device(): lax.all_to_all(attended.reshape(devices, capacity, per_half * 128), ('req...  14.6 us
    all_to_all x1, waiting for transfers between devices, per_device(): lax.all_to_all(outgoing.reshape(devices, capacity, width), ('req', 'mlp')...  11.8 us
    all_to_all x1, starting transfers between devices, per_device(): lax.all_to_all(outgoing.reshape(devices, capacity, width), ('req', 'mlp')...  11.2 us
    all_to_all x2, waiting for transfers between devices, per_device(): lax.all_to_all(attended.reshape(devices, capacity, per_half * 128), ('req...  8.91 us
    dot_general x1, matrix products, per_device(): jnp.dot(hidden, w_fc2, preferred_element_type=jnp.float32)  8.34 us
  transfers between devices with their start and end apart: 3, of which 2 were waited for; matrix products, arithmetic and copies ran while one was open for 3% of the time, Pallas kernels for 8%

profile of v9, /device:TPU:0, one launch (start us, length us, event | category | flops | bytes accessed | tf_op | source)
XLA Modules:
  0.0 128.8 jit_solution(4892404089280734042)
XLA Ops:
  0.0 0.0 copy-start
  0.0 0.8 fusion.55
  0.8 0.1 fusion.53
  0.9 0.2 reduce_window_sum.22
  1.0 0.2 select_reduce_fusion.1
  1.2 0.7 fusion.54
  1.9 1.3 %convolution_convert_fusion.2 = bf16[256,1024]{1,0:T(8,128)(2,1)S(1)} fusion(bf16[128,1024]{1,0:T(8,128)(2,1)} %param.14, s32[128]{0:T(128)S(1)} %fusion.54), kind=kOutput, calls=%fused_computation.21 | convolution fusion | flops 67403776 | bytes 786944 | tf_op jit(solution)/shard_map/tr,td->rd/dot_general | solution.py:336
  3.2 0.0 copy-start.13
  3.2 1.0 reshape.245
  4.2 0.0 copy-done.9
  4.2 11.2 %all-to-all-start = ((bf16[128,2,1024]{2,1,0:T(2,128)(2,1)}), bf16[128,2,1024]{2,1,0:T(2,128)(2,1)S(1)}, u32[]{:S(2)}, u32[]{:S(2)}) async-start(bf16[128,2,1024]{2,1,0:T(2,128)(2,1)} %reshape.245), calls=%async_computation | async-start | bytes 1048576 | tf_op jit(solution)/shard_map/all_to_all | solution.py:339
  15.4 0.0 copy-done.5
  15.4 0.1 compare_convert_fusion
  15.5 0.1 copy.25
  15.6 0.2 reduce_window_sum.23
  15.7 0.1 copy.26
  15.9 0.0 copy-done.8
  15.9 0.2 select_reduce_fusion
  16.0 0.1 copy.28
  16.2 0.1 reduce_sum.86.rfill_ref
  16.3 0.1 copy.30
  16.4 0.1 add.122
  16.5 0.0 copy-done.13
  16.5 0.1 broadcast_bitcast_fusion
  16.6 0.1 copy.27
  16.7 0.1 copy.33
  16.8 0.1 select_n.90.nrow_ref
  17.0 0.1 reshape_reshape.3.rreq_ref
  17.0 0.1 copy.32
  17.2 0.1 select_n.88.ntag_ref
  17.3 11.8 %all-to-all-done = bf16[128,2,1024]{2,1,0:T(2,128)(2,1)S(1)} async-done(((bf16[128,2,1024]{2,1,0:T(2,128)(2,1)}), bf16[128,2,1024]{2,1,0:T(2,128)(2,1)S(1)}, u32[]{:S(2)}, u32[]{:S(2)}) %all-to-all-start) | async-done | bytes 524320 | tf_op jit(solution)/shard_map/all_to_all | solution.py:339
  29.1 0.2 reshape.246
  29.3 4.6 %convolution_convert_fusion.q_ref.kn_ref.vn_ref = bf16[256,3072]{1,0:T(8,128)(2,1)S(1)} fusion(bf16[256,1024]{1,0:T(8,128)(2,1)S(1)} %reshape.246, bf16[1024,3072]{1,0:T(8,128)(2,1)} %param.20), kind=kOutput, calls=%fused_computation | convolution fusion | flops 1611399168 | bytes 8388608 | tf_op jit(solution)/shard_map/dot_general | solution.py:346
  33.9 10.4 %shard_map.136 = bf16[256,512]{1,0:T(8,128)(2,1)S(1)} custom-call(bf16[256,3072]{1,0:T(8,128)(2,1)S(1)} %convolution_convert_fusion.q_ref.kn_ref.vn_ref, bf16[256,3072]{1,0:T(8,128)(2,1)S(1)} %convolution_convert_fusion.q_ref.kn_ref.vn_ref, bf16[256,3072]{1,0:T(8,128)(2,1)S(1)} %convolution_convert_fusion.q_ref.kn_ref.vn_ref, bf16[2048,1024]{1,0:T(8,128)(2,1)} %bitcast.24, ...), custom_call_target="tpu_custom_call" | custom-call | tf_op jit(solution)/shard_map/pallas_call | solution.py:98
  44.3 0.8 reshape.250
  45.1 4.6 %all-to-all-start.1 = ((bf16[128,2,512]{2,1,0:T(2,128)(2,1)}), bf16[128,2,512]{2,1,0:T(2,128)(2,1)S(1)}, u32[]{:S(2)}, u32[]{:S(2)}) async-start(bf16[128,2,512]{2,1,0:T(2,128)(2,1)} %reshape.250), calls=%async_computation.1 | async-start | bytes 524288 | tf_op jit(solution)/shard_map/all_to_all | solution.py:360
  49.7 10.4 %shard_map.137 = bf16[256,512]{1,0:T(8,128)(2,1)S(1)} custom-call(bf16[256,3072]{1,0:T(8,128)(2,1)S(1)} %convolution_convert_fusion.q_ref.kn_ref.vn_ref, bf16[256,3072]{1,0:T(8,128)(2,1)S(1)} %convolution_convert_fusion.q_ref.kn_ref.vn_ref, bf16[256,3072]{1,0:T(8,128)(2,1)S(1)} %convolution_convert_fusion.q_ref.kn_ref.vn_ref, bf16[2048,1024]{1,0:T(8,128)(2,1)} %bitcast.25, ...), custom_call_target="tpu_custom_call" | custom-call | tf_op jit(solution)/shard_map/pallas_call | solution.py:98
  60.1 0.0 copy-start.4
  60.2 0.0 copy-start.10
  60.2 0.8 reshape.252
  61.0 0.0 all-to-all-done.1
  61.0 9.9 %all-to-all-start.2 = ((bf16[128,2,512]{2,1,0:T(2,128)(2,1)}), bf16[128,2,512]{2,1,0:T(2,128)(2,1)S(1)}, u32[]{:S(2)}, u32[]{:S(2)}) async-start(bf16[128,2,512]{2,1,0:T(2,128)(2,1)} %reshape.252), calls=%async_computation.2 | async-start | bytes 524288 | tf_op jit(solution)/shard_map/all_to_all | solution.py:360
  70.9 0.1 reshape.251
  71.0 1.7 %fusion.11 = f32[128,1024]{1,0:T(8,128)S(1)} fusion(bf16[256,512]{1,0:T(8,128)(2,1)S(1)} %reshape.251, bf16[1024,1024]{1,0:T(8,128)(2,1)} %param.21, s32[128]{0:T(128)} %copy-done.9), kind=kOutput, calls=%fused_computation.26 | convolution fusion | flops 167870464 | bytes 1835520 | tf_op jit(solution)/shard_map/dot_general | solution.py:371
  72.7 0.0 copy-start.6
  72.7 0.0 copy-start.7
  72.7 8.9 %all-to-all-done.2 = bf16[128,2,512]{2,1,0:T(2,128)(2,1)S(1)} async-done(((bf16[128,2,512]{2,1,0:T(2,128)(2,1)}), bf16[128,2,512]{2,1,0:T(2,128)(2,1)S(1)}, u32[]{:S(2)}, u32[]{:S(2)}) %all-to-all-start.2) | async-done | bytes 262176 | tf_op jit(solution)/shard_map/all_to_all | solution.py:360
  81.7 0.1 reshape.253
  81.8 0.0 copy-done.4
  81.8 0.0 copy-done.10
  81.8 1.8 %fusion.86 = (f32[128]{0:T(128)S(1)}, f32[128,1024]{1,0:T(8,128)S(1)}) fusion(bf16[128,1024]{1,0:T(8,128)(2,1)S(1)} %copy-done.4, f32[128,1024]{1,0:T(8,128)S(1)} %fusion.11, bf16[1024,1024]{1,0:T(8,128)(2,1)} %param.21, bf16[256,512]{1,0:T(8,128)(2,1)S(1)} %reshape.253, s32[128]{0:T(128)S(1)} %copy-done.10), kind=kOutput, calls=%fused_computation.130 | convolution fusion | flops 168394624 | bytes 2622464 | tf_op jit(solution)/shard_map/dot_general | solution.py:371
  83.6 0.2 multiply_reduce_fusion.1
  83.8 0.0 copy-done.6
  83.8 0.2 add_convert_fusion.1.x_ref
  84.0 0.4 copy-done.2
  84.4 14.7 %shard_map.138 = bf16[1024,1024]{1,0:T(8,128)(2,1)S(1)} custom-call(bf16[128,1024]{1,0:T(8,128)(2,1)S(1)} %add_convert_fusion.1.x_ref), custom_call_target="tpu_custom_call" | custom-call | tf_op jit(solution)/shard_map/pallas_call | solution.py:285
  99.0 1.3 %copy-done.1 = bf16[1024,1024]{1,0:T(8,128)(2,1)} copy-done((bf16[1024,1024]{1,0:T(8,128)(2,1)}, bf16[1024,1024]{1,0:T(8,128)(2,1)S(1)}, u32[]{:S(2)}) %copy-start.1) | copy-done | bytes 2097176
  100.4 8.3 %convolution_convert_fusion.1.part_ref = bf16[1024,1024]{1,0:T(8,128)(2,1)S(1)} fusion(bf16[512,1024]{1,0:T(8,128)(2,1)S(1)} %copy-done, bf16[1024,1024]{1,0:T(8,128)(2,1)} %copy-done.1, bf16[1024,512]{1,0:T(8,128)(2,1)} %param.22), kind=kOutput, calls=%fused_computation.20 | convolution fusion | flops 2182610944 | bytes 6291456 | tf_op jit(solution)/shard_map/dot_general | solution.py:381
  108.7 0.0 copy-start.11
  108.8 0.0 copy-start.12
  108.8 18.4 %shard_map.139 = f32[128,1024]{1,0:T(8,128)S(1)} custom-call(bf16[1024,1024]{1,0:T(8,128)(2,1)S(1)} %convolution_convert_fusion.1.part_ref), custom_call_target="tpu_custom_call" | custom-call | tf_op jit(solution)/shard_map/pallas_call | solution.py:199
  127.2 0.3 fusion.45
  127.5 0.3 multiply_reduce_fusion
  127.8 1.0 add_convert_fusion
  (21 shorter events, 0.1 us)
Async XLA Ops:
  0.0 100.4 %copy-start = (bf16[512,1024]{1,0:T(8,128)(2,1)S(1)}, bf16[512,1024]{1,0:T(8,128)(2,1)}, u32[]{:S(2)}) copy-start(bf16[512,1024]{1,0:T(8,128)(2,1)} %param.23) | copy-start | bytes 3145732
  0.0 15.4 %copy-start.5 = (s32[16384,1]{0,1:T(1,128)S(1)}, s32[16384,1]{0,1:T(1,128)}, u32[]{:S(2)}) copy-start(s32[16384,1]{0,1:T(1,128)} %param.15) | copy-start | bytes 196612
  0.0 15.9 %copy-start.8 = (s32[16384]{0:T(1024)S(1)}, s32[16384]{0:T(1024)}, u32[]{:S(2)}) copy-start(s32[16384]{0:T(1024)} %param.16) | copy-start | bytes 196612
  1.9 2.4 %copy-start.9 = (s32[128]{0:T(128)}, s32[128]{0:T(128)S(1)}, u32[]{:S(2)}) copy-start(s32[128]{0:T(128)S(1)} %fusion.54) | copy-start | bytes 1540
  3.2 13.3 %copy-start.13 = (s32[4]{0:T(128)S(1)}, s32[4]{0:T(128)}, u32[]{:S(2)}) copy-start(s32[4]{0:T(128)} %param.17) | copy-start | bytes 52
  4.2 24.9 %all-to-all-start = ((bf16[128,2,1024]{2,1,0:T(2,128)(2,1)}), bf16[128,2,1024]{2,1,0:T(2,128)(2,1)S(1)}, u32[]{:S(2)}, u32[]{:S(2)}) async-start(bf16[128,2,1024]{2,1,0:T(2,128)(2,1)} %reshape.245), calls=%async_computation | async-start | bytes 1048576 | tf_op jit(solution)/shard_map/all_to_all | solution.py:339
  45.1 15.8 %all-to-all-start.1 = ((bf16[128,2,512]{2,1,0:T(2,128)(2,1)}), bf16[128,2,512]{2,1,0:T(2,128)(2,1)S(1)}, u32[]{:S(2)}, u32[]{:S(2)}) async-start(bf16[128,2,512]{2,1,0:T(2,128)(2,1)} %reshape.250), calls=%async_computation.1 | async-start | bytes 524288 | tf_op jit(solution)/shard_map/all_to_all | solution.py:360
  60.1 21.6 %copy-start.4 = (bf16[128,1024]{1,0:T(8,128)(2,1)S(1)}, bf16[128,1024]{1,0:T(8,128)(2,1)}, u32[]{:S(2)}) copy-start(bf16[128,1024]{1,0:T(8,128)(2,1)} %param.14) | copy-start | bytes 786436
  60.2 21.6 %copy-start.10 = (s32[128]{0:T(128)S(1)}, s32[128]{0:T(128)}, u32[]{:S(2)}) copy-start(s32[128]{0:T(128)} %copy-done.9) | copy-start | bytes 1540
  61.0 20.7 %all-to-all-start.2 = ((bf16[128,2,512]{2,1,0:T(2,128)(2,1)}), bf16[128,2,512]{2,1,0:T(2,128)(2,1)S(1)}, u32[]{:S(2)}, u32[]{:S(2)}) async-start(bf16[128,2,512]{2,1,0:T(2,128)(2,1)} %reshape.252), calls=%async_computation.2 | async-start | bytes 524288 | tf_op jit(solution)/shard_map/all_to_all | solution.py:360
  72.7 11.1 %copy-start.6 = (f32[1024]{0:T(1024)S(1)}, f32[1024]{0:T(1024)}, u32[]{:S(2)}) copy-start(f32[1024]{0:T(1024)} %param.25) | copy-start | bytes 12292
  72.7 11.1 %copy-start.7 = (f32[1024]{0:T(1024)S(1)}, f32[1024]{0:T(1024)}, u32[]{:S(2)}) copy-start(f32[1024]{0:T(1024)} %param.24) | copy-start | bytes 12292
  83.6 0.8 copy-start.2
  99.0 1.4 %copy-start.1 = (bf16[1024,1024]{1,0:T(8,128)(2,1)}, bf16[1024,1024]{1,0:T(8,128)(2,1)S(1)}, u32[]{:S(2)}) copy-start(bf16[1024,1024]{1,0:T(8,128)(2,1)S(1)} %shard_map.138) | copy-start | bytes 6291460
  108.7 18.5 %copy-start.3 = (f32[128,1024]{1,0:T(8,128)S(1)}, f32[128,1024]{1,0:T(8,128)}, u32[]{:S(2)}) copy-start(f32[128,1024]{1,0:T(8,128)} %copy-done.2) | copy-start | bytes 1572868
  108.7 19.1 %copy-start.11 = (f32[1024]{0:T(1024)S(1)}, f32[1024]{0:T(1024)}, u32[]{:S(2)}) copy-start(f32[1024]{0:T(1024)} %param.27) | copy-start | bytes 12292
  108.8 19.1 %copy-start.12 = (f32[1024]{0:T(1024)S(1)}, f32[1024]{0:T(1024)}, u32[]{:S(2)}) copy-start(f32[1024]{0:T(1024)} %param.26) | copy-start | bytes 12292

commit v10 on v8

--- a/solution.py
+++ b/solution.py
@@ -216,7 +216,9 @@
     )(partial)
 
 
-def gather_kernel(x_ref, o_ref, ring_send, ring_recv, pair_send, pair_recv):
+def gather_kernel(
+    x_ref, w1_ref, w2_ref, o_ref, held, ring_send, ring_recv, pair_send, pair_recv
+):
     req = lax.axis_index("req")
     me = lax.axis_index("mlp")
     chips = lax.axis_size("mlp") // 2
@@ -233,18 +235,18 @@
     pl.semaphore_signal(barrier, 1, device_id=(req, behind * 2 + core), device_id_type=pl.DeviceIdType.MESH)
     pl.semaphore_wait(barrier, 3)
 
-    def block_rows(z):
-        return pl.ds(pl.multiple_of((z * 2 + core) * rows, rows), rows)
-
-    origins = (me // 2, behind, ahead, across)
+    def block_rows(z, which):
+        return pl.ds(pl.multiple_of((z * 2 + which) * rows, rows), rows)
+
+    origins = (chip, behind, ahead, across)
 
     def ring_copy(kind):
-        source = x_ref if kind < 2 else o_ref.at[block_rows(behind)]
+        source = x_ref if kind < 2 else held.at[block_rows(behind, core)]
         origin = chip if kind < 2 else behind
         target = ahead if kind != 1 else behind
         return pltpu.make_async_remote_copy(
             src_ref=source,
-            dst_ref=o_ref.at[block_rows(origin)],
+            dst_ref=held.at[block_rows(origin, core)],
             send_sem=ring_send.at[kind],
             recv_sem=ring_recv.at[kind],
             device_id=(req, target * 2 + core),
@@ -252,42 +254,60 @@
         )
 
     def pair_copy(kind):
-        source = x_ref if kind == 0 else o_ref.at[block_rows(origins[kind])]
+        source = x_ref if kind == 0 else held.at[block_rows(origins[kind], core)]
         return pltpu.make_async_remote_copy(
             src_ref=source,
-            dst_ref=o_ref.at[block_rows(origins[kind])],
+            dst_ref=held.at[block_rows(origins[kind], core)],
             send_sem=pair_send.at[kind],
             recv_sem=pair_recv.at[kind],
             device_id=(req, partner),
             device_id_type=pl.DeviceIdType.MESH,
         )
 
+    def feed_forward(block, place):
+        hidden = jnp.dot(block, w1_ref[...], preferred_element_type=jnp.float32)
+        hidden = (hidden * 0.5 * (1.0 + lax.erf(hidden * (2.0 ** -0.5)))).astype(jnp.bfloat16)
+        o_ref[place, :] = jnp.dot(hidden, w2_ref[...], preferred_element_type=jnp.float32).astype(
+            o_ref.dtype
+        )
+
     ring_copy(0).start()
     ring_copy(1).start()
     pair_copy(0).start()
-    o_ref[block_rows(chip), :] = x_ref[...]
+    feed_forward(x_ref[...], block_rows(chip, core))
     ring_copy(0).wait_recv()
     ring_copy(2).start()
     pair_copy(1).start()
+    feed_forward(held[block_rows(behind, core), :], block_rows(behind, core))
     ring_copy(1).wait_recv()
     pair_copy(2).start()
+    feed_forward(held[block_rows(ahead, core), :], block_rows(ahead, core))
     ring_copy(2).wait_recv()
     pair_copy(3).start()
+    feed_forward(held[block_rows(across, core), :], block_rows(across, core))
+    partner_origins = (chip, ahead, behind, across)
+    for kind in range(4):
+        copy = pair_copy(kind)
+        copy.wait_recv()
+        place = block_rows(partner_origins[kind], 1 - core)
+        feed_forward(held[place, :], place)
     for kind in range(3):
         ring_copy(kind).wait_send()
     for kind in range(4):
-        pair_copy(kind).wait()
-
-
-def gather_rows(block):
+        pair_copy(kind).wait_send()
+
+
+def gather_rows(block, w_fc1, w_fc2):
     groups = lax.axis_size("mlp")
     chips = groups // 2
+    total = groups * block.shape[0]
     return pl.pallas_call(
         gather_kernel,
-        in_specs=[pl.BlockSpec(memory_space=pltpu.VMEM)],
+        in_specs=[pl.BlockSpec(memory_space=pltpu.VMEM)] * 3,
         out_specs=pl.BlockSpec(memory_space=pltpu.VMEM),
-        out_shape=jax.ShapeDtypeStruct((groups * block.shape[0], block.shape[1]), block.dtype),
+        out_shape=jax.ShapeDtypeStruct((total, w_fc2.shape[1]), jnp.bfloat16),
         scratch_shapes=[
+            pltpu.VMEM((total, block.shape[1]), block.dtype),
             pltpu.SemaphoreType.DMA((chips,)),
             pltpu.SemaphoreType.DMA((chips,)),
             pltpu.SemaphoreType.DMA((chips,)),
@@ -296,7 +316,7 @@
         compiler_params=pltpu.CompilerParams(
             collective_id=2, has_side_effects=True, vmem_limit_bytes=48 * 1024 * 1024
         ),
-    )(block)
+    )(block, w_fc1, w_fc2)
 
 
 def per_device(
@@ -364,13 +384,7 @@
     normed = layer_norm(projected_out + tokens.astype(jnp.float32), ln1_gain, ln1_bias).astype(
         jnp.bfloat16
     )
-    gathered = gather_rows(normed)
-    hidden = jax.nn.gelu(
-        jnp.dot(gathered, w_fc1, preferred_element_type=jnp.float32), approximate=False
-    ).astype(jnp.bfloat16)
-    summed = scatter_sum(
-        jnp.dot(hidden, w_fc2, preferred_element_type=jnp.float32).astype(jnp.bfloat16)
-    )
+    summed = scatter_sum(gather_rows(normed, w_fc1, w_fc2))
     return layer_norm(normed.astype(jnp.float32) + summed, ln2_gain, ln2_bias).astype(jnp.bfloat16)
 
 

time: 120 us -> 117 us (0.975)
  matrix products: 16.2 us -> 8.39 us
  other arithmetic: 3.46 us -> 5.53 us
  Pallas kernels: 52.6 us -> 54.5 us
    dot_general x1 -> x0, matrix products: 9.63 us -> none  [per_device(): jnp.dot(hidden, w_fc2, preferred_element_type=jnp.float32)]
    reshape x1, local copies, waits for them, and re-layouts: 0.2 us -> 2.12 us  [per_device(): returned.reshape(slot_count, width)]
    dot_general x1, matrix products: 0.69 us -> 2.47 us  [per_device(): jnp.dot(attn_rows, w_out, preferred_element_type=jnp.float32)]
    unnamed x28 -> x30, local copies, waits for them, and re-layouts: 3.07 us -> 1.36 us
    pallas_call x1, Pallas kernels: 14.4 us -> 16 us  [gather_rows(): pl.pallas_call(gather_kernel, in_specs=[pl.BlockSpec(memory_space=pltpu.V...]
where the time goes in v10:
time: 117 us
  Pallas kernels  54.5 us (47%)
  blocking collectives  18.4 us (16%)
  waiting for transfers between devices  11.8 us (10%)
  starting transfers between devices  11.2 us (10%)
  matrix products  8.39 us (7%)
  local copies, waits for them, and re-layouts  6.95 us (6%)
  other arithmetic  5.53 us (5%)
    pallas_call x1, Pallas kernels, attend(): pl.pallas_call(attention_kernel, grid=(pairs,), in_specs=[pl.BlockSpec((s...  19.7 us
    pallas_call x1, Pallas kernels, scatter_sum(): pl.pallas_call(scatter_kernel, in_specs=[pl.BlockSpec(memory_space=pltpu....  18.7 us
    all_to_all x1, blocking collectives, per_device(): lax.all_to_all(attended.reshape(devices, capacity, width), ('req', 'mlp')...  18.4 us
    pallas_call x1, Pallas kernels, gather_rows(): pl.pallas_call(gather_kernel, in_specs=[pl.BlockSpec(memory_space=pltpu.V...  16 us
    all_to_all x1, waiting for transfers between devices, per_device(): lax.all_to_all(outgoing.reshape(devices, capacity, width), ('req', 'mlp')...  11.8 us
    all_to_all x1, starting transfers between devices, per_device(): lax.all_to_all(outgoing.reshape(devices, capacity, width), ('req', 'mlp')...  11.2 us
    dot_general x1, matrix products, per_device(): jnp.dot(arrived.reshape(slot_count, width), w_qkv, preferred_element_type...  4.58 us
    dot_general x1, matrix products, per_device(): jnp.dot(attn_rows, w_out, preferred_element_type=jnp.float32)  2.47 us
  transfers between devices with their start and end apart: 1, of which 1 were waited for; matrix products, arithmetic and copies ran while one was open for 2% of the time, Pallas kernels for 0%

profile of v10, /device:TPU:0, one launch (start us, length us, event | category | flops | bytes accessed | tf_op | source)
XLA Modules:
  0.0 117.0 jit_solution(1930701957326060887)
XLA Ops:
  0.0 0.0 copy-start
  0.0 0.0 copy-start.5
  0.0 0.0 copy-start.8
  0.0 0.0 copy-start.13
  0.0 0.8 fusion.8
  0.8 0.1 fusion.6
  0.9 0.2 reduce_window_sum.22
  1.1 0.2 select_reduce_fusion.1
  1.3 0.7 fusion.7
  1.9 1.3 %convolution_convert_fusion.1 = bf16[256,1024]{1,0:T(8,128)(2,1)S(1)} fusion(bf16[128,1024]{1,0:T(8,128)(2,1)} %param.14, s32[128]{0:T(128)S(1)} %fusion.7), kind=kOutput, calls=%fused_computation.1 | convolution fusion | flops 67403776 | bytes 786944 | tf_op jit(solution)/shard_map/tr,td->rd/dot_general | solution.py:356
  3.3 1.0 reshape.234
  4.3 11.2 %all-to-all-start = ((bf16[128,2,1024]{2,1,0:T(2,128)(2,1)}), bf16[128,2,1024]{2,1,0:T(2,128)(2,1)S(1)}, u32[]{:S(2)}, u32[]{:S(2)}) async-start(bf16[128,2,1024]{2,1,0:T(2,128)(2,1)} %reshape.234), calls=%async_computation | async-start | bytes 1048576 | tf_op jit(solution)/shard_map/all_to_all | solution.py:359
  15.4 0.0 copy-done.9
  15.5 0.0 copy-done.5
  15.5 0.1 compare_convert_fusion
  15.5 0.1 copy.23
  15.6 0.2 reduce_window_sum.23
  15.8 0.1 copy.24
  15.9 0.0 copy-done.8
  15.9 0.2 select_reduce_fusion
  16.1 0.1 copy.26
  16.2 0.1 reduce_sum.86.rfill_ref
  16.3 0.1 copy.28
  16.4 0.1 add.116
  16.6 0.0 copy-done.13
  16.6 0.1 broadcast_bitcast_fusion
  16.6 0.1 copy.25
  16.8 0.1 copy.31
  16.9 0.1 select_n.85.nrow_ref
  17.0 0.1 reshape_reshape.3.rreq_ref
  17.1 0.1 copy.30
  17.2 0.1 select_n.83.ntag_ref
  17.4 11.8 %all-to-all-done = bf16[128,2,1024]{2,1,0:T(2,128)(2,1)S(1)} async-done(((bf16[128,2,1024]{2,1,0:T(2,128)(2,1)}), bf16[128,2,1024]{2,1,0:T(2,128)(2,1)S(1)}, u32[]{:S(2)}, u32[]{:S(2)}) %all-to-all-start) | async-done | bytes 524320 | tf_op jit(solution)/shard_map/all_to_all | solution.py:359
  29.2 0.2 reshape.235
  29.4 4.6 %convolution_convert_fusion.q_ref.kn_ref.vn_ref = bf16[256,3072]{1,0:T(8,128)(2,1)S(1)} fusion(bf16[256,1024]{1,0:T(8,128)(2,1)S(1)} %reshape.235, bf16[1024,3072]{1,0:T(8,128)(2,1)} %param.20), kind=kOutput, calls=%fused_computation | convolution fusion | flops 1611399168 | bytes 8388608 | tf_op jit(solution)/shard_map/dot_general | solution.py:366
  33.9 19.7 %shard_map.136 = bf16[256,1024]{1,0:T(8,128)(2,1)S(1)} custom-call(bf16[256,3072]{1,0:T(8,128)(2,1)S(1)} %convolution_convert_fusion.q_ref.kn_ref.vn_ref, bf16[256,3072]{1,0:T(8,128)(2,1)S(1)} %convolution_convert_fusion.q_ref.kn_ref.vn_ref, bf16[256,3072]{1,0:T(8,128)(2,1)S(1)} %convolution_convert_fusion.q_ref.kn_ref.vn_ref, bf16[2048,1024]{1,0:T(8,128)(2,1)} %bitcast.21, ...), custom_call_target="tpu_custom_call" | custom-call | tf_op jit(solution)/shard_map/pallas_call | solution.py:98
  53.6 0.0 copy-start.4
  53.7 0.0 copy-start.10
  53.7 0.2 reshape.239
  53.9 0.0 copy-start.6
  53.9 0.0 copy-start.7
  53.9 18.4 %all_to_all.10 = bf16[128,2,1024]{2,1,0:T(2,128)(2,1)} all-to-all(bf16[128,2,1024]{2,1,0:T(2,128)(2,1)S(1)} %reshape.239), channel_id=1, replica_groups=mesh['req'=16,'mlp'=8] {'req','mlp'}, dimensions={0} | all-to-all | bytes 1048576 | tf_op jit(solution)/shard_map/all_to_all | solution.py:373
  72.3 2.1 %reshape.240 = bf16[256,1024]{1,0:T(8,128)(2,1)} reshape(bf16[128,2,1024]{2,1,0:T(2,128)(2,1)} %all_to_all.10) | data formatting | bytes 1048576 | tf_op jit(solution)/shard_map/reshape | solution.py:381
  74.4 0.0 copy-done
  74.4 0.0 copy-done.4
  74.4 0.0 copy-done.10
  74.4 2.5 %fusion.9 = (f32[128]{0:T(128)S(1)}, f32[128,1024]{1,0:T(8,128)}) fusion(bf16[128,1024]{1,0:T(8,128)(2,1)S(1)} %copy-done.4, bf16[1024,1024]{1,0:T(8,128)(2,1)S(1)} %copy-done, bf16[256,1024]{1,0:T(8,128)(2,1)} %reshape.240, s32[128]{0:T(128)S(1)} %copy-done.10), kind=kOutput, calls=%fused_computation.44 | convolution fusion | flops 336101248 | bytes 3408896 | tf_op jit(solution)/shard_map/dot_general | solution.py:383
  76.9 1.2 %multiply_reduce_fusion.1 = f32[128]{0:T(128)S(1)} fusion(f32[128,1024]{1,0:T(8,128)} %get-tuple-element.12, f32[128]{0:T(128)S(1)} %broadcast_multiply_fusion.1), kind=kLoop, calls=%fused_computation.8 | loop fusion | flops 393088 | bytes 525312 | tf_op jit(solution)/shard_map/reduce_sum | solution.py:16
  78.1 0.0 copy-done.6
  78.1 0.0 copy-done.7
  78.2 1.2 %add_convert_fusion.1.x_ref = bf16[128,1024]{1,0:T(8,128)(2,1)S(1)} fusion(f32[128,1024]{1,0:T(8,128)} %get-tuple-element.12, f32[1024]{0:T(1024)S(1)} %copy-done.6, f32[1024]{0:T(1024)S(1)} %copy-done.7, f32[128]{0:T(128)S(1)} %add_rsqrt_fusion.1, f32[128]{0:T(128)S(1)} %broadcast_multiply_fusion.1), kind=kLoop, calls=%fused_computation.7 | loop fusion | flops 655360 | bytes 795648 | tf_op jit(solution)/shard_map/convert_element_type | solution.py:384
  79.4 0.0 copy-done.1
  79.4 0.0 copy-start.2
  79.4 1.2 %copy-done.2 = bf16[512,1024]{1,0:T(8,128)(2,1)S(1)} copy-done((bf16[512,1024]{1,0:T(8,128)(2,1)S(1)}, bf16[512,1024]{1,0:T(8,128)(2,1)}, u32[]{:S(2)}) %copy-start.2) | copy-done | bytes 1048600
  80.6 16.0 %shard_map.137.part_ref = bf16[1024,1024]{1,0:T(8,128)(2,1)S(1)} custom-call(bf16[128,1024]{1,0:T(8,128)(2,1)S(1)} %add_convert_fusion.1.x_ref, bf16[1024,512]{1,0:T(8,128)(2,1)S(1)} %copy-done.1, bf16[512,1024]{1,0:T(8,128)(2,1)S(1)} %copy-done.2), custom_call_target="tpu_custom_call" | custom-call | tf_op jit(solution)/shard_map/pallas_call | solution.py:304
  96.6 0.0 copy-start.11
  96.6 0.0 copy-start.12
  96.7 18.7 %shard_map.138 = f32[128,1024]{1,0:T(8,128)S(1)} custom-call(bf16[1024,1024]{1,0:T(8,128)(2,1)S(1)} %shard_map.137.part_ref), custom_call_target="tpu_custom_call" | custom-call | tf_op jit(solution)/shard_map/pallas_call | solution.py:199
  115.4 0.0 copy-done.3
  115.4 0.3 fusion
  115.7 0.3 multiply_reduce_fusion
  116.0 0.0 copy-done.11
  116.0 0.0 copy-done.12
  116.0 1.0 add_convert_fusion
  (13 shorter events, 0.1 us)
Async XLA Ops:
  0.0 74.4 %copy-start = (bf16[1024,1024]{1,0:T(8,128)(2,1)S(1)}, bf16[1024,1024]{1,0:T(8,128)(2,1)}, u32[]{:S(2)}) copy-start(bf16[1024,1024]{1,0:T(8,128)(2,1)} %param.21) | copy-start | bytes 6291460
  0.0 15.5 %copy-start.5 = (s32[16384,1]{0,1:T(1,128)S(1)}, s32[16384,1]{0,1:T(1,128)}, u32[]{:S(2)}) copy-start(s32[16384,1]{0,1:T(1,128)} %param.15) | copy-start | bytes 196612
  0.0 15.9 %copy-start.8 = (s32[16384]{0:T(1024)S(1)}, s32[16384]{0:T(1024)}, u32[]{:S(2)}) copy-start(s32[16384]{0:T(1024)} %param.16) | copy-start | bytes 196612
  0.0 16.6 %copy-start.13 = (s32[4]{0:T(128)S(1)}, s32[4]{0:T(128)}, u32[]{:S(2)}) copy-start(s32[4]{0:T(128)} %param.17) | copy-start | bytes 52
  1.9 13.5 %copy-start.9 = (s32[128]{0:T(128)}, s32[128]{0:T(128)S(1)}, u32[]{:S(2)}) copy-start(s32[128]{0:T(128)S(1)} %fusion.7) | copy-start | bytes 1540
  4.3 24.9 %all-to-all-start = ((bf16[128,2,1024]{2,1,0:T(2,128)(2,1)}), bf16[128,2,1024]{2,1,0:T(2,128)(2,1)S(1)}, u32[]{:S(2)}, u32[]{:S(2)}) async-start(bf16[128,2,1024]{2,1,0:T(2,128)(2,1)} %reshape.234), calls=%async_computation | async-start | bytes 1048576 | tf_op jit(solution)/shard_map/all_to_all | solution.py:359
  53.6 20.8 %copy-start.4 = (bf16[128,1024]{1,0:T(8,128)(2,1)S(1)}, bf16[128,1024]{1,0:T(8,128)(2,1)}, u32[]{:S(2)}) copy-start(bf16[128,1024]{1,0:T(8,128)(2,1)} %param.14) | copy-start | bytes 786436
  53.7 20.8 %copy-start.10 = (s32[128]{0:T(128)S(1)}, s32[128]{0:T(128)}, u32[]{:S(2)}) copy-start(s32[128]{0:T(128)} %copy-done.9) | copy-start | bytes 1540
  53.9 24.3 %copy-start.6 = (f32[1024]{0:T(1024)S(1)}, f32[1024]{0:T(1024)}, u32[]{:S(2)}) copy-start(f32[1024]{0:T(1024)} %param.25) | copy-start | bytes 12292
  53.9 24.3 %copy-start.7 = (f32[1024]{0:T(1024)S(1)}, f32[1024]{0:T(1024)}, u32[]{:S(2)}) copy-start(f32[1024]{0:T(1024)} %param.24) | copy-start | bytes 12292
  72.3 7.1 %copy-start.1 = (bf16[1024,512]{1,0:T(8,128)(2,1)S(1)}, bf16[1024,512]{1,0:T(8,128)(2,1)}, u32[]{:S(2)}) copy-start(bf16[1024,512]{1,0:T(8,128)(2,1)} %w1_ref.1) | copy-start | bytes 3145732
  79.4 1.2 %copy-start.2 = (bf16[512,1024]{1,0:T(8,128)(2,1)S(1)}, bf16[512,1024]{1,0:T(8,128)(2,1)}, u32[]{:S(2)}) copy-start(bf16[512,1024]{1,0:T(8,128)(2,1)} %w2_ref.1) | copy-start | bytes 3145732
  80.6 34.8 %copy-start.3 = (f32[128,1024]{1,0:T(8,128)S(1)}, f32[128,1024]{1,0:T(8,128)}, u32[]{:S(2)}) copy-start(f32[128,1024]{1,0:T(8,128)} %get-tuple-element.12) | copy-start | bytes 1572868
  96.6 19.4 %copy-start.11 = (f32[1024]{0:T(1024)S(1)}, f32[1024]{0:T(1024)}, u32[]{:S(2)}) copy-start(f32[1024]{0:T(1024)} %param.27) | copy-start | bytes 12292
  96.6 19.4 %copy-start.12 = (f32[1024]{0:T(1024)S(1)}, f32[1024]{0:T(1024)}, u32[]{:S(2)}) copy-start(f32[1024]{0:T(1024)} %param.26) | copy-start | bytes 12292

commit v11 on v10

--- a/solution.py
+++ b/solution.py
@@ -357,7 +357,7 @@
         jnp.bfloat16
     )
     arrived = lax.all_to_all(
-        outgoing.reshape(devices, capacity, width),
+        outgoing.reshape(devices, capacity * width // 128, 128),
         ("req", "mlp"),
         split_axis=0,
         concat_axis=0,
@@ -371,7 +371,7 @@
     )
     attended = attend(projections, cache_k, cache_v, cache_len, global_row, slot_request, filled)
     returned = lax.all_to_all(
-        attended.reshape(devices, capacity, width),
+        attended.reshape(devices, capacity * width // 128, 128),
         ("req", "mlp"),
         split_axis=0,
         concat_axis=0,

time: 117 us -> 118 us (level)
  no operation moved by 1% of the time
where the time goes in v11:
time: 118 us; the launch traced here: 117 us
  Pallas kernels  54.4 us (46%)
  blocking collectives  18.4 us (16%)
  waiting for transfers between devices  11.8 us (10%)
  starting transfers between devices  11.2 us (9%)
  matrix products  8.39 us (7%)
  local copies, waits for them, and re-layouts  7.04 us (6%)
  other arithmetic  5.53 us (5%)
    pallas_call x1, Pallas kernels, attend(): pl.pallas_call(attention_kernel, grid=(pairs,), in_specs=[pl.BlockSpec((s...  19.7 us
    pallas_call x1, Pallas kernels, scatter_sum(): pl.pallas_call(scatter_kernel, in_specs=[pl.BlockSpec(memory_space=pltpu....  18.7 us
    all_to_all x1, blocking collectives, per_device(): lax.all_to_all(attended.reshape(devices, capacity * width // 128, 128), (...  18.4 us
    pallas_call x1, Pallas kernels, gather_rows(): pl.pallas_call(gather_kernel, in_specs=[pl.BlockSpec(memory_space=pltpu.V...  16 us
    all_to_all x1, waiting for transfers between devices, per_device(): lax.all_to_all(outgoing.reshape(devices, capacity * width // 128, 128), (...  11.8 us
    all_to_all x1, starting transfers between devices, per_device(): lax.all_to_all(outgoing.reshape(devices, capacity * width // 128, 128), (...  11.2 us
    dot_general x1, matrix products, per_device(): jnp.dot(arrived.reshape(slot_count, width), w_qkv, preferred_element_type...  4.58 us
    dot_general x1, matrix products, per_device(): jnp.dot(attn_rows, w_out, preferred_element_type=jnp.float32)  2.47 us
  transfers between devices with their start and end apart: 1, of which 1 were waited for; matrix products, arithmetic and copies ran while one was open for 2% of the time, Pallas kernels for 0%

profile of v11, /device:TPU:0, one launch (start us, length us, event | category | flops | bytes accessed | tf_op | source)
XLA Modules:
  0.0 117.0 jit_solution(9077862979665507215)
XLA Ops:
  0.0 0.0 copy-start
  0.0 0.0 copy-start.5
  0.0 0.0 copy-start.8
  0.0 0.0 copy-start.13
  0.0 0.8 fusion.8
  0.8 0.1 fusion.6
  0.9 0.2 reduce_window_sum.22
  1.1 0.2 select_reduce_fusion.1
  1.3 0.7 fusion.7
  1.9 1.3 %convolution_convert_fusion.1 = bf16[256,1024]{1,0:T(8,128)(2,1)S(1)} fusion(bf16[128,1024]{1,0:T(8,128)(2,1)} %param.14, s32[128]{0:T(128)S(1)} %fusion.7), kind=kOutput, calls=%fused_computation.1 | convolution fusion | flops 67403776 | bytes 786944 | tf_op jit(solution)/shard_map/tr,td->rd/dot_general | solution.py:356
  3.3 1.0 reshape.234
  4.3 11.2 %all-to-all-start = ((bf16[128,16,128]{2,1,0:T(8,128)(2,1)}), bf16[128,16,128]{2,1,0:T(8,128)(2,1)S(1)}, u32[]{:S(2)}, u32[]{:S(2)}) async-start(bf16[128,16,128]{2,1,0:T(8,128)(2,1)} %reshape.234), calls=%async_computation | async-start | bytes 1048576 | tf_op jit(solution)/shard_map/all_to_all | solution.py:359
  15.5 0.0 copy-done.9
  15.5 0.0 copy-done.5
  15.5 0.1 compare_convert_fusion
  15.6 0.1 copy.23
  15.7 0.2 reduce_window_sum.23
  15.8 0.1 copy.24
  15.9 0.0 copy-done.8
  16.0 0.2 select_reduce_fusion
  16.1 0.1 copy.26
  16.3 0.1 reduce_sum.86.rfill_ref
  16.4 0.1 copy.28
  16.5 0.1 add.116
  16.6 0.0 copy-done.13
  16.6 0.1 broadcast_bitcast_fusion
  16.7 0.1 copy.25
  16.8 0.1 copy.31
  16.9 0.1 select_n.85.nrow_ref
  17.0 0.1 reshape_reshape.3.rreq_ref
  17.1 0.1 copy.30
  17.2 0.1 select_n.83.ntag_ref
  17.4 11.8 %all-to-all-done = bf16[128,16,128]{2,1,0:T(8,128)(2,1)S(1)} async-done(((bf16[128,16,128]{2,1,0:T(8,128)(2,1)}), bf16[128,16,128]{2,1,0:T(8,128)(2,1)S(1)}, u32[]{:S(2)}, u32[]{:S(2)}) %all-to-all-start) | async-done | bytes 524320 | tf_op jit(solution)/shard_map/all_to_all | solution.py:359
  29.2 0.2 reshape.235
  29.4 4.6 %convolution_convert_fusion.q_ref.kn_ref.vn_ref = bf16[256,3072]{1,0:T(8,128)(2,1)S(1)} fusion(bf16[256,1024]{1,0:T(8,128)(2,1)S(1)} %reshape.235, bf16[1024,3072]{1,0:T(8,128)(2,1)} %param.20), kind=kOutput, calls=%fused_computation | convolution fusion | flops 1611399168 | bytes 8388608 | tf_op jit(solution)/shard_map/dot_general | solution.py:366
  34.0 19.7 %shard_map.136 = bf16[256,1024]{1,0:T(8,128)(2,1)S(1)} custom-call(bf16[256,3072]{1,0:T(8,128)(2,1)S(1)} %convolution_convert_fusion.q_ref.kn_ref.vn_ref, bf16[256,3072]{1,0:T(8,128)(2,1)S(1)} %convolution_convert_fusion.q_ref.kn_ref.vn_ref, bf16[256,3072]{1,0:T(8,128)(2,1)S(1)} %convolution_convert_fusion.q_ref.kn_ref.vn_ref, bf16[2048,1024]{1,0:T(8,128)(2,1)} %bitcast.21, ...), custom_call_target="tpu_custom_call" | custom-call | tf_op jit(solution)/shard_map/pallas_call | solution.py:98
  53.7 0.0 copy-start.4
  53.7 0.0 copy-start.10
  53.7 0.2 reshape.239
  53.9 0.0 copy-start.6
  53.9 0.0 copy-start.7
  54.0 18.4 %all_to_all.10 = bf16[128,16,128]{2,1,0:T(8,128)(2,1)} all-to-all(bf16[128,16,128]{2,1,0:T(8,128)(2,1)S(1)} %reshape.239), channel_id=1, replica_groups=mesh['req'=16,'mlp'=8] {'req','mlp'}, dimensions={0} | all-to-all | bytes 1048576 | tf_op jit(solution)/shard_map/all_to_all | solution.py:373
  72.3 2.1 %reshape.240 = bf16[256,1024]{1,0:T(8,128)(2,1)} reshape(bf16[128,16,128]{2,1,0:T(8,128)(2,1)} %all_to_all.10) | data formatting | bytes 1048576 | tf_op jit(solution)/shard_map/reshape | solution.py:381
  74.5 0.0 copy-done
  74.5 0.0 copy-done.4
  74.5 0.0 copy-done.10
  74.5 2.5 %fusion.9 = (f32[128]{0:T(128)S(1)}, f32[128,1024]{1,0:T(8,128)}) fusion(bf16[128,1024]{1,0:T(8,128)(2,1)S(1)} %copy-done.4, bf16[1024,1024]{1,0:T(8,128)(2,1)S(1)} %copy-done, bf16[256,1024]{1,0:T(8,128)(2,1)} %reshape.240, s32[128]{0:T(128)S(1)} %copy-done.10), kind=kOutput, calls=%fused_computation.44 | convolution fusion | flops 336101248 | bytes 3408896 | tf_op jit(solution)/shard_map/dot_general | solution.py:383
  77.0 1.2 %multiply_reduce_fusion.1 = f32[128]{0:T(128)S(1)} fusion(f32[128,1024]{1,0:T(8,128)} %get-tuple-element.12, f32[128]{0:T(128)S(1)} %broadcast_multiply_fusion.1), kind=kLoop, calls=%fused_computation.8 | loop fusion | flops 393088 | bytes 525312 | tf_op jit(solution)/shard_map/reduce_sum | solution.py:16
  78.2 0.0 copy-done.6
  78.2 0.0 copy-done.7
  78.2 1.2 %add_convert_fusion.1.x_ref = bf16[128,1024]{1,0:T(8,128)(2,1)S(1)} fusion(f32[128,1024]{1,0:T(8,128)} %get-tuple-element.12, f32[1024]{0:T(1024)S(1)} %copy-done.6, f32[1024]{0:T(1024)S(1)} %copy-done.7, f32[128]{0:T(128)S(1)} %add_rsqrt_fusion.1, f32[128]{0:T(128)S(1)} %broadcast_multiply_fusion.1), kind=kLoop, calls=%fused_computation.7 | loop fusion | flops 655360 | bytes 795648 | tf_op jit(solution)/shard_map/convert_element_type | solution.py:384
  79.4 0.0 copy-done.1
  79.4 0.0 copy-start.2
  79.5 1.2 %copy-done.2 = bf16[512,1024]{1,0:T(8,128)(2,1)S(1)} copy-done((bf16[512,1024]{1,0:T(8,128)(2,1)S(1)}, bf16[512,1024]{1,0:T(8,128)(2,1)}, u32[]{:S(2)}) %copy-start.2) | copy-done | bytes 1048600
  80.7 16.0 %shard_map.137.part_ref = bf16[1024,1024]{1,0:T(8,128)(2,1)S(1)} custom-call(bf16[128,1024]{1,0:T(8,128)(2,1)S(1)} %add_convert_fusion.1.x_ref, bf16[1024,512]{1,0:T(8,128)(2,1)S(1)} %copy-done.1, bf16[512,1024]{1,0:T(8,128)(2,1)S(1)} %copy-done.2), custom_call_target="tpu_custom_call" | custom-call | tf_op jit(solution)/shard_map/pallas_call | solution.py:304
  96.7 0.0 copy-start.11
  96.7 0.0 copy-start.12
  96.7 18.7 %shard_map.138 = f32[128,1024]{1,0:T(8,128)S(1)} custom-call(bf16[1024,1024]{1,0:T(8,128)(2,1)S(1)} %shard_map.137.part_ref), custom_call_target="tpu_custom_call" | custom-call | tf_op jit(solution)/shard_map/pallas_call | solution.py:199
  115.5 0.0 copy-done.3
  115.5 0.3 fusion
  115.7 0.3 multiply_reduce_fusion
  116.1 0.0 copy-done.11
  116.1 0.0 copy-done.12
  116.1 1.0 add_convert_fusion
  (13 shorter events, 0.1 us)
Async XLA Ops:
  0.0 74.5 %copy-start = (bf16[1024,1024]{1,0:T(8,128)(2,1)S(1)}, bf16[1024,1024]{1,0:T(8,128)(2,1)}, u32[]{:S(2)}) copy-start(bf16[1024,1024]{1,0:T(8,128)(2,1)} %param.21) | copy-start | bytes 6291460
  0.0 15.5 %copy-start.5 = (s32[16384,1]{0,1:T(1,128)S(1)}, s32[16384,1]{0,1:T(1,128)}, u32[]{:S(2)}) copy-start(s32[16384,1]{0,1:T(1,128)} %param.15) | copy-start | bytes 196612
  0.0 15.9 %copy-start.8 = (s32[16384]{0:T(1024)S(1)}, s32[16384]{0:T(1024)}, u32[]{:S(2)}) copy-start(s32[16384]{0:T(1024)} %param.16) | copy-start | bytes 196612
  0.0 16.6 %copy-start.13 = (s32[4]{0:T(128)S(1)}, s32[4]{0:T(128)}, u32[]{:S(2)}) copy-start(s32[4]{0:T(128)} %param.17) | copy-start | bytes 52
  1.9 13.5 %copy-start.9 = (s32[128]{0:T(128)}, s32[128]{0:T(128)S(1)}, u32[]{:S(2)}) copy-start(s32[128]{0:T(128)S(1)} %fusion.7) | copy-start | bytes 1540
  4.3 24.9 %all-to-all-start = ((bf16[128,16,128]{2,1,0:T(8,128)(2,1)}), bf16[128,16,128]{2,1,0:T(8,128)(2,1)S(1)}, u32[]{:S(2)}, u32[]{:S(2)}) async-start(bf16[128,16,128]{2,1,0:T(8,128)(2,1)} %reshape.234), calls=%async_computation | async-start | bytes 1048576 | tf_op jit(solution)/shard_map/all_to_all | solution.py:359
  53.7 20.8 %copy-start.4 = (bf16[128,1024]{1,0:T(8,128)(2,1)S(1)}, bf16[128,1024]{1,0:T(8,128)(2,1)}, u32[]{:S(2)}) copy-start(bf16[128,1024]{1,0:T(8,128)(2,1)} %param.14) | copy-start | bytes 786436
  53.7 20.8 %copy-start.10 = (s32[128]{0:T(128)S(1)}, s32[128]{0:T(128)}, u32[]{:S(2)}) copy-start(s32[128]{0:T(128)} %copy-done.9) | copy-start | bytes 1540
  53.9 24.3 %copy-start.6 = (f32[1024]{0:T(1024)S(1)}, f32[1024]{0:T(1024)}, u32[]{:S(2)}) copy-start(f32[1024]{0:T(1024)} %param.25) | copy-start | bytes 12292
  53.9 24.3 %copy-start.7 = (f32[1024]{0:T(1024)S(1)}, f32[1024]{0:T(1024)}, u32[]{:S(2)}) copy-start(f32[1024]{0:T(1024)} %param.24) | copy-start | bytes 12292
  72.3 7.1 %copy-start.1 = (bf16[1024,512]{1,0:T(8,128)(2,1)S(1)}, bf16[1024,512]{1,0:T(8,128)(2,1)}, u32[]{:S(2)}) copy-start(bf16[1024,512]{1,0:T(8,128)(2,1)} %w1_ref.1) | copy-start | bytes 3145732
  79.4 1.2 %copy-start.2 = (bf16[512,1024]{1,0:T(8,128)(2,1)S(1)}, bf16[512,1024]{1,0:T(8,128)(2,1)}, u32[]{:S(2)}) copy-start(bf16[512,1024]{1,0:T(8,128)(2,1)} %w2_ref.1) | copy-start | bytes 3145732
  80.7 34.8 %copy-start.3 = (f32[128,1024]{1,0:T(8,128)S(1)}, f32[128,1024]{1,0:T(8,128)}, u32[]{:S(2)}) copy-start(f32[128,1024]{1,0:T(8,128)} %get-tuple-element.12) | copy-start | bytes 1572868
  96.7 19.4 %copy-start.11 = (f32[1024]{0:T(1024)S(1)}, f32[1024]{0:T(1024)}, u32[]{:S(2)}) copy-start(f32[1024]{0:T(1024)} %param.27) | copy-start | bytes 12292
  96.7 19.4 %copy-start.12 = (f32[1024]{0:T(1024)S(1)}, f32[1024]{0:T(1024)}, u32[]{:S(2)}) copy-start(f32[1024]{0:T(1024)} %param.26) | copy-start | bytes 12292

commit v12 on v10

--- a/solution.py
+++ b/solution.py
@@ -217,8 +217,12 @@
 
 
 def gather_kernel(
-    x_ref, w1_ref, w2_ref, o_ref, held, ring_send, ring_recv, pair_send, pair_recv
+    x_ref, w1_hbm, w2_hbm, o_ref, held, w1_ref, w2_ref, load_sem, ring_send, ring_recv, pair_send, pair_recv
 ):
+    load_one = pltpu.make_async_copy(w1_hbm, w1_ref, load_sem.at[0])
+    load_two = pltpu.make_async_copy(w2_hbm, w2_ref, load_sem.at[1])
+    load_one.start()
+    load_two.start()
     req = lax.axis_index("req")
     me = lax.axis_index("mlp")
     chips = lax.axis_size("mlp") // 2
@@ -274,6 +278,8 @@
     ring_copy(0).start()
     ring_copy(1).start()
     pair_copy(0).start()
+    load_one.wait()
+    load_two.wait()
     feed_forward(x_ref[...], block_rows(chip, core))
     ring_copy(0).wait_recv()
     ring_copy(2).start()
@@ -303,11 +309,18 @@
     total = groups * block.shape[0]
     return pl.pallas_call(
         gather_kernel,
-        in_specs=[pl.BlockSpec(memory_space=pltpu.VMEM)] * 3,
+        in_specs=[
+            pl.BlockSpec(memory_space=pltpu.VMEM),
+            pl.BlockSpec(memory_space=pl.ANY),
+            pl.BlockSpec(memory_space=pl.ANY),
+        ],
         out_specs=pl.BlockSpec(memory_space=pltpu.VMEM),
         out_shape=jax.ShapeDtypeStruct((total, w_fc2.shape[1]), jnp.bfloat16),
         scratch_shapes=[
             pltpu.VMEM((total, block.shape[1]), block.dtype),
+            pltpu.VMEM(w_fc1.shape, w_fc1.dtype),
+            pltpu.VMEM(w_fc2.shape, w_fc2.dtype),
+            pltpu.SemaphoreType.DMA((2,)),
             pltpu.SemaphoreType.DMA((chips,)),
             pltpu.SemaphoreType.DMA((chips,)),
             pltpu.SemaphoreType.DMA((chips,)),

time: 117 us -> 118 us (level)
  no operation moved by 1% of the time
where the time goes in v12:
time: 118 us; the launch traced here: 117 us
  Pallas kernels  54.7 us (46%)
  blocking collectives  18.4 us (16%)
  waiting for transfers between devices  11.8 us (10%)
  starting transfers between devices  11.2 us (9%)
  matrix products  8.39 us (7%)
  local copies, waits for them, and re-layouts  6.95 us (6%)
  other arithmetic  5.53 us (5%)
    pallas_call x1, Pallas kernels, attend(): pl.pallas_call(attention_kernel, grid=(pairs,), in_specs=[pl.BlockSpec((s...  19.7 us
    pallas_call x1, Pallas kernels, scatter_sum(): pl.pallas_call(scatter_kernel, in_specs=[pl.BlockSpec(memory_space=pltpu....  18.7 us
    all_to_all x1, blocking collectives, per_device(): lax.all_to_all(attended.reshape(devices, capacity, width), ('req', 'mlp')...  18.4 us
    pallas_call x1, Pallas kernels, gather_rows(): pl.pallas_call(gather_kernel, in_specs=[pl.BlockSpec(memory_space=pltpu.V...  16.3 us
    all_to_all x1, waiting for transfers between devices, per_device(): lax.all_to_all(outgoing.reshape(devices, capacity, width), ('req', 'mlp')...  11.8 us
    all_to_all x1, starting transfers between devices, per_device(): lax.all_to_all(outgoing.reshape(devices, capacity, width), ('req', 'mlp')...  11.2 us
    dot_general x1, matrix products, per_device(): jnp.dot(arrived.reshape(slot_count, width), w_qkv, preferred_element_type...  4.58 us
    dot_general x1, matrix products, per_device(): jnp.dot(attn_rows, w_out, preferred_element_type=jnp.float32)  2.47 us
  transfers between devices with their start and end apart: 1, of which 1 were waited for; matrix products, arithmetic and copies ran while one was open for 2% of the time, Pallas kernels for 0%

profile of v12, /device:TPU:0, one launch (start us, length us, event | category | flops | bytes accessed | tf_op | source)
XLA Modules:
  0.0 117.3 jit_solution(8262618913425284375)
XLA Ops:
  0.0 0.0 copy-start
  0.0 0.0 copy-start.5
  0.0 0.0 copy-start.8
  0.0 0.0 copy-start.13
  0.0 0.8 fusion.8
  0.8 0.1 fusion.6
  0.9 0.2 reduce_window_sum.22
  1.1 0.2 select_reduce_fusion.1
  1.3 0.7 fusion.7
  1.9 1.3 %convolution_convert_fusion.1 = bf16[256,1024]{1,0:T(8,128)(2,1)S(1)} fusion(bf16[128,1024]{1,0:T(8,128)(2,1)} %param.14, s32[128]{0:T(128)S(1)} %fusion.7), kind=kOutput, calls=%fused_computation.1 | convolution fusion | flops 67403776 | bytes 786944 | tf_op jit(solution)/shard_map/tr,td->rd/dot_general | solution.py:369
  3.3 1.0 reshape.234
  4.3 11.2 %all-to-all-start = ((bf16[128,2,1024]{2,1,0:T(2,128)(2,1)}), bf16[128,2,1024]{2,1,0:T(2,128)(2,1)S(1)}, u32[]{:S(2)}, u32[]{:S(2)}) async-start(bf16[128,2,1024]{2,1,0:T(2,128)(2,1)} %reshape.234), calls=%async_computation | async-start | bytes 1048576 | tf_op jit(solution)/shard_map/all_to_all | solution.py:372
  15.4 0.0 copy-done.9
  15.5 0.0 copy-done.5
  15.5 0.1 compare_convert_fusion
  15.5 0.1 copy.23
  15.6 0.2 reduce_window_sum.23
  15.8 0.1 copy.24
  15.9 0.0 copy-done.8
  15.9 0.2 select_reduce_fusion
  16.1 0.1 copy.26
  16.2 0.1 reduce_sum.86.rfill_ref
  16.3 0.1 copy.28
  16.4 0.1 add.116
  16.6 0.0 copy-done.13
  16.6 0.1 broadcast_bitcast_fusion
  16.6 0.1 copy.25
  16.8 0.1 copy.31
  16.9 0.1 select_n.85.nrow_ref
  17.0 0.1 reshape_reshape.3.rreq_ref
  17.1 0.1 copy.30
  17.2 0.1 select_n.83.ntag_ref
  17.4 11.8 %all-to-all-done = bf16[128,2,1024]{2,1,0:T(2,128)(2,1)S(1)} async-done(((bf16[128,2,1024]{2,1,0:T(2,128)(2,1)}), bf16[128,2,1024]{2,1,0:T(2,128)(2,1)S(1)}, u32[]{:S(2)}, u32[]{:S(2)}) %all-to-all-start) | async-done | bytes 524320 | tf_op jit(solution)/shard_map/all_to_all | solution.py:372
  29.2 0.2 reshape.235
  29.4 4.6 %convolution_convert_fusion.q_ref.kn_ref.vn_ref = bf16[256,3072]{1,0:T(8,128)(2,1)S(1)} fusion(bf16[256,1024]{1,0:T(8,128)(2,1)S(1)} %reshape.235, bf16[1024,3072]{1,0:T(8,128)(2,1)} %param.20), kind=kOutput, calls=%fused_computation | convolution fusion | flops 1611399168 | bytes 8388608 | tf_op jit(solution)/shard_map/dot_general | solution.py:379
  33.9 19.7 %shard_map.136 = bf16[256,1024]{1,0:T(8,128)(2,1)S(1)} custom-call(bf16[256,3072]{1,0:T(8,128)(2,1)S(1)} %convolution_convert_fusion.q_ref.kn_ref.vn_ref, bf16[256,3072]{1,0:T(8,128)(2,1)S(1)} %convolution_convert_fusion.q_ref.kn_ref.vn_ref, bf16[256,3072]{1,0:T(8,128)(2,1)S(1)} %convolution_convert_fusion.q_ref.kn_ref.vn_ref, bf16[2048,1024]{1,0:T(8,128)(2,1)} %bitcast.21, ...), custom_call_target="tpu_custom_call" | custom-call | tf_op jit(solution)/shard_map/pallas_call | solution.py:98
  53.6 0.0 copy-start.4
  53.7 0.0 copy-start.10
  53.7 0.2 reshape.239
  53.9 0.0 copy-start.6
  53.9 0.0 copy-start.7
  53.9 18.4 %all_to_all.10 = bf16[128,2,1024]{2,1,0:T(2,128)(2,1)} all-to-all(bf16[128,2,1024]{2,1,0:T(2,128)(2,1)S(1)} %reshape.239), channel_id=1, replica_groups=mesh['req'=16,'mlp'=8] {'req','mlp'}, dimensions={0} | all-to-all | bytes 1048576 | tf_op jit(solution)/shard_map/all_to_all | solution.py:386
  72.3 2.1 %reshape.240 = bf16[256,1024]{1,0:T(8,128)(2,1)} reshape(bf16[128,2,1024]{2,1,0:T(2,128)(2,1)} %all_to_all.10) | data formatting | bytes 1048576 | tf_op jit(solution)/shard_map/reshape | solution.py:394
  74.4 0.0 copy-done
  74.4 0.0 copy-done.4
  74.4 0.0 copy-done.10
  74.4 2.5 %fusion.9 = (f32[128]{0:T(128)S(1)}, f32[128,1024]{1,0:T(8,128)}) fusion(bf16[128,1024]{1,0:T(8,128)(2,1)S(1)} %copy-done.4, bf16[1024,1024]{1,0:T(8,128)(2,1)S(1)} %copy-done, bf16[256,1024]{1,0:T(8,128)(2,1)} %reshape.240, s32[128]{0:T(128)S(1)} %copy-done.10), kind=kOutput, calls=%fused_computation.44 | convolution fusion | flops 336101248 | bytes 3408896 | tf_op jit(solution)/shard_map/dot_general | solution.py:396
  76.9 1.2 %multiply_reduce_fusion.1 = f32[128]{0:T(128)S(1)} fusion(f32[128,1024]{1,0:T(8,128)} %get-tuple-element.12, f32[128]{0:T(128)S(1)} %broadcast_multiply_fusion.1), kind=kLoop, calls=%fused_computation.8 | loop fusion | flops 393088 | bytes 525312 | tf_op jit(solution)/shard_map/reduce_sum | solution.py:16
  78.1 0.0 copy-done.6
  78.1 0.0 copy-done.7
  78.2 1.2 %add_convert_fusion.1.x_ref = bf16[128,1024]{1,0:T(8,128)(2,1)S(1)} fusion(f32[128,1024]{1,0:T(8,128)} %get-tuple-element.12, f32[1024]{0:T(1024)S(1)} %copy-done.6, f32[1024]{0:T(1024)S(1)} %copy-done.7, f32[128]{0:T(128)S(1)} %add_rsqrt_fusion.1, f32[128]{0:T(128)S(1)} %broadcast_multiply_fusion.1), kind=kLoop, calls=%fused_computation.7 | loop fusion | flops 655360 | bytes 795648 | tf_op jit(solution)/shard_map/convert_element_type | solution.py:397
  79.4 0.0 copy-done.1
  79.4 0.0 copy-start.2
  79.4 1.2 %copy-done.2 = bf16[512,1024]{1,0:T(8,128)(2,1)S(1)} copy-done((bf16[512,1024]{1,0:T(8,128)(2,1)S(1)}, bf16[512,1024]{1,0:T(8,128)(2,1)}, u32[]{:S(2)}) %copy-start.2) | copy-done | bytes 1048600
  80.6 16.3 %shard_map.137.part_ref = bf16[1024,1024]{1,0:T(8,128)(2,1)S(1)} custom-call(bf16[128,1024]{1,0:T(8,128)(2,1)S(1)} %add_convert_fusion.1.x_ref, bf16[1024,512]{1,0:T(8,128)(2,1)S(1)} %copy-done.1, bf16[512,1024]{1,0:T(8,128)(2,1)S(1)} %copy-done.2), custom_call_target="tpu_custom_call" | custom-call | tf_op jit(solution)/shard_map/pallas_call | solution.py:310
  96.9 0.0 copy-start.11
  97.0 0.0 copy-start.12
  97.0 18.7 %shard_map.138 = f32[128,1024]{1,0:T(8,128)S(1)} custom-call(bf16[1024,1024]{1,0:T(8,128)(2,1)S(1)} %shard_map.137.part_ref), custom_call_target="tpu_custom_call" | custom-call | tf_op jit(solution)/shard_map/pallas_call | solution.py:199
  115.7 0.0 copy-done.3
  115.7 0.3 fusion
  116.0 0.3 multiply_reduce_fusion
  116.3 0.0 copy-done.11
  116.3 0.0 copy-done.12
  116.3 1.0 add_convert_fusion
  (13 shorter events, 0.1 us)
Async XLA Ops:
  0.0 74.4 %copy-start = (bf16[1024,1024]{1,0:T(8,128)(2,1)S(1)}, bf16[1024,1024]{1,0:T(8,128)(2,1)}, u32[]{:S(2)}) copy-start(bf16[1024,1024]{1,0:T(8,128)(2,1)} %param.21) | copy-start | bytes 6291460
  0.0 15.5 %copy-start.5 = (s32[16384,1]{0,1:T(1,128)S(1)}, s32[16384,1]{0,1:T(1,128)}, u32[]{:S(2)}) copy-start(s32[16384,1]{0,1:T(1,128)} %param.15) | copy-start | bytes 196612
  0.0 15.9 %copy-start.8 = (s32[16384]{0:T(1024)S(1)}, s32[16384]{0:T(1024)}, u32[]{:S(2)}) copy-start(s32[16384]{0:T(1024)} %param.16) | copy-start | bytes 196612
  0.0 16.6 %copy-start.13 = (s32[4]{0:T(128)S(1)}, s32[4]{0:T(128)}, u32[]{:S(2)}) copy-start(s32[4]{0:T(128)} %param.17) | copy-start | bytes 52
  1.9 13.5 %copy-start.9 = (s32[128]{0:T(128)}, s32[128]{0:T(128)S(1)}, u32[]{:S(2)}) copy-start(s32[128]{0:T(128)S(1)} %fusion.7) | copy-start | bytes 1540
  4.3 24.9 %all-to-all-start = ((bf16[128,2,1024]{2,1,0:T(2,128)(2,1)}), bf16[128,2,1024]{2,1,0:T(2,128)(2,1)S(1)}, u32[]{:S(2)}, u32[]{:S(2)}) async-start(bf16[128,2,1024]{2,1,0:T(2,128)(2,1)} %reshape.234), calls=%async_computation | async-start | bytes 1048576 | tf_op jit(solution)/shard_map/all_to_all | solution.py:372
  53.6 20.8 %copy-start.4 = (bf16[128,1024]{1,0:T(8,128)(2,1)S(1)}, bf16[128,1024]{1,0:T(8,128)(2,1)}, u32[]{:S(2)}) copy-start(bf16[128,1024]{1,0:T(8,128)(2,1)} %param.14) | copy-start | bytes 786436
  53.7 20.8 %copy-start.10 = (s32[128]{0:T(128)S(1)}, s32[128]{0:T(128)}, u32[]{:S(2)}) copy-start(s32[128]{0:T(128)} %copy-done.9) | copy-start | bytes 1540
  53.9 24.3 %copy-start.6 = (f32[1024]{0:T(1024)S(1)}, f32[1024]{0:T(1024)}, u32[]{:S(2)}) copy-start(f32[1024]{0:T(1024)} %param.25) | copy-start | bytes 12292
  53.9 24.3 %copy-start.7 = (f32[1024]{0:T(1024)S(1)}, f32[1024]{0:T(1024)}, u32[]{:S(2)}) copy-start(f32[1024]{0:T(1024)} %param.24) | copy-start | bytes 12292
  72.3 7.1 %copy-start.1 = (bf16[1024,512]{1,0:T(8,128)(2,1)S(1)}, bf16[1024,512]{1,0:T(8,128)(2,1)}, u32[]{:S(2)}) copy-start(bf16[1024,512]{1,0:T(8,128)(2,1)} %w1_hbm.1) | copy-start | bytes 3145732
  79.4 1.2 %copy-start.2 = (bf16[512,1024]{1,0:T(8,128)(2,1)S(1)}, bf16[512,1024]{1,0:T(8,128)(2,1)}, u32[]{:S(2)}) copy-start(bf16[512,1024]{1,0:T(8,128)(2,1)} %w2_hbm.1) | copy-start | bytes 3145732
  80.6 35.1 %copy-start.3 = (f32[128,1024]{1,0:T(8,128)S(1)}, f32[128,1024]{1,0:T(8,128)}, u32[]{:S(2)}) copy-start(f32[128,1024]{1,0:T(8,128)} %get-tuple-element.12) | copy-start | bytes 1572868
  96.9 19.3 %copy-start.11 = (f32[1024]{0:T(1024)S(1)}, f32[1024]{0:T(1024)}, u32[]{:S(2)}) copy-start(f32[1024]{0:T(1024)} %param.27) | copy-start | bytes 12292
  97.0 19.3 %copy-start.12 = (f32[1024]{0:T(1024)S(1)}, f32[1024]{0:T(1024)}, u32[]{:S(2)}) copy-start(f32[1024]{0:T(1024)} %param.26) | copy-start | bytes 12292

commit v13 on v10

--- a/solution.py
+++ b/solution.py
@@ -40,7 +40,7 @@
 ):
     head_dim = q_ref.shape[1] // 2
     score_scale = head_dim ** (-0.5)
-    q = q_ref[...]
+    q = q_ref[...] * jnp.asarray(score_scale, q_ref.dtype)
     keys = k_ref[...]
     values = v_ref[...]
     key_new = kn_ref[...]
@@ -54,13 +54,8 @@
     for half in range(2):
         in_head = (lane // head_dim) == half
         q_head = jnp.where(in_head, q, jnp.zeros_like(q))
-        old_score = (
-            lax.dot_general(q_head, keys, contract, preferred_element_type=jnp.float32) * score_scale
-        )
-        new_score = (
-            lax.dot_general(q_head, key_new, contract, preferred_element_type=jnp.float32)
-            * score_scale
-        )
+        old_score = lax.dot_general(q_head, keys, contract, preferred_element_type=jnp.float32)
+        new_score = lax.dot_general(q_head, key_new, contract, preferred_element_type=jnp.float32)
         old_exp = jnp.where(old_mask, jnp.exp(old_score), jnp.float32(0.0))
         new_exp = jnp.where(new_mask, jnp.exp(new_score), jnp.float32(0.0))
         total = jnp.sum(old_exp, axis=1, keepdims=True) + jnp.sum(new_exp, axis=1, keepdims=True)

time: 117 us -> 117 us (level)
  no operation moved by 1% of the time
where the time goes in v13:
time: 117 us; the launch traced here: 116 us
  Pallas kernels  53.7 us (46%)
  blocking collectives  18.4 us (16%)
  waiting for transfers between devices  11.8 us (10%)
  starting transfers between devices  11.2 us (10%)
  matrix products  8.39 us (7%)
  local copies, waits for them, and re-layouts  6.95 us (6%)
  other arithmetic  5.53 us (5%)
    pallas_call x1, Pallas kernels, attend(): pl.pallas_call(attention_kernel, grid=(pairs,), in_specs=[pl.BlockSpec((s...  19 us
    pallas_call x1, Pallas kernels, scatter_sum(): pl.pallas_call(scatter_kernel, in_specs=[pl.BlockSpec(memory_space=pltpu....  18.7 us
    all_to_all x1, blocking collectives, per_device(): lax.all_to_all(attended.reshape(devices, capacity, width), ('req', 'mlp')...  18.4 us
    pallas_call x1, Pallas kernels, gather_rows(): pl.pallas_call(gather_kernel, in_specs=[pl.BlockSpec(memory_space=pltpu.V...  16 us
    all_to_all x1, waiting for transfers between devices, per_device(): lax.all_to_all(outgoing.reshape(devices, capacity, width), ('req', 'mlp')...  11.8 us
    all_to_all x1, starting transfers between devices, per_device(): lax.all_to_all(outgoing.reshape(devices, capacity, width), ('req', 'mlp')...  11.2 us
    dot_general x1, matrix products, per_device(): jnp.dot(arrived.reshape(slot_count, width), w_qkv, preferred_element_type...  4.58 us
    dot_general x1, matrix products, per_device(): jnp.dot(attn_rows, w_out, preferred_element_type=jnp.float32)  2.46 us
  transfers between devices with their start and end apart: 1, of which 1 were waited for; matrix products, arithmetic and copies ran while one was open for 2% of the time, Pallas kernels for 0%

profile of v13, /device:TPU:0, one launch (start us, length us, event | category | flops | bytes accessed | tf_op | source)
XLA Modules:
  0.0 116.3 jit_solution(8997349803570526795)
XLA Ops:
  0.0 0.0 copy-start
  0.0 0.0 copy-start.5
  0.0 0.0 copy-start.8
  0.0 0.0 copy-start.13
  0.0 0.8 fusion.8
  0.8 0.1 fusion.6
  0.9 0.2 reduce_window_sum.22
  1.1 0.2 select_reduce_fusion.1
  1.3 0.7 fusion.7
  1.9 1.3 %convolution_convert_fusion.1 = bf16[256,1024]{1,0:T(8,128)(2,1)S(1)} fusion(bf16[128,1024]{1,0:T(8,128)(2,1)} %param.14, s32[128]{0:T(128)S(1)} %fusion.7), kind=kOutput, calls=%fused_computation.1 | convolution fusion | flops 67403776 | bytes 786944 | tf_op jit(solution)/shard_map/tr,td->rd/dot_general | solution.py:351
  3.3 1.0 reshape.234
  4.3 11.2 %all-to-all-start = ((bf16[128,2,1024]{2,1,0:T(2,128)(2,1)}), bf16[128,2,1024]{2,1,0:T(2,128)(2,1)S(1)}, u32[]{:S(2)}, u32[]{:S(2)}) async-start(bf16[128,2,1024]{2,1,0:T(2,128)(2,1)} %reshape.234), calls=%async_computation | async-start | bytes 1048576 | tf_op jit(solution)/shard_map/all_to_all | solution.py:354
  15.4 0.0 copy-done.9
  15.5 0.0 copy-done.5
  15.5 0.1 compare_convert_fusion
  15.5 0.1 copy.23
  15.6 0.2 reduce_window_sum.23
  15.8 0.1 copy.24
  15.9 0.0 copy-done.8
  15.9 0.2 select_reduce_fusion
  16.1 0.1 copy.26
  16.2 0.1 reduce_sum.86.rfill_ref
  16.3 0.1 copy.28
  16.4 0.1 add.116
  16.6 0.0 copy-done.13
  16.6 0.1 broadcast_bitcast_fusion
  16.6 0.1 copy.25
  16.8 0.1 copy.31
  16.9 0.1 select_n.85.nrow_ref
  17.0 0.1 reshape_reshape.3.rreq_ref
  17.1 0.1 copy.30
  17.2 0.1 select_n.83.ntag_ref
  17.4 11.8 %all-to-all-done = bf16[128,2,1024]{2,1,0:T(2,128)(2,1)S(1)} async-done(((bf16[128,2,1024]{2,1,0:T(2,128)(2,1)}), bf16[128,2,1024]{2,1,0:T(2,128)(2,1)S(1)}, u32[]{:S(2)}, u32[]{:S(2)}) %all-to-all-start) | async-done | bytes 524320 | tf_op jit(solution)/shard_map/all_to_all | solution.py:354
  29.2 0.2 reshape.235
  29.4 4.6 %convolution_convert_fusion.q_ref.kn_ref.vn_ref = bf16[256,3072]{1,0:T(8,128)(2,1)S(1)} fusion(bf16[256,1024]{1,0:T(8,128)(2,1)S(1)} %reshape.235, bf16[1024,3072]{1,0:T(8,128)(2,1)} %param.20), kind=kOutput, calls=%fused_computation | convolution fusion | flops 1611399168 | bytes 8388608 | tf_op jit(solution)/shard_map/dot_general | solution.py:361
  33.9 19.0 %shard_map.136 = bf16[256,1024]{1,0:T(8,128)(2,1)S(1)} custom-call(bf16[256,3072]{1,0:T(8,128)(2,1)S(1)} %convolution_convert_fusion.q_ref.kn_ref.vn_ref, bf16[256,3072]{1,0:T(8,128)(2,1)S(1)} %convolution_convert_fusion.q_ref.kn_ref.vn_ref, bf16[256,3072]{1,0:T(8,128)(2,1)S(1)} %convolution_convert_fusion.q_ref.kn_ref.vn_ref, bf16[2048,1024]{1,0:T(8,128)(2,1)} %bitcast.21, ...), custom_call_target="tpu_custom_call" | custom-call | tf_op jit(solution)/shard_map/pallas_call | solution.py:93
  52.9 0.0 copy-start.4
  52.9 0.0 copy-start.10
  53.0 0.2 reshape.239
  53.2 0.0 copy-start.6
  53.2 0.0 copy-start.7
  53.2 18.4 %all_to_all.10 = bf16[128,2,1024]{2,1,0:T(2,128)(2,1)} all-to-all(bf16[128,2,1024]{2,1,0:T(2,128)(2,1)S(1)} %reshape.239), channel_id=1, replica_groups=mesh['req'=16,'mlp'=8] {'req','mlp'}, dimensions={0} | all-to-all | bytes 1048576 | tf_op jit(solution)/shard_map/all_to_all | solution.py:368
  71.6 2.1 %reshape.240 = bf16[256,1024]{1,0:T(8,128)(2,1)} reshape(bf16[128,2,1024]{2,1,0:T(2,128)(2,1)} %all_to_all.10) | data formatting | bytes 1048576 | tf_op jit(solution)/shard_map/reshape | solution.py:376
  73.7 0.0 copy-done
  73.7 0.0 copy-done.4
  73.7 0.0 copy-done.10
  73.7 2.5 %fusion.9 = (f32[128]{0:T(128)S(1)}, f32[128,1024]{1,0:T(8,128)}) fusion(bf16[128,1024]{1,0:T(8,128)(2,1)S(1)} %copy-done.4, bf16[1024,1024]{1,0:T(8,128)(2,1)S(1)} %copy-done, bf16[256,1024]{1,0:T(8,128)(2,1)} %reshape.240, s32[128]{0:T(128)S(1)} %copy-done.10), kind=kOutput, calls=%fused_computation.44 | convolution fusion | flops 336101248 | bytes 3408896 | tf_op jit(solution)/shard_map/dot_general | solution.py:378
  76.2 1.2 %multiply_reduce_fusion.1 = f32[128]{0:T(128)S(1)} fusion(f32[128,1024]{1,0:T(8,128)} %get-tuple-element.12, f32[128]{0:T(128)S(1)} %broadcast_multiply_fusion.1), kind=kLoop, calls=%fused_computation.8 | loop fusion | flops 393088 | bytes 525312 | tf_op jit(solution)/shard_map/reduce_sum | solution.py:16
  77.4 0.0 copy-done.6
  77.4 0.0 copy-done.7
  77.4 1.2 %add_convert_fusion.1.x_ref = bf16[128,1024]{1,0:T(8,128)(2,1)S(1)} fusion(f32[128,1024]{1,0:T(8,128)} %get-tuple-element.12, f32[1024]{0:T(1024)S(1)} %copy-done.6, f32[1024]{0:T(1024)S(1)} %copy-done.7, f32[128]{0:T(128)S(1)} %add_rsqrt_fusion.1, f32[128]{0:T(128)S(1)} %broadcast_multiply_fusion.1), kind=kLoop, calls=%fused_computation.7 | loop fusion | flops 655360 | bytes 795648 | tf_op jit(solution)/shard_map/convert_element_type | solution.py:379
  78.6 0.0 copy-done.1
  78.7 0.0 copy-start.2
  78.7 1.2 %copy-done.2 = bf16[512,1024]{1,0:T(8,128)(2,1)S(1)} copy-done((bf16[512,1024]{1,0:T(8,128)(2,1)S(1)}, bf16[512,1024]{1,0:T(8,128)(2,1)}, u32[]{:S(2)}) %copy-start.2) | copy-done | bytes 1048600
  79.9 16.0 %shard_map.137.part_ref = bf16[1024,1024]{1,0:T(8,128)(2,1)S(1)} custom-call(bf16[128,1024]{1,0:T(8,128)(2,1)S(1)} %add_convert_fusion.1.x_ref, bf16[1024,512]{1,0:T(8,128)(2,1)S(1)} %copy-done.1, bf16[512,1024]{1,0:T(8,128)(2,1)S(1)} %copy-done.2), custom_call_target="tpu_custom_call" | custom-call | tf_op jit(solution)/shard_map/pallas_call | solution.py:299
  95.9 0.0 copy-start.11
  95.9 0.0 copy-start.12
  95.9 18.7 %shard_map.138 = f32[128,1024]{1,0:T(8,128)S(1)} custom-call(bf16[1024,1024]{1,0:T(8,128)(2,1)S(1)} %shard_map.137.part_ref), custom_call_target="tpu_custom_call" | custom-call | tf_op jit(solution)/shard_map/pallas_call | solution.py:194
  114.7 0.0 copy-done.3
  114.7 0.3 fusion
  115.0 0.3 multiply_reduce_fusion
  115.3 0.0 copy-done.11
  115.3 0.0 copy-done.12
  115.3 1.0 add_convert_fusion
  (13 shorter events, 0.1 us)
Async XLA Ops:
  0.0 73.7 %copy-start = (bf16[1024,1024]{1,0:T(8,128)(2,1)S(1)}, bf16[1024,1024]{1,0:T(8,128)(2,1)}, u32[]{:S(2)}) copy-start(bf16[1024,1024]{1,0:T(8,128)(2,1)} %param.21) | copy-start | bytes 6291460
  0.0 15.5 %copy-start.5 = (s32[16384,1]{0,1:T(1,128)S(1)}, s32[16384,1]{0,1:T(1,128)}, u32[]{:S(2)}) copy-start(s32[16384,1]{0,1:T(1,128)} %param.15) | copy-start | bytes 196612
  0.0 15.9 %copy-start.8 = (s32[16384]{0:T(1024)S(1)}, s32[16384]{0:T(1024)}, u32[]{:S(2)}) copy-start(s32[16384]{0:T(1024)} %param.16) | copy-start | bytes 196612
  0.0 16.6 %copy-start.13 = (s32[4]{0:T(128)S(1)}, s32[4]{0:T(128)}, u32[]{:S(2)}) copy-start(s32[4]{0:T(128)} %param.17) | copy-start | bytes 52
  1.9 13.5 %copy-start.9 = (s32[128]{0:T(128)}, s32[128]{0:T(128)S(1)}, u32[]{:S(2)}) copy-start(s32[128]{0:T(128)S(1)} %fusion.7) | copy-start | bytes 1540
  4.3 24.9 %all-to-all-start = ((bf16[128,2,1024]{2,1,0:T(2,128)(2,1)}), bf16[128,2,1024]{2,1,0:T(2,128)(2,1)S(1)}, u32[]{:S(2)}, u32[]{:S(2)}) async-start(bf16[128,2,1024]{2,1,0:T(2,128)(2,1)} %reshape.234), calls=%async_computation | async-start | bytes 1048576 | tf_op jit(solution)/shard_map/all_to_all | solution.py:354
  52.9 20.8 %copy-start.4 = (bf16[128,1024]{1,0:T(8,128)(2,1)S(1)}, bf16[128,1024]{1,0:T(8,128)(2,1)}, u32[]{:S(2)}) copy-start(bf16[128,1024]{1,0:T(8,128)(2,1)} %param.14) | copy-start | bytes 786436
  52.9 20.8 %copy-start.10 = (s32[128]{0:T(128)S(1)}, s32[128]{0:T(128)}, u32[]{:S(2)}) copy-start(s32[128]{0:T(128)} %copy-done.9) | copy-start | bytes 1540
  53.2 24.3 %copy-start.6 = (f32[1024]{0:T(1024)S(1)}, f32[1024]{0:T(1024)}, u32[]{:S(2)}) copy-start(f32[1024]{0:T(1024)} %param.25) | copy-start | bytes 12292
  53.2 24.3 %copy-start.7 = (f32[1024]{0:T(1024)S(1)}, f32[1024]{0:T(1024)}, u32[]{:S(2)}) copy-start(f32[1024]{0:T(1024)} %param.24) | copy-start | bytes 12292
  71.6 7.1 %copy-start.1 = (bf16[1024,512]{1,0:T(8,128)(2,1)S(1)}, bf16[1024,512]{1,0:T(8,128)(2,1)}, u32[]{:S(2)}) copy-start(bf16[1024,512]{1,0:T(8,128)(2,1)} %w1_ref.1) | copy-start | bytes 3145732
  78.7 1.2 %copy-start.2 = (bf16[512,1024]{1,0:T(8,128)(2,1)S(1)}, bf16[512,1024]{1,0:T(8,128)(2,1)}, u32[]{:S(2)}) copy-start(bf16[512,1024]{1,0:T(8,128)(2,1)} %w2_ref.1) | copy-start | bytes 3145732
  79.9 34.8 %copy-start.3 = (f32[128,1024]{1,0:T(8,128)S(1)}, f32[128,1024]{1,0:T(8,128)}, u32[]{:S(2)}) copy-start(f32[128,1024]{1,0:T(8,128)} %get-tuple-element.12) | copy-start | bytes 1572868
  95.9 19.4 %copy-start.11 = (f32[1024]{0:T(1024)S(1)}, f32[1024]{0:T(1024)}, u32[]{:S(2)}) copy-start(f32[1024]{0:T(1024)} %param.27) | copy-start | bytes 12292
  95.9 19.4 %copy-start.12 = (f32[1024]{0:T(1024)S(1)}, f32[1024]{0:T(1024)}, u32[]{:S(2)}) copy-start(f32[1024]{0:T(1024)} %param.26) | copy-start | bytes 12292

commit v14 on v13

--- a/solution.py
+++ b/solution.py
@@ -124,95 +124,9 @@
     )
 
 
-def scatter_kernel(part_ref, o_ref, pair_buf, send_buf, ring_buf, pair_send, pair_recv, ring_send, ring_recv):
-    req = lax.axis_index("req")
-    me = lax.axis_index("mlp")
-    chips = lax.axis_size("mlp") // 2
-    chip, core = me // 2, lax.rem(me, 2)
-    partner = chip * 2 + 1 - core
-    step = 1 - 2 * core
-    ahead = lax.rem(chip + step + chips, chips)
-    behind = lax.rem(chip - step + chips, chips)
-    across = lax.rem(chip + 2, chips)
-    rows = o_ref.shape[0]
-    barrier = pltpu.get_barrier_semaphore()
-    pl.semaphore_signal(barrier, 1, device_id=(req, partner), device_id_type=pl.DeviceIdType.MESH)
-    pl.semaphore_signal(barrier, 1, device_id=(req, ahead * 2 + core), device_id_type=pl.DeviceIdType.MESH)
-    pl.semaphore_signal(barrier, 1, device_id=(req, behind * 2 + core), device_id_type=pl.DeviceIdType.MESH)
-    pl.semaphore_wait(barrier, 3)
-
-    def pair_copy(z):
-        block = z * 2 + 1 - core
-        return pltpu.make_async_remote_copy(
-            src_ref=part_ref.at[pl.ds(pl.multiple_of(block * rows, rows), rows)],
-            dst_ref=pair_buf.at[z],
-            send_sem=pair_send.at[z],
-            recv_sem=pair_recv.at[z],
-            device_id=(req, partner),
-            device_id_type=pl.DeviceIdType.MESH,
-        )
-
-    for z in range(chips):
-        pair_copy(z).start()
-    for z in range(chips):
-        pair_copy(z).wait()
-
-    def summed(z):
-        mine = part_ref[pl.ds(pl.multiple_of((z * 2 + core) * rows, rows), rows), :]
-        return mine.astype(jnp.float32) + pair_buf[z].astype(jnp.float32)
-
-    def ring_copy(kind, target):
-        return pltpu.make_async_remote_copy(
-            src_ref=send_buf.at[kind],
-            dst_ref=ring_buf.at[kind],
-            send_sem=ring_send.at[kind],
-            recv_sem=ring_recv.at[kind],
-            device_id=(req, target * 2 + core),
-            device_id_type=pl.DeviceIdType.MESH,
-        )
-
-    send_buf[1] = summed(across).astype(send_buf.dtype)
-    ring_copy(1, ahead).start()
-    send_buf[0] = summed(behind).astype(send_buf.dtype)
-    ring_copy(0, behind).start()
-    ring_copy(1, ahead).wait_recv()
-    send_buf[2] = (summed(ahead) + ring_buf[1].astype(jnp.float32)).astype(send_buf.dtype)
-    ring_copy(2, ahead).start()
-    total = summed(chip)
-    ring_copy(0, behind).wait()
-    total = total + ring_buf[0].astype(jnp.float32)
-    ring_copy(1, ahead).wait_send()
-    ring_copy(2, ahead).wait()
-    o_ref[...] = total + ring_buf[2].astype(jnp.float32)
-
-
-def scatter_sum(partial):
-    groups = lax.axis_size("mlp")
-    chips = groups // 2
-    rows = partial.shape[0] // groups
-    width = partial.shape[1]
-    return pl.pallas_call(
-        scatter_kernel,
-        in_specs=[pl.BlockSpec(memory_space=pltpu.VMEM)],
-        out_specs=pl.BlockSpec(memory_space=pltpu.VMEM),
-        out_shape=jax.ShapeDtypeStruct((rows, width), jnp.float32),
-        scratch_shapes=[
-            pltpu.VMEM((chips, rows, width), partial.dtype),
-            pltpu.VMEM((3, rows, width), partial.dtype),
-            pltpu.VMEM((3, rows, width), partial.dtype),
-            pltpu.SemaphoreType.DMA((chips,)),
-            pltpu.SemaphoreType.DMA((chips,)),
-            pltpu.SemaphoreType.DMA((3,)),
-            pltpu.SemaphoreType.DMA((3,)),
-        ],
-        compiler_params=pltpu.CompilerParams(
-            collective_id=1, has_side_effects=True, vmem_limit_bytes=48 * 1024 * 1024
-        ),
-    )(partial)
-
-
-def gather_kernel(
-    x_ref, w1_ref, w2_ref, o_ref, held, ring_send, ring_recv, pair_send, pair_recv
+def block_kernel(
+    x_ref, w1_ref, w2_ref, o_ref, held, parts, pair_buf, send_buf, ring_buf,
+    ring_send, ring_recv, pair_send, pair_recv, back_send, back_recv, sum_send, sum_recv,
 ):
     req = lax.axis_index("req")
     me = lax.axis_index("mlp")
@@ -259,11 +173,21 @@
             device_id_type=pl.DeviceIdType.MESH,
         )
 
+    def back_copy(z):
+        return pltpu.make_async_remote_copy(
+            src_ref=parts.at[block_rows(z, 1 - core)],
+            dst_ref=pair_buf.at[z],
+            send_sem=back_send.at[z],
+            recv_sem=back_recv.at[z],
+            device_id=(req, partner),
+            device_id_type=pl.DeviceIdType.MESH,
+        )
+
     def feed_forward(block, place):
         hidden = jnp.dot(block, w1_ref[...], preferred_element_type=jnp.float32)
         hidden = (hidden * 0.5 * (1.0 + lax.erf(hidden * (2.0 ** -0.5)))).astype(jnp.bfloat16)
-        o_ref[place, :] = jnp.dot(hidden, w2_ref[...], preferred_element_type=jnp.float32).astype(
-            o_ref.dtype
+        parts[place, :] = jnp.dot(hidden, w2_ref[...], preferred_element_type=jnp.float32).astype(
+            parts.dtype
         )
 
     ring_copy(0).start()
@@ -282,31 +206,71 @@
     feed_forward(held[block_rows(across, core), :], block_rows(across, core))
     partner_origins = (chip, ahead, behind, across)
     for kind in range(4):
-        copy = pair_copy(kind)
-        copy.wait_recv()
+        pair_copy(kind).wait_recv()
         place = block_rows(partner_origins[kind], 1 - core)
         feed_forward(held[place, :], place)
+        back_copy(partner_origins[kind]).start()
     for kind in range(3):
         ring_copy(kind).wait_send()
     for kind in range(4):
         pair_copy(kind).wait_send()
-
-
-def gather_rows(block, w_fc1, w_fc2):
+    for z in range(chips):
+        back_copy(z).wait()
+
+    def summed(z):
+        mine = parts[block_rows(z, core), :]
+        return mine.astype(jnp.float32) + pair_buf[z].astype(jnp.float32)
+
+    def sum_copy(kind, target):
+        return pltpu.make_async_remote_copy(
+            src_ref=send_buf.at[kind],
+            dst_ref=ring_buf.at[kind],
+            send_sem=sum_send.at[kind],
+            recv_sem=sum_recv.at[kind],
+            device_id=(req, target * 2 + core),
+            device_id_type=pl.DeviceIdType.MESH,
+        )
+
+    send_buf[1] = summed(across).astype(send_buf.dtype)
+    sum_copy(1, ahead).start()
+    send_buf[0] = summed(behind).astype(send_buf.dtype)
+    sum_copy(0, behind).start()
+    sum_copy(1, ahead).wait_recv()
+    send_buf[2] = (summed(ahead) + ring_buf[1].astype(jnp.float32)).astype(send_buf.dtype)
+    sum_copy(2, ahead).start()
+    total = summed(chip)
+    sum_copy(0, behind).wait()
+    total = total + ring_buf[0].astype(jnp.float32)
+    sum_copy(1, ahead).wait_send()
+    sum_copy(2, ahead).wait()
+    o_ref[...] = total + ring_buf[2].astype(jnp.float32)
+
+
+def feed_forward_block(block, w_fc1, w_fc2):
     groups = lax.axis_size("mlp")
     chips = groups // 2
-    total = groups * block.shape[0]
+    rows, width = block.shape
+    total = groups * rows
+    out_width = w_fc2.shape[1]
     return pl.pallas_call(
-        gather_kernel,
+        block_kernel,
         in_specs=[pl.BlockSpec(memory_space=pltpu.VMEM)] * 3,
         out_specs=pl.BlockSpec(memory_space=pltpu.VMEM),
-        out_shape=jax.ShapeDtypeStruct((total, w_fc2.shape[1]), jnp.bfloat16),
+        out_shape=jax.ShapeDtypeStruct((rows, out_width), jnp.float32),
         scratch_shapes=[
-            pltpu.VMEM((total, block.shape[1]), block.dtype),
+            pltpu.VMEM((total, width), block.dtype),
+            pltpu.VMEM((total, out_width), jnp.bfloat16),
+            pltpu.VMEM((chips, rows, out_width), jnp.bfloat16),
+            pltpu.VMEM((3, rows, out_width), jnp.bfloat16),
+            pltpu.VMEM((3, rows, out_width), jnp.bfloat16),
+            pltpu.SemaphoreType.DMA((3,)),
+            pltpu.SemaphoreType.DMA((3,)),
             pltpu.SemaphoreType.DMA((chips,)),
             pltpu.SemaphoreType.DMA((chips,)),
             pltpu.SemaphoreType.DMA((chips,)),
             pltpu.SemaphoreType.DMA((chips,)),
+            pltpu.SemaphoreType.DMA((3,)),
+            pltpu.SemaphoreType.DMA((3,)),
         ],
         compiler_params=pltpu.CompilerParams(
             collective_id=2, has_side_effects=True, vmem_limit_bytes=48 * 1024 * 1024
@@ -379,7 +343,7 @@
     normed = layer_norm(projected_out + tokens.astype(jnp.float32), ln1_gain, ln1_bias).astype(
         jnp.bfloat16
     )
-    summed = scatter_sum(gather_rows(normed, w_fc1, w_fc2))
+    summed = feed_forward_block(normed, w_fc1, w_fc2)
     return layer_norm(normed.astype(jnp.float32) + summed, ln2_gain, ln2_bias).astype(jnp.bfloat16)
 
 

time: 117 us -> 114 us (0.974)
  Pallas kernels: 53.7 us -> 50.7 us
    pallas_call x2 -> x1, Pallas kernels: 34.8 us -> 31.8 us  [feed_forward_block(): pl.pallas_call(block_kernel, in_specs=[pl.BlockSpec(memory_space=pltpu.VM...]
where the time goes in v14:
time: 114 us; the launch traced here: 113 us
  Pallas kernels  50.7 us (44%)
  blocking collectives  18.4 us (16%)
  waiting for transfers between devices  11.8 us (10%)
  starting transfers between devices  11.2 us (10%)
  matrix products  8.39 us (7%)
  local copies, waits for them, and re-layouts  6.94 us (6%)
  other arithmetic  5.59 us (5%)
    pallas_call x1, Pallas kernels, feed_forward_block(): pl.pallas_call(block_kernel, in_specs=[pl.BlockSpec(memory_space=pltpu.VM...  31.8 us
    pallas_call x1, Pallas kernels, attend(): pl.pallas_call(attention_kernel, grid=(pairs,), in_specs=[pl.BlockSpec((s...  19 us
    all_to_all x1, blocking collectives, per_device(): lax.all_to_all(attended.reshape(devices, capacity, width), ('req', 'mlp')...  18.4 us
    all_to_all x1, waiting for transfers between devices, per_device(): lax.all_to_all(outgoing.reshape(devices, capacity, width), ('req', 'mlp')...  11.8 us
    all_to_all x1, starting transfers between devices, per_device(): lax.all_to_all(outgoing.reshape(devices, capacity, width), ('req', 'mlp')...  11.2 us
    dot_general x1, matrix products, per_device(): jnp.dot(arrived.reshape(slot_count, width), w_qkv, preferred_element_type...  4.58 us
    dot_general x1, matrix products, per_device(): jnp.dot(attn_rows, w_out, preferred_element_type=jnp.float32)  2.46 us
  transfers between devices with their start and end apart: 1, of which 1 were waited for; matrix products, arithmetic and copies ran while one was open for 2% of the time, Pallas kernels for 0%

profile of v14, /device:TPU:0, one launch (start us, length us, event | category | flops | bytes accessed | tf_op | source)
XLA Modules:
  0.0 113.3 jit_solution(4147242828222425291)
XLA Ops:
  0.0 0.0 copy-start
  0.0 0.0 copy-start.5
  0.0 0.0 copy-start.8
  0.0 0.0 copy-start.13
  0.0 0.8 fusion.8
  0.8 0.1 fusion.6
  0.9 0.2 reduce_window_sum.22
  1.1 0.2 select_reduce_fusion.1
  1.3 0.7 fusion.7
  1.9 0.0 copy-start.9
  1.9 1.3 %convolution_convert_fusion.1 = bf16[256,1024]{1,0:T(8,128)(2,1)S(1)} fusion(bf16[128,1024]{1,0:T(8,128)(2,1)} %param.14, s32[128]{0:T(128)S(1)} %fusion.7), kind=kOutput, calls=%fused_computation.1 | convolution fusion | flops 67403776 | bytes 786944 | tf_op jit(solution)/shard_map/tr,td->rd/dot_general | solution.py:315
  3.3 1.0 reshape.234
  4.3 11.2 %all-to-all-start = ((bf16[128,2,1024]{2,1,0:T(2,128)(2,1)}), bf16[128,2,1024]{2,1,0:T(2,128)(2,1)S(1)}, u32[]{:S(2)}, u32[]{:S(2)}) async-start(bf16[128,2,1024]{2,1,0:T(2,128)(2,1)} %reshape.234), calls=%async_computation | async-start | bytes 1048576 | tf_op jit(solution)/shard_map/all_to_all | solution.py:318
  15.4 0.0 copy-done.9
  15.5 0.0 copy-done.5
  15.5 0.1 compare_convert_fusion
  15.5 0.1 copy.23
  15.6 0.2 reduce_window_sum.23
  15.8 0.1 copy.24
  15.9 0.0 copy-done.8
  15.9 0.2 select_reduce_fusion
  16.1 0.1 copy.26
  16.2 0.1 reduce_sum.86.rfill_ref
  16.3 0.1 copy.28
  16.4 0.1 add.116
  16.6 0.0 copy-done.13
  16.6 0.1 broadcast_bitcast_fusion
  16.6 0.1 copy.25
  16.8 0.1 copy.31
  16.9 0.1 select_n.85.nrow_ref
  17.0 0.1 reshape_reshape.3.rreq_ref
  17.1 0.1 copy.30
  17.2 0.1 select_n.83.ntag_ref
  17.4 11.8 %all-to-all-done = bf16[128,2,1024]{2,1,0:T(2,128)(2,1)S(1)} async-done(((bf16[128,2,1024]{2,1,0:T(2,128)(2,1)}), bf16[128,2,1024]{2,1,0:T(2,128)(2,1)S(1)}, u32[]{:S(2)}, u32[]{:S(2)}) %all-to-all-start) | async-done | bytes 524320 | tf_op jit(solution)/shard_map/all_to_all | solution.py:318
  29.2 0.2 reshape.235
  29.4 4.6 %convolution_convert_fusion.q_ref.kn_ref.vn_ref = bf16[256,3072]{1,0:T(8,128)(2,1)S(1)} fusion(bf16[256,1024]{1,0:T(8,128)(2,1)S(1)} %reshape.235, bf16[1024,3072]{1,0:T(8,128)(2,1)} %param.20), kind=kOutput, calls=%fused_computation | convolution fusion | flops 1611399168 | bytes 8388608 | tf_op jit(solution)/shard_map/dot_general | solution.py:325
  33.9 19.0 %shard_map.136 = bf16[256,1024]{1,0:T(8,128)(2,1)S(1)} custom-call(bf16[256,3072]{1,0:T(8,128)(2,1)S(1)} %convolution_convert_fusion.q_ref.kn_ref.vn_ref, bf16[256,3072]{1,0:T(8,128)(2,1)S(1)} %convolution_convert_fusion.q_ref.kn_ref.vn_ref, bf16[256,3072]{1,0:T(8,128)(2,1)S(1)} %convolution_convert_fusion.q_ref.kn_ref.vn_ref, bf16[2048,1024]{1,0:T(8,128)(2,1)} %bitcast.21, ...), custom_call_target="tpu_custom_call" | custom-call | tf_op jit(solution)/shard_map/pallas_call | solution.py:93
  52.9 0.0 copy-start.4
  52.9 0.0 copy-start.10
  53.0 0.2 reshape.239
  53.2 0.0 copy-start.6
  53.2 0.0 copy-start.7
  53.2 18.4 %all_to_all.10 = bf16[128,2,1024]{2,1,0:T(2,128)(2,1)} all-to-all(bf16[128,2,1024]{2,1,0:T(2,128)(2,1)S(1)} %reshape.239), channel_id=1, replica_groups=mesh['req'=16,'mlp'=8] {'req','mlp'}, dimensions={0} | all-to-all | bytes 1048576 | tf_op jit(solution)/shard_map/all_to_all | solution.py:332
  71.6 0.0 copy-start.1
  71.6 2.1 %reshape.240 = bf16[256,1024]{1,0:T(8,128)(2,1)} reshape(bf16[128,2,1024]{2,1,0:T(2,128)(2,1)} %all_to_all.10) | data formatting | bytes 1048576 | tf_op jit(solution)/shard_map/reshape | solution.py:340
  73.7 0.0 copy-done
  73.7 0.0 copy-done.4
  73.7 0.0 copy-done.10
  73.7 2.5 %fusion.9 = (f32[128]{0:T(128)S(1)}, f32[128,1024]{1,0:T(8,128)}) fusion(bf16[128,1024]{1,0:T(8,128)(2,1)S(1)} %copy-done.4, bf16[1024,1024]{1,0:T(8,128)(2,1)S(1)} %copy-done, bf16[256,1024]{1,0:T(8,128)(2,1)} %reshape.240, s32[128]{0:T(128)S(1)} %copy-done.10), kind=kOutput, calls=%fused_computation.44 | convolution fusion | flops 336101248 | bytes 3408896 | tf_op jit(solution)/shard_map/dot_general | solution.py:342
  76.2 0.0 copy-start.12
  76.2 1.3 %multiply_reduce_fusion.1 = f32[128]{0:T(128)S(1)} fusion(f32[128,1024]{1,0:T(8,128)} %get-tuple-element.12, f32[128]{0:T(128)S(1)} %broadcast_multiply_fusion.1), kind=kLoop, calls=%fused_computation.8 | loop fusion | flops 393088 | bytes 525312 | tf_op jit(solution)/shard_map/reduce_sum | solution.py:16
  77.5 0.0 copy-done.6
  77.5 0.0 copy-done.7
  77.5 1.2 %add_convert_fusion.1.x_ref = bf16[128,1024]{1,0:T(8,128)(2,1)S(1)} fusion(f32[128,1024]{1,0:T(8,128)} %get-tuple-element.12, f32[1024]{0:T(1024)S(1)} %copy-done.6, f32[1024]{0:T(1024)S(1)} %copy-done.7, f32[128]{0:T(128)S(1)} %add_rsqrt_fusion.1, f32[128]{0:T(128)S(1)} %broadcast_multiply_fusion.1), kind=kLoop, calls=%fused_computation.7 | loop fusion | flops 655360 | bytes 795648 | tf_op jit(solution)/shard_map/convert_element_type | solution.py:343
  78.7 0.0 copy-done.1
  78.7 0.0 copy-start.2
  78.7 1.2 %copy-done.2 = bf16[512,1024]{1,0:T(8,128)(2,1)S(1)} copy-done((bf16[512,1024]{1,0:T(8,128)(2,1)S(1)}, bf16[512,1024]{1,0:T(8,128)(2,1)}, u32[]{:S(2)}) %copy-start.2) | copy-done | bytes 1048600
  80.0 31.8 %shard_map.137 = f32[128,1024]{1,0:T(8,128)S(1)} custom-call(bf16[128,1024]{1,0:T(8,128)(2,1)S(1)} %add_convert_fusion.1.x_ref, bf16[1024,512]{1,0:T(8,128)(2,1)S(1)} %copy-done.1, bf16[512,1024]{1,0:T(8,128)(2,1)S(1)} %copy-done.2), custom_call_target="tpu_custom_call" | custom-call | tf_op jit(solution)/shard_map/pallas_call | solution.py:255
  111.7 0.0 copy-done.3
  111.7 0.3 fusion
  112.0 0.3 multiply_reduce_fusion
  112.3 0.0 copy-done.11
  112.3 0.0 copy-done.12
  112.3 1.0 add_convert_fusion
  (12 shorter events, 0.1 us)
Async XLA Ops:
  0.0 73.7 %copy-start = (bf16[1024,1024]{1,0:T(8,128)(2,1)S(1)}, bf16[1024,1024]{1,0:T(8,128)(2,1)}, u32[]{:S(2)}) copy-start(bf16[1024,1024]{1,0:T(8,128)(2,1)} %param.21) | copy-start | bytes 6291460
  0.0 15.5 %copy-start.5 = (s32[16384,1]{0,1:T(1,128)S(1)}, s32[16384,1]{0,1:T(1,128)}, u32[]{:S(2)}) copy-start(s32[16384,1]{0,1:T(1,128)} %param.15) | copy-start | bytes 196612
  0.0 15.9 %copy-start.8 = (s32[16384]{0:T(1024)S(1)}, s32[16384]{0:T(1024)}, u32[]{:S(2)}) copy-start(s32[16384]{0:T(1024)} %param.16) | copy-start | bytes 196612
  0.0 16.6 %copy-start.13 = (s32[4]{0:T(128)S(1)}, s32[4]{0:T(128)}, u32[]{:S(2)}) copy-start(s32[4]{0:T(128)} %param.17) | copy-start | bytes 52
  1.9 13.5 %copy-start.9 = (s32[128]{0:T(128)}, s32[128]{0:T(128)S(1)}, u32[]{:S(2)}) copy-start(s32[128]{0:T(128)S(1)} %fusion.7) | copy-start | bytes 1540
  4.3 24.9 %all-to-all-start = ((bf16[128,2,1024]{2,1,0:T(2,128)(2,1)}), bf16[128,2,1024]{2,1,0:T(2,128)(2,1)S(1)}, u32[]{:S(2)}, u32[]{:S(2)}) async-start(bf16[128,2,1024]{2,1,0:T(2,128)(2,1)} %reshape.234), calls=%async_computation | async-start | bytes 1048576 | tf_op jit(solution)/shard_map/all_to_all | solution.py:318
  52.9 20.8 %copy-start.4 = (bf16[128,1024]{1,0:T(8,128)(2,1)S(1)}, bf16[128,1024]{1,0:T(8,128)(2,1)}, u32[]{:S(2)}) copy-start(bf16[128,1024]{1,0:T(8,128)(2,1)} %param.14) | copy-start | bytes 786436
  52.9 20.8 %copy-start.10 = (s32[128]{0:T(128)S(1)}, s32[128]{0:T(128)}, u32[]{:S(2)}) copy-start(s32[128]{0:T(128)} %copy-done.9) | copy-start | bytes 1540
  53.2 24.3 %copy-start.6 = (f32[1024]{0:T(1024)S(1)}, f32[1024]{0:T(1024)}, u32[]{:S(2)}) copy-start(f32[1024]{0:T(1024)} %param.25) | copy-start | bytes 12292
  53.2 24.3 %copy-start.7 = (f32[1024]{0:T(1024)S(1)}, f32[1024]{0:T(1024)}, u32[]{:S(2)}) copy-start(f32[1024]{0:T(1024)} %param.24) | copy-start | bytes 12292
  71.6 7.2 %copy-start.1 = (bf16[1024,512]{1,0:T(8,128)(2,1)S(1)}, bf16[1024,512]{1,0:T(8,128)(2,1)}, u32[]{:S(2)}) copy-start(bf16[1024,512]{1,0:T(8,128)(2,1)} %w1_ref.1) | copy-start | bytes 3145732
  76.2 35.6 %copy-start.3 = (f32[128,1024]{1,0:T(8,128)S(1)}, f32[128,1024]{1,0:T(8,128)}, u32[]{:S(2)}) copy-start(f32[128,1024]{1,0:T(8,128)} %get-tuple-element.12) | copy-start | bytes 1572868
  76.2 36.1 %copy-start.11 = (f32[1024]{0:T(1024)S(1)}, f32[1024]{0:T(1024)}, u32[]{:S(2)}) copy-start(f32[1024]{0:T(1024)} %param.27) | copy-start | bytes 12292
  76.2 36.1 %copy-start.12 = (f32[1024]{0:T(1024)S(1)}, f32[1024]{0:T(1024)}, u32[]{:S(2)}) copy-start(f32[1024]{0:T(1024)} %param.26) | copy-start | bytes 12292
  78.7 1.2 %copy-start.2 = (bf16[512,1024]{1,0:T(8,128)(2,1)S(1)}, bf16[512,1024]{1,0:T(8,128)(2,1)}, u32[]{:S(2)}) copy-start(bf16[512,1024]{1,0:T(8,128)(2,1)} %w2_ref.1) | copy-start | bytes 3145732

commit v15 on v14

--- a/solution.py
+++ b/solution.py
@@ -214,8 +214,6 @@
         ring_copy(kind).wait_send()
     for kind in range(4):
         pair_copy(kind).wait_send()
-    for z in range(chips):
-        back_copy(z).wait()
 
     def summed(z):
         mine = parts[block_rows(z, core), :]
@@ -231,14 +229,20 @@
             device_id_type=pl.DeviceIdType.MESH,
         )
 
+    back_copy(behind).wait_recv()
+    send_buf[0] = summed(behind).astype(send_buf.dtype)
+    sum_copy(0, behind).start()
+    back_copy(across).wait_recv()
     send_buf[1] = summed(across).astype(send_buf.dtype)
     sum_copy(1, ahead).start()
-    send_buf[0] = summed(behind).astype(send_buf.dtype)
-    sum_copy(0, behind).start()
+    back_copy(ahead).wait_recv()
     sum_copy(1, ahead).wait_recv()
     send_buf[2] = (summed(ahead) + ring_buf[1].astype(jnp.float32)).astype(send_buf.dtype)
     sum_copy(2, ahead).start()
+    back_copy(chip).wait_recv()
     total = summed(chip)
+    for z in range(chips):
+        back_copy(z).wait_send()
     sum_copy(0, behind).wait()
     total = total + ring_buf[0].astype(jnp.float32)
     sum_copy(1, ahead).wait_send()
@@ -336,8 +340,11 @@
         concat_axis=0,
         tiled=True,
     )
-    attn_rows = jnp.dot(
-        dispatch, returned.reshape(slot_count, width), preferred_element_type=jnp.float32
+    attn_rows = jnp.einsum(
+        "tsc,scd->td",
+        dispatch.reshape(tok_dev, devices, capacity),
+        returned,
+        preferred_element_type=jnp.float32,
     ).astype(jnp.bfloat16)
     projected_out = jnp.dot(attn_rows, w_out, preferred_element_type=jnp.float32)
     normed = layer_norm(projected_out + tokens.astype(jnp.float32), ln1_gain, ln1_bias).astype(

time: 114 us -> 112 us (0.982)
  blocking collectives: 18.4 us -> 0 us
  waiting for transfers between devices: 11.8 us -> 25.1 us
  starting transfers between devices: 11.2 us -> 17 us
  Pallas kernels: 50.7 us -> 49.4 us
  local copies, waits for them, and re-layouts: 6.94 us -> 5.64 us
    all_to_all x1 -> x0, blocking collectives: 18.4 us -> none  [per_device(): lax.all_to_all(attended.reshape(devices, capacity, width), ('req', 'mlp')...]
    all_to_all x0 -> x1, waiting for transfers between devices: none -> 13.3 us  [per_device(): lax.all_to_all(attended.reshape(devices, capacity, width), ('req', 'mlp')...]
    all_to_all x0 -> x1, starting transfers between devices: none -> 5.87 us  [per_device(): lax.all_to_all(attended.reshape(devices, capacity, width), ('req', 'mlp')...]
    reshape x1 -> x0, local copies, waits for them, and re-layouts: 2.12 us -> none  [per_device(): returned.reshape(slot_count, width)]
    pallas_call x1, Pallas kernels: 31.8 us -> 30.6 us  [feed_forward_block(): pl.pallas_call(block_kernel, in_specs=[pl.BlockSpec(memory_space=pltpu.VM...]
  transfers between devices with their start and end apart: 1 -> 2, of which waited for: 1 -> 2; matrix products, arithmetic and copies ran while one was open for 2% -> 2% of each run, Pallas kernels for 0% -> 0%
where the time goes in v15:
time: 112 us; the launch traced here: 111 us
  Pallas kernels  49.4 us (44%)
  waiting for transfers between devices  25.1 us (22%)
  starting transfers between devices  17 us (15%)
  matrix products  8.41 us (8%)
  local copies, waits for them, and re-layouts  5.64 us (5%)
  other arithmetic  5.6 us (5%)
    pallas_call x1, Pallas kernels, feed_forward_block(): pl.pallas_call(block_kernel, in_specs=[pl.BlockSpec(memory_space=pltpu.VM...  30.6 us
    pallas_call x1, Pallas kernels, attend(): pl.pallas_call(attention_kernel, grid=(pairs,), in_specs=[pl.BlockSpec((s...  18.9 us
    all_to_all x1, waiting for transfers between devices, per_device(): lax.all_to_all(attended.reshape(devices, capacity, width), ('req', 'mlp')...  13.3 us
    all_to_all x1, waiting for transfers between devices, per_device(): lax.all_to_all(outgoing.reshape(devices, capacity, width), ('req', 'mlp')...  11.8 us
    all_to_all x1, starting transfers between devices, per_device(): lax.all_to_all(outgoing.reshape(devices, capacity, width), ('req', 'mlp')...  11.2 us
    all_to_all x1, starting transfers between devices, per_device(): lax.all_to_all(attended.reshape(devices, capacity, width), ('req', 'mlp')...  5.87 us
    dot_general x1, matrix products, per_device(): jnp.dot(arrived.reshape(slot_count, width), w_qkv, preferred_element_type...  4.58 us
    dot_general x1, matrix products, per_device(): jnp.dot(attn_rows, w_out, preferred_element_type=jnp.float32)  2.48 us
  transfers between devices with their start and end apart: 2, of which 2 were waited for; matrix products, arithmetic and copies ran while one was open for 2% of the time, Pallas kernels for 0%

profile of v15, /device:TPU:0, one launch (start us, length us, event | category | flops | bytes accessed | tf_op | source)
XLA Modules:
  0.0 111.5 jit_solution(18214921900870035356)
XLA Ops:
  0.0 0.0 copy-start
  0.0 0.0 copy-start.5
  0.0 0.0 copy-start.8
  0.0 0.0 copy-start.13
  0.0 0.8 fusion.15
  0.8 0.1 fusion.11
  0.9 0.2 reduce_window_sum.22
  1.1 0.2 select_reduce_fusion.1
  1.3 0.7 fusion.14
  1.9 0.0 copy-start.9
  1.9 1.3 %convolution_convert_fusion.1 = bf16[256,1024]{1,0:T(8,128)(2,1)S(1)} fusion(bf16[128,1024]{1,0:T(8,128)(2,1)} %param.14, s32[128]{0:T(128)S(1)} %fusion.14), kind=kOutput, calls=%fused_computation.1 | convolution fusion | flops 67403776 | bytes 786944 | tf_op jit(solution)/shard_map/tr,td->rd/dot_general | solution.py:319
  3.3 1.0 reshape.246
  4.3 0.0 copy-done.9
  4.3 11.2 %all-to-all-start = ((bf16[128,2,1024]{2,1,0:T(2,128)(2,1)}), bf16[128,2,1024]{2,1,0:T(2,128)(2,1)S(1)}, u32[]{:S(2)}, u32[]{:S(2)}) async-start(bf16[128,2,1024]{2,1,0:T(2,128)(2,1)} %reshape.246), calls=%async_computation | async-start | bytes 1048576 | tf_op jit(solution)/shard_map/all_to_all | solution.py:322
  15.4 0.0 copy-done.5
  15.5 0.1 compare_convert_fusion
  15.5 0.1 copy.35
  15.6 0.2 reduce_window_sum.23
  15.8 0.1 copy.36
  15.9 0.0 copy-done.8
  15.9 0.2 select_reduce_fusion
  16.1 0.1 copy.38
  16.2 0.1 copy.40
  16.3 0.1 add.120
  16.4 0.1 reduce_sum.86.rfill_ref
  16.5 0.0 copy-done.13
  16.6 0.1 broadcast_bitcast_fusion
  16.6 0.1 copy.37
  16.7 0.1 copy.42
  16.9 0.1 select_n.83.ntag_ref
  17.0 0.1 copy.43
  17.1 0.1 select_n.85.nrow_ref
  17.3 0.1 reshape_reshape.3.rreq_ref
  17.4 11.8 %all-to-all-done = bf16[128,2,1024]{2,1,0:T(2,128)(2,1)S(1)} async-done(((bf16[128,2,1024]{2,1,0:T(2,128)(2,1)}), bf16[128,2,1024]{2,1,0:T(2,128)(2,1)S(1)}, u32[]{:S(2)}, u32[]{:S(2)}) %all-to-all-start) | async-done | bytes 524320 | tf_op jit(solution)/shard_map/all_to_all | solution.py:322
  29.2 0.2 reshape.247
  29.4 4.6 %convolution_convert_fusion.q_ref.kn_ref.vn_ref = bf16[256,3072]{1,0:T(8,128)(2,1)S(1)} fusion(bf16[256,1024]{1,0:T(8,128)(2,1)S(1)} %reshape.247, bf16[1024,3072]{1,0:T(8,128)(2,1)} %param.20), kind=kOutput, calls=%fused_computation | convolution fusion | flops 1611399168 | bytes 8388608 | tf_op jit(solution)/shard_map/dot_general | solution.py:329
  34.0 0.0 copy-start.4
  34.0 0.0 copy-start.10
  34.0 18.9 %shard_map.136 = bf16[256,1024]{1,0:T(8,128)(2,1)S(1)} custom-call(bf16[256,3072]{1,0:T(8,128)(2,1)S(1)} %convolution_convert_fusion.q_ref.kn_ref.vn_ref, bf16[256,3072]{1,0:T(8,128)(2,1)S(1)} %convolution_convert_fusion.q_ref.kn_ref.vn_ref, bf16[256,3072]{1,0:T(8,128)(2,1)S(1)} %convolution_convert_fusion.q_ref.kn_ref.vn_ref, bf16[2048,1024]{1,0:T(8,128)(2,1)} %bitcast.28, ...), custom_call_target="tpu_custom_call" | custom-call | tf_op jit(solution)/shard_map/pallas_call | solution.py:93
  52.9 0.0 copy-start.6
  52.9 0.0 copy-start.7
  52.9 1.0 reshape.251
  53.9 0.0 copy-start.1
  53.9 5.9 %all-to-all-start.1 = ((bf16[128,2,1024]{2,1,0:T(2,128)(2,1)}), bf16[128,2,1024]{2,1,0:T(2,128)(2,1)}, u32[]{:S(2)}, u32[]{:S(2)}) async-start(bf16[128,2,1024]{2,1,0:T(2,128)(2,1)} %reshape.251), calls=%async_computation.1 | async-start | bytes 1048576 | tf_op jit(solution)/shard_map/all_to_all | solution.py:336
  59.8 13.3 %all-to-all-done.1 = bf16[128,2,1024]{2,1,0:T(2,128)(2,1)} async-done(((bf16[128,2,1024]{2,1,0:T(2,128)(2,1)}), bf16[128,2,1024]{2,1,0:T(2,128)(2,1)}, u32[]{:S(2)}, u32[]{:S(2)}) %all-to-all-start.1) | async-done | bytes 524320 | tf_op jit(solution)/shard_map/all_to_all | solution.py:336
  73.1 0.0 copy-done
  73.1 0.0 copy-done.4
  73.1 0.0 copy-done.10
  73.1 2.5 %fusion.16 = (f32[128]{0:T(128)S(1)}, f32[128,1024]{1,0:T(8,128)}) fusion(bf16[128,1024]{1,0:T(8,128)(2,1)S(1)} %copy-done.4, bf16[1024,1024]{1,0:T(8,128)(2,1)S(1)} %copy-done, bf16[128,2,1024]{2,1,0:T(2,128)(2,1)} %all-to-all-done.1, s32[128,2]{0,1:T(2,128)S(1)} %multiply_add_fusion, s32[128]{0:T(128)S(1)} %copy-done.10), kind=kOutput, calls=%fused_computation.49 | convolution fusion | flops 336101248 | bytes 3409920 | tf_op jit(solution)/shard_map/dot_general | solution.py:349
  75.6 0.0 copy-start.12
  75.6 1.3 %multiply_reduce_fusion.1 = f32[128]{0:T(128)S(1)} fusion(f32[128,1024]{1,0:T(8,128)} %get-tuple-element.12, f32[128]{0:T(128)S(1)} %broadcast_multiply_fusion.1), kind=kLoop, calls=%fused_computation.10 | loop fusion | flops 393088 | bytes 525312 | tf_op jit(solution)/shard_map/reduce_sum | solution.py:16
  76.9 0.0 copy-done.6
  76.9 0.0 copy-done.7
  76.9 1.2 %add_convert_fusion.1.x_ref = bf16[128,1024]{1,0:T(8,128)(2,1)S(1)} fusion(f32[128,1024]{1,0:T(8,128)} %get-tuple-element.12, f32[1024]{0:T(1024)S(1)} %copy-done.6, f32[1024]{0:T(1024)S(1)} %copy-done.7, f32[128]{0:T(128)S(1)} %add_rsqrt_fusion.1, f32[128]{0:T(128)S(1)} %broadcast_multiply_fusion.1), kind=kLoop, calls=%fused_computation.9 | loop fusion | flops 655360 | bytes 795648 | tf_op jit(solution)/shard_map/convert_element_type | solution.py:350
  78.1 0.0 copy-done.1
  78.1 0.0 copy-start.2
  78.1 1.2 %copy-done.2 = bf16[512,1024]{1,0:T(8,128)(2,1)S(1)} copy-done((bf16[512,1024]{1,0:T(8,128)(2,1)S(1)}, bf16[512,1024]{1,0:T(8,128)(2,1)}, u32[]{:S(2)}) %copy-start.2) | copy-done | bytes 1048600
  79.3 30.6 %shard_map.137 = f32[128,1024]{1,0:T(8,128)S(1)} custom-call(bf16[128,1024]{1,0:T(8,128)(2,1)S(1)} %add_convert_fusion.1.x_ref, bf16[1024,512]{1,0:T(8,128)(2,1)S(1)} %copy-done.1, bf16[512,1024]{1,0:T(8,128)(2,1)S(1)} %copy-done.2), custom_call_target="tpu_custom_call" | custom-call | tf_op jit(solution)/shard_map/pallas_call | solution.py:259
  109.9 0.0 copy-done.3
  109.9 0.3 fusion.3
  110.2 0.3 multiply_reduce_fusion
  110.5 0.0 copy-done.11
  110.5 0.0 copy-done.12
  110.5 1.0 add_convert_fusion
  (13 shorter events, 0.1 us)
Async XLA Ops:
  0.0 73.1 %copy-start = (bf16[1024,1024]{1,0:T(8,128)(2,1)S(1)}, bf16[1024,1024]{1,0:T(8,128)(2,1)}, u32[]{:S(2)}) copy-start(bf16[1024,1024]{1,0:T(8,128)(2,1)} %param.21) | copy-start | bytes 6291460
  0.0 15.4 %copy-start.5 = (s32[16384,1]{0,1:T(1,128)S(1)}, s32[16384,1]{0,1:T(1,128)}, u32[]{:S(2)}) copy-start(s32[16384,1]{0,1:T(1,128)} %param.15) | copy-start | bytes 196612
  0.0 15.9 %copy-start.8 = (s32[16384]{0:T(1024)S(1)}, s32[16384]{0:T(1024)}, u32[]{:S(2)}) copy-start(s32[16384]{0:T(1024)} %param.16) | copy-start | bytes 196612
  0.0 16.5 %copy-start.13 = (s32[4]{0:T(128)S(1)}, s32[4]{0:T(128)}, u32[]{:S(2)}) copy-start(s32[4]{0:T(128)} %param.17) | copy-start | bytes 52
  1.9 2.4 %copy-start.9 = (s32[128]{0:T(128)}, s32[128]{0:T(128)S(1)}, u32[]{:S(2)}) copy-start(s32[128]{0:T(128)S(1)} %fusion.14) | copy-start | bytes 1540
  4.3 24.9 %all-to-all-start = ((bf16[128,2,1024]{2,1,0:T(2,128)(2,1)}), bf16[128,2,1024]{2,1,0:T(2,128)(2,1)S(1)}, u32[]{:S(2)}, u32[]{:S(2)}) async-start(bf16[128,2,1024]{2,1,0:T(2,128)(2,1)} %reshape.246), calls=%async_computation | async-start | bytes 1048576 | tf_op jit(solution)/shard_map/all_to_all | solution.py:322
  34.0 39.1 %copy-start.4 = (bf16[128,1024]{1,0:T(8,128)(2,1)S(1)}, bf16[128,1024]{1,0:T(8,128)(2,1)}, u32[]{:S(2)}) copy-start(bf16[128,1024]{1,0:T(8,128)(2,1)} %param.14) | copy-start | bytes 786436
  34.0 39.1 %copy-start.10 = (s32[128]{0:T(128)S(1)}, s32[128]{0:T(128)}, u32[]{:S(2)}) copy-start(s32[128]{0:T(128)} %copy-done.9) | copy-start | bytes 1540
  52.9 24.0 %copy-start.6 = (f32[1024]{0:T(1024)S(1)}, f32[1024]{0:T(1024)}, u32[]{:S(2)}) copy-start(f32[1024]{0:T(1024)} %param.25) | copy-start | bytes 12292
  52.9 24.0 %copy-start.7 = (f32[1024]{0:T(1024)S(1)}, f32[1024]{0:T(1024)}, u32[]{:S(2)}) copy-start(f32[1024]{0:T(1024)} %param.24) | copy-start | bytes 12292
  53.9 24.2 %copy-start.1 = (bf16[1024,512]{1,0:T(8,128)(2,1)S(1)}, bf16[1024,512]{1,0:T(8,128)(2,1)}, u32[]{:S(2)}) copy-start(bf16[1024,512]{1,0:T(8,128)(2,1)} %w1_ref.1) | copy-start | bytes 3145732
  53.9 19.2 %all-to-all-start.1 = ((bf16[128,2,1024]{2,1,0:T(2,128)(2,1)}), bf16[128,2,1024]{2,1,0:T(2,128)(2,1)}, u32[]{:S(2)}, u32[]{:S(2)}) async-start(bf16[128,2,1024]{2,1,0:T(2,128)(2,1)} %reshape.251), calls=%async_computation.1 | async-start | bytes 1048576 | tf_op jit(solution)/shard_map/all_to_all | solution.py:336
  75.6 34.4 %copy-start.3 = (f32[128,1024]{1,0:T(8,128)S(1)}, f32[128,1024]{1,0:T(8,128)}, u32[]{:S(2)}) copy-start(f32[128,1024]{1,0:T(8,128)} %get-tuple-element.12) | copy-start | bytes 1572868
  75.6 34.9 %copy-start.11 = (f32[1024]{0:T(1024)S(1)}, f32[1024]{0:T(1024)}, u32[]{:S(2)}) copy-start(f32[1024]{0:T(1024)} %param.27) | copy-start | bytes 12292
  75.6 34.9 %copy-start.12 = (f32[1024]{0:T(1024)S(1)}, f32[1024]{0:T(1024)}, u32[]{:S(2)}) copy-start(f32[1024]{0:T(1024)} %param.26) | copy-start | bytes 12292
  78.1 1.2 %copy-start.2 = (bf16[512,1024]{1,0:T(8,128)(2,1)S(1)}, bf16[512,1024]{1,0:T(8,128)(2,1)}, u32[]{:S(2)}) copy-start(bf16[512,1024]{1,0:T(8,128)(2,1)} %w2_ref.1) | copy-start | bytes 3145732

commit v16 on v15

--- a/solution.py
+++ b/solution.py
@@ -125,9 +125,10 @@
 
 
 def block_kernel(
-    x_ref, w1_ref, w2_ref, o_ref, held, parts, pair_buf, send_buf, ring_buf,
+    y_ref, gain_ref, shift_ref, w1_ref, w2_ref, o_ref, x_ref, held, parts, pair_buf, send_buf, ring_buf,
     ring_send, ring_recv, pair_send, pair_recv, back_send, back_recv, sum_send, sum_recv,
 ):
+    x_ref[...] = layer_norm(y_ref[...], gain_ref[...], shift_ref[...]).astype(x_ref.dtype)
     req = lax.axis_index("req")
     me = lax.axis_index("mlp")
     chips = lax.axis_size("mlp") // 2
@@ -247,10 +248,10 @@
     total = total + ring_buf[0].astype(jnp.float32)
     sum_copy(1, ahead).wait_send()
     sum_copy(2, ahead).wait()
-    o_ref[...] = total + ring_buf[2].astype(jnp.float32)
-
-
-def feed_forward_block(block, w_fc1, w_fc2):
+    o_ref[...] = x_ref[...].astype(jnp.float32) + (total + ring_buf[2].astype(jnp.float32))
+
+
+def feed_forward_block(block, gain, shift, w_fc1, w_fc2):
     groups = lax.axis_size("mlp")
     chips = groups // 2
     rows, width = block.shape
@@ -258,11 +259,12 @@
     out_width = w_fc2.shape[1]
     return pl.pallas_call(
         block_kernel,
-        in_specs=[pl.BlockSpec(memory_space=pltpu.VMEM)] * 3,
+        in_specs=[pl.BlockSpec(memory_space=pltpu.VMEM)] * 5,
         out_specs=pl.BlockSpec(memory_space=pltpu.VMEM),
         out_shape=jax.ShapeDtypeStruct((rows, out_width), jnp.float32),
         scratch_shapes=[
-            pltpu.VMEM((total, width), block.dtype),
+            pltpu.VMEM((rows, width), jnp.bfloat16),
+            pltpu.VMEM((total, width), jnp.bfloat16),
             pltpu.VMEM((total, out_width), jnp.bfloat16),
             pltpu.VMEM((chips, rows, out_width), jnp.bfloat16),
             pltpu.VMEM((3, rows, out_width), jnp.bfloat16),
@@ -279,7 +281,7 @@
         compiler_params=pltpu.CompilerParams(
             collective_id=2, has_side_effects=True, vmem_limit_bytes=48 * 1024 * 1024
         ),
-    )(block, w_fc1, w_fc2)
+    )(block, gain.reshape(1, -1), shift.reshape(1, -1), w_fc1, w_fc2)
 
 
 def per_device(
@@ -347,11 +349,10 @@
         preferred_element_type=jnp.float32,
     ).astype(jnp.bfloat16)
     projected_out = jnp.dot(attn_rows, w_out, preferred_element_type=jnp.float32)
-    normed = layer_norm(projected_out + tokens.astype(jnp.float32), ln1_gain, ln1_bias).astype(
-        jnp.bfloat16
-    )
-    summed = feed_forward_block(normed, w_fc1, w_fc2)
-    return layer_norm(normed.astype(jnp.float32) + summed, ln2_gain, ln2_bias).astype(jnp.bfloat16)
+    mixed = feed_forward_block(
+        projected_out + tokens.astype(jnp.float32), ln1_gain, ln1_bias, w_fc1, w_fc2
+    )
+    return layer_norm(mixed, ln2_gain, ln2_bias).astype(jnp.bfloat16)
 
 
 def solution(mesh):

time: 112 us -> 108 us (0.964)
  other arithmetic: 5.6 us -> 2.75 us
  matrix products: 8.41 us -> 6.56 us
  starting transfers between devices: 17 us -> 15.8 us
  local copies, waits for them, and re-layouts: 5.64 us -> 6.83 us
    dot_general x1, matrix products: 2.48 us -> 0.63 us  [per_device(): jnp.dot(attn_rows, w_out, preferred_element_type=jnp.float32)]
    reduce_sum x2 -> x1, other arithmetic: 1.59 us -> 0.2 us  [layer_norm(): spread = jnp.mean(center * center, axis=-1, keepdims=True)]
    convert_element_type x2 -> x1, other arithmetic: 2.16 us -> 0.86 us  [per_device(): return layer_norm(mixed, ln2_gain, ln2_bias).astype(jnp.bfloat16)]
    all_to_all x1, starting transfers between devices: 5.87 us -> 4.61 us  [per_device(): lax.all_to_all(attended.reshape(devices, capacity, width), ('req', 'mlp')...]
    unnamed x30 -> x28, local copies, waits for them, and re-layouts: 1.36 us -> 2.58 us
where the time goes in v16:
time: 108 us; the launch traced here: 107 us
  Pallas kernels  49.8 us (46%)
  waiting for transfers between devices  25.5 us (24%)
  starting transfers between devices  15.8 us (15%)
  local copies, waits for them, and re-layouts  6.83 us (6%)
  matrix products  6.56 us (6%)
  other arithmetic  2.75 us (3%)
    pallas_call x1, Pallas kernels, feed_forward_block(): pl.pallas_call(block_kernel, in_specs=[pl.BlockSpec(memory_space=pltpu.VM...  30.8 us
    pallas_call x1, Pallas kernels, attend(): pl.pallas_call(attention_kernel, grid=(pairs,), in_specs=[pl.BlockSpec((s...  19 us
    all_to_all x1, waiting for transfers between devices, per_device(): lax.all_to_all(attended.reshape(devices, capacity, width), ('req', 'mlp')...  13.7 us
    all_to_all x1, waiting for transfers between devices, per_device(): lax.all_to_all(outgoing.reshape(devices, capacity, width), ('req', 'mlp')...  11.8 us
    all_to_all x1, starting transfers between devices, per_device(): lax.all_to_all(outgoing.reshape(devices, capacity, width), ('req', 'mlp')...  11.2 us
    all_to_all x1, starting transfers between devices, per_device(): lax.all_to_all(attended.reshape(devices, capacity, width), ('req', 'mlp')...  4.61 us
    dot_general x1, matrix products, per_device(): jnp.dot(arrived.reshape(slot_count, width), w_qkv, preferred_element_type...  4.58 us
    unnamed x28, local copies, waits for them, and re-layouts  2.58 us
  transfers between devices with their start and end apart: 2, of which 2 were waited for; matrix products, arithmetic and copies ran while one was open for 2% of the time, Pallas kernels for 0%

profile of v16, /device:TPU:0, one launch (start us, length us, event | category | flops | bytes accessed | tf_op | source)
XLA Modules:
  0.0 107.5 jit_solution(824796165354506502)
XLA Ops:
  0.0 0.0 copy-start
  0.0 0.0 copy-start.6
  0.0 0.0 copy-start.7
  0.0 0.0 copy-start.12
  0.0 0.8 fusion.14
  0.8 0.1 fusion.10
  0.9 0.2 reduce_window_sum.22
  1.1 0.2 select_reduce_fusion.1
  1.3 0.7 fusion.13
  1.9 0.0 copy-start.8
  1.9 1.3 %convolution_convert_fusion.1 = bf16[256,1024]{1,0:T(8,128)(2,1)S(1)} fusion(bf16[128,1024]{1,0:T(8,128)(2,1)} %param.14, s32[128]{0:T(128)S(1)} %fusion.13), kind=kOutput, calls=%fused_computation.1 | convolution fusion | flops 67403776 | bytes 786944 | tf_op jit(solution)/shard_map/tr,td->rd/dot_general | solution.py:321
  3.3 1.0 reshape.238
  4.3 0.0 copy-done.8
  4.3 11.2 %all-to-all-start = ((bf16[128,2,1024]{2,1,0:T(2,128)(2,1)}), bf16[128,2,1024]{2,1,0:T(2,128)(2,1)S(1)}, u32[]{:S(2)}, u32[]{:S(2)}) async-start(bf16[128,2,1024]{2,1,0:T(2,128)(2,1)} %reshape.238), calls=%async_computation | async-start | bytes 1048576 | tf_op jit(solution)/shard_map/all_to_all | solution.py:324
  15.4 0.0 copy-done.6
  15.5 0.1 compare_convert_fusion
  15.5 0.1 copy.35
  15.6 0.2 reduce_window_sum.23
  15.8 0.1 copy.36
  15.9 0.0 copy-done.7
  15.9 0.2 select_reduce_fusion
  16.1 0.1 copy.38
  16.2 0.1 copy.40
  16.3 0.1 add.101
  16.4 0.1 reduce_sum.66.rfill_ref
  16.5 0.0 copy-done.12
  16.6 0.1 broadcast_bitcast_fusion
  16.6 0.1 copy.37
  16.7 0.1 copy.42
  16.9 0.1 select_n.83.ntag_ref
  17.0 0.1 copy.43
  17.1 0.1 select_n.85.nrow_ref
  17.3 0.1 reshape_reshape.3.rreq_ref
  17.4 11.8 %all-to-all-done = bf16[128,2,1024]{2,1,0:T(2,128)(2,1)S(1)} async-done(((bf16[128,2,1024]{2,1,0:T(2,128)(2,1)}), bf16[128,2,1024]{2,1,0:T(2,128)(2,1)S(1)}, u32[]{:S(2)}, u32[]{:S(2)}) %all-to-all-start) | async-done | bytes 524320 | tf_op jit(solution)/shard_map/all_to_all | solution.py:324
  29.2 0.2 reshape.239
  29.4 4.6 %convolution_convert_fusion.q_ref.kn_ref.vn_ref = bf16[256,3072]{1,0:T(8,128)(2,1)S(1)} fusion(bf16[256,1024]{1,0:T(8,128)(2,1)S(1)} %reshape.239, bf16[1024,3072]{1,0:T(8,128)(2,1)} %param.20), kind=kOutput, calls=%fused_computation | convolution fusion | flops 1611399168 | bytes 8388608 | tf_op jit(solution)/shard_map/dot_general | solution.py:331
  33.9 0.0 copy-start.5
  34.0 0.0 copy-start.9
  34.0 19.0 %shard_map.136 = bf16[256,1024]{1,0:T(8,128)(2,1)S(1)} custom-call(bf16[256,3072]{1,0:T(8,128)(2,1)S(1)} %convolution_convert_fusion.q_ref.kn_ref.vn_ref, bf16[256,3072]{1,0:T(8,128)(2,1)S(1)} %convolution_convert_fusion.q_ref.kn_ref.vn_ref, bf16[256,3072]{1,0:T(8,128)(2,1)S(1)} %convolution_convert_fusion.q_ref.kn_ref.vn_ref, bf16[2048,1024]{1,0:T(8,128)(2,1)} %bitcast.30, ...), custom_call_target="tpu_custom_call" | custom-call | tf_op jit(solution)/shard_map/pallas_call | solution.py:93
  52.9 0.0 copy-start.3
  53.0 0.0 copy-start.4
  53.0 1.0 reshape.243
  54.0 4.6 %all-to-all-start.1 = ((bf16[128,2,1024]{2,1,0:T(2,128)(2,1)}), bf16[128,2,1024]{2,1,0:T(2,128)(2,1)S(1)}, u32[]{:S(2)}, u32[]{:S(2)}) async-start(bf16[128,2,1024]{2,1,0:T(2,128)(2,1)} %reshape.243), calls=%async_computation.1 | async-start | bytes 1048576 | tf_op jit(solution)/shard_map/all_to_all | solution.py:338
  58.6 0.0 copy-start.10
  58.6 0.0 copy-start.11
  58.6 13.7 %all-to-all-done.1 = bf16[128,2,1024]{2,1,0:T(2,128)(2,1)S(1)} async-done(((bf16[128,2,1024]{2,1,0:T(2,128)(2,1)}), bf16[128,2,1024]{2,1,0:T(2,128)(2,1)S(1)}, u32[]{:S(2)}, u32[]{:S(2)}) %all-to-all-start.1) | async-done | bytes 524320 | tf_op jit(solution)/shard_map/all_to_all | solution.py:338
  72.3 0.0 copy-done
  72.3 0.0 copy-done.5
  72.3 0.0 copy-done.9
  72.3 0.6 convolution_add_fusion.y_ref
  72.9 0.0 copy-done.3
  73.0 0.0 copy-done.4
  73.0 0.0 copy-start.1
  73.0 1.2 %copy-done.1 = bf16[1024,512]{1,0:T(8,128)(2,1)S(1)} copy-done((bf16[1024,512]{1,0:T(8,128)(2,1)S(1)}, bf16[1024,512]{1,0:T(8,128)(2,1)}, u32[]{:S(2)}) %copy-start.1) | copy-done | bytes 1048600
  74.2 0.0 copy-start.2
  74.2 1.2 %copy-done.2 = bf16[512,1024]{1,0:T(8,128)(2,1)S(1)} copy-done((bf16[512,1024]{1,0:T(8,128)(2,1)S(1)}, bf16[512,1024]{1,0:T(8,128)(2,1)}, u32[]{:S(2)}) %copy-start.2) | copy-done | bytes 1048600
  75.4 30.8 %shard_map.137 = f32[128,1024]{1,0:T(8,128)S(1)} custom-call(f32[128,1024]{1,0:T(8,128)S(1)} %convolution_add_fusion.y_ref, f32[1,1024]{1,0:T(1,128)S(1)} %bitcast.28, f32[1,1024]{1,0:T(1,128)S(1)} %bitcast.29, bf16[1024,512]{1,0:T(8,128)(2,1)S(1)} %copy-done.1, bf16[512,1024]{1,0:T(8,128)(2,1)S(1)} %copy-done.2), custom_call_target="tpu_custom_call" | custom-call | tf_op jit(solution)/shard_map/pallas_call | solution.py:260
  106.2 0.1 reduce_sum.64
  106.4 0.2 multiply_reduce_fusion
  106.6 0.0 copy-done.10
  106.6 0.0 copy-done.11
  106.6 0.9 add_convert_fusion
  (9 shorter events, 0.1 us)
Async XLA Ops:
  0.0 72.3 %copy-start = (bf16[1024,1024]{1,0:T(8,128)(2,1)S(1)}, bf16[1024,1024]{1,0:T(8,128)(2,1)}, u32[]{:S(2)}) copy-start(bf16[1024,1024]{1,0:T(8,128)(2,1)} %param.21) | copy-start | bytes 6291460
  0.0 15.4 %copy-start.6 = (s32[16384,1]{0,1:T(1,128)S(1)}, s32[16384,1]{0,1:T(1,128)}, u32[]{:S(2)}) copy-start(s32[16384,1]{0,1:T(1,128)} %param.15) | copy-start | bytes 196612
  0.0 15.9 %copy-start.7 = (s32[16384]{0:T(1024)S(1)}, s32[16384]{0:T(1024)}, u32[]{:S(2)}) copy-start(s32[16384]{0:T(1024)} %param.16) | copy-start | bytes 196612
  0.0 16.5 %copy-start.12 = (s32[4]{0:T(128)S(1)}, s32[4]{0:T(128)}, u32[]{:S(2)}) copy-start(s32[4]{0:T(128)} %param.17) | copy-start | bytes 52
  1.9 2.4 %copy-start.8 = (s32[128]{0:T(128)}, s32[128]{0:T(128)S(1)}, u32[]{:S(2)}) copy-start(s32[128]{0:T(128)S(1)} %fusion.13) | copy-start | bytes 1540
  4.3 24.9 %all-to-all-start = ((bf16[128,2,1024]{2,1,0:T(2,128)(2,1)}), bf16[128,2,1024]{2,1,0:T(2,128)(2,1)S(1)}, u32[]{:S(2)}, u32[]{:S(2)}) async-start(bf16[128,2,1024]{2,1,0:T(2,128)(2,1)} %reshape.238), calls=%async_computation | async-start | bytes 1048576 | tf_op jit(solution)/shard_map/all_to_all | solution.py:324
  33.9 38.3 %copy-start.5 = (bf16[128,1024]{1,0:T(8,128)(2,1)S(1)}, bf16[128,1024]{1,0:T(8,128)(2,1)}, u32[]{:S(2)}) copy-start(bf16[128,1024]{1,0:T(8,128)(2,1)} %param.14) | copy-start | bytes 786436
  34.0 38.3 %copy-start.9 = (s32[128]{0:T(128)S(1)}, s32[128]{0:T(128)}, u32[]{:S(2)}) copy-start(s32[128]{0:T(128)} %copy-done.8) | copy-start | bytes 1540
  52.9 20.0 %copy-start.3 = (f32[1024]{0:T(1024)S(1)}, f32[1024]{0:T(1024)}, u32[]{:S(2)}) copy-start(f32[1024]{0:T(1024)} %param.24) | copy-start | bytes 12292
  53.0 20.0 %copy-start.4 = (f32[1024]{0:T(1024)S(1)}, f32[1024]{0:T(1024)}, u32[]{:S(2)}) copy-start(f32[1024]{0:T(1024)} %param.25) | copy-start | bytes 12292
  54.0 18.3 %all-to-all-start.1 = ((bf16[128,2,1024]{2,1,0:T(2,128)(2,1)}), bf16[128,2,1024]{2,1,0:T(2,128)(2,1)S(1)}, u32[]{:S(2)}, u32[]{:S(2)}) async-start(bf16[128,2,1024]{2,1,0:T(2,128)(2,1)} %reshape.243), calls=%async_computation.1 | async-start | bytes 1048576 | tf_op jit(solution)/shard_map/all_to_all | solution.py:338
  58.6 48.0 %copy-start.10 = (f32[1024]{0:T(1024)S(1)}, f32[1024]{0:T(1024)}, u32[]{:S(2)}) copy-start(f32[1024]{0:T(1024)} %param.27) | copy-start | bytes 12292
  58.6 48.0 %copy-start.11 = (f32[1024]{0:T(1024)S(1)}, f32[1024]{0:T(1024)}, u32[]{:S(2)}) copy-start(f32[1024]{0:T(1024)} %param.26) | copy-start | bytes 12292
  73.0 1.2 %copy-start.1 = (bf16[1024,512]{1,0:T(8,128)(2,1)S(1)}, bf16[1024,512]{1,0:T(8,128)(2,1)}, u32[]{:S(2)}) copy-start(bf16[1024,512]{1,0:T(8,128)(2,1)} %w1_ref.1) | copy-start | bytes 3145732
  74.2 1.2 %copy-start.2 = (bf16[512,1024]{1,0:T(8,128)(2,1)S(1)}, bf16[512,1024]{1,0:T(8,128)(2,1)}, u32[]{:S(2)}) copy-start(bf16[512,1024]{1,0:T(8,128)(2,1)} %w2_ref.1) | copy-start | bytes 3145732

commit v17 on v16

--- a/solution.py
+++ b/solution.py
@@ -125,9 +125,13 @@
 
 
 def block_kernel(
-    y_ref, gain_ref, shift_ref, w1_ref, w2_ref, o_ref, x_ref, held, parts, pair_buf, send_buf, ring_buf,
+    y_ref, gain_ref, shift_ref, w1_hbm, w2_hbm, o_ref, w1_ref, w2_ref, load_sem, x_ref, held, parts, pair_buf, send_buf, ring_buf,
     ring_send, ring_recv, pair_send, pair_recv, back_send, back_recv, sum_send, sum_recv,
 ):
+    load_one = pltpu.make_async_copy(w1_hbm, w1_ref, load_sem.at[0])
+    load_two = pltpu.make_async_copy(w2_hbm, w2_ref, load_sem.at[1])
+    load_one.start()
+    load_two.start()
     x_ref[...] = layer_norm(y_ref[...], gain_ref[...], shift_ref[...]).astype(x_ref.dtype)
     req = lax.axis_index("req")
     me = lax.axis_index("mlp")
@@ -194,6 +198,8 @@
     ring_copy(0).start()
     ring_copy(1).start()
     pair_copy(0).start()
+    load_one.wait()
+    load_two.wait()
     feed_forward(x_ref[...], block_rows(chip, core))
     ring_copy(0).wait_recv()
     ring_copy(2).start()
@@ -259,10 +265,13 @@
     out_width = w_fc2.shape[1]
     return pl.pallas_call(
         block_kernel,
-        in_specs=[pl.BlockSpec(memory_space=pltpu.VMEM)] * 5,
+        in_specs=[pl.BlockSpec(memory_space=pltpu.VMEM)] * 3 + [pl.BlockSpec(memory_space=pl.ANY)] * 2,
         out_specs=pl.BlockSpec(memory_space=pltpu.VMEM),
         out_shape=jax.ShapeDtypeStruct((rows, out_width), jnp.float32),
         scratch_shapes=[
+            pltpu.VMEM(w_fc1.shape, w_fc1.dtype),
+            pltpu.VMEM(w_fc2.shape, w_fc2.dtype),
+            pltpu.SemaphoreType.DMA((2,)),
             pltpu.VMEM((rows, width), jnp.bfloat16),
             pltpu.VMEM((total, width), jnp.bfloat16),
             pltpu.VMEM((total, out_width), jnp.bfloat16),
@@ -279,7 +288,7 @@
             pltpu.SemaphoreType.DMA((3,)),
         ],
         compiler_params=pltpu.CompilerParams(
-            collective_id=2, has_side_effects=True, vmem_limit_bytes=48 * 1024 * 1024
+            collective_id=2, has_side_effects=True, vmem_limit_bytes=62 * 1024 * 1024
         ),
     )(block, gain.reshape(1, -1), shift.reshape(1, -1), w_fc1, w_fc2)
 

time: 108 us -> 111 us (1.028)
  other arithmetic: 2.75 us -> 5.87 us
  local copies, waits for them, and re-layouts: 6.83 us -> 4.29 us
  Pallas kernels: 49.8 us -> 51.8 us
    unnamed x28 -> x16, local copies, waits for them, and re-layouts: 2.58 us -> 0.12 us
    pallas_call x1, Pallas kernels: 30.8 us -> 32.8 us  [feed_forward_block(): pl.pallas_call(block_kernel, in_specs=[pl.BlockSpec(memory_space=pltpu.VM...]
where the time goes in v17:
time: 111 us
  Pallas kernels  51.8 us (47%)
  waiting for transfers between devices  25.5 us (23%)
  starting transfers between devices  15.8 us (14%)
  matrix products  7.36 us (7%)
  other arithmetic  5.87 us (5%)
  local copies, waits for them, and re-layouts  4.29 us (4%)
    pallas_call x1, Pallas kernels, feed_forward_block(): pl.pallas_call(block_kernel, in_specs=[pl.BlockSpec(memory_space=pltpu.VM...  32.8 us
    pallas_call x1, Pallas kernels, attend(): pl.pallas_call(attention_kernel, grid=(pairs,), in_specs=[pl.BlockSpec((s...  19.1 us
    all_to_all x1, waiting for transfers between devices, per_device(): lax.all_to_all(attended.reshape(devices, capacity, width), ('req', 'mlp')...  13.7 us
    all_to_all x1, waiting for transfers between devices, per_device(): lax.all_to_all(outgoing.reshape(devices, capacity, width), ('req', 'mlp')...  11.8 us
    all_to_all x1, starting transfers between devices, per_device(): lax.all_to_all(outgoing.reshape(devices, capacity, width), ('req', 'mlp')...  11.1 us
    all_to_all x1, starting transfers between devices, per_device(): lax.all_to_all(attended.reshape(devices, capacity, width), ('req', 'mlp')...  4.61 us
    dot_general x1, matrix products, per_device(): jnp.dot(arrived.reshape(slot_count, width), w_qkv, preferred_element_type...  4.58 us
  transfers between devices with their start and end apart: 2, of which 2 were waited for; matrix products, arithmetic and copies ran while one was open for 2% of the time, Pallas kernels for 0%

profile of v17, /device:TPU:0, one launch (start us, length us, event | category | flops | bytes accessed | tf_op | source)
XLA Modules:
  0.0 110.8 jit_solution(7804177283934844123)
XLA Ops:
  0.0 0.0 copy-start
  0.0 0.0 copy-start.3
  0.0 0.0 copy-start.4
  0.0 0.7 fusion.14
  0.7 0.1 fusion.10
  0.8 0.2 reduce_window_sum.22
  1.0 0.2 select_reduce_fusion.1
  1.2 0.7 fusion.13
  1.8 1.3 %convolution_convert_fusion.1 = bf16[256,1024]{1,0:T(8,128)(2,1)S(1)} fusion(bf16[128,1024]{1,0:T(8,128)(2,1)} %param.14, s32[128]{0:T(128)S(1)} %fusion.13), kind=kOutput, calls=%fused_computation.1 | convolution fusion | flops 67403776 | bytes 786944 | tf_op jit(solution)/shard_map/tr,td->rd/dot_general | solution.py:330
  3.2 1.0 reshape.238
  4.2 11.1 %all-to-all-start = ((bf16[128,2,1024]{2,1,0:T(2,128)(2,1)}), bf16[128,2,1024]{2,1,0:T(2,128)(2,1)S(1)}, u32[]{:S(2)}, u32[]{:S(2)}) async-start(bf16[128,2,1024]{2,1,0:T(2,128)(2,1)} %reshape.238), calls=%async_computation | async-start | bytes 1048576 | tf_op jit(solution)/shard_map/all_to_all | solution.py:333
  15.3 0.0 copy-done.3
  15.3 0.1 compare_convert_fusion
  15.4 0.1 copy.35
  15.5 0.2 reduce_window_sum.23
  15.7 0.1 copy.36
  15.8 0.0 copy-done.4
  15.8 0.2 select_reduce_fusion
  16.0 0.1 copy.38
  16.1 0.1 copy.40
  16.2 0.1 add.101
  16.3 0.1 reduce_sum.66.rfill_ref
  16.4 0.0 copy-done
  16.4 0.1 broadcast_bitcast_fusion
  16.5 0.1 copy.37
  16.6 0.1 copy.42
  16.7 0.1 select_n.83.ntag_ref
  16.9 0.1 copy.43
  17.0 0.1 select_n.85.nrow_ref
  17.1 0.1 reshape_reshape.3.rreq_ref
  17.3 11.8 %all-to-all-done = bf16[128,2,1024]{2,1,0:T(2,128)(2,1)S(1)} async-done(((bf16[128,2,1024]{2,1,0:T(2,128)(2,1)}), bf16[128,2,1024]{2,1,0:T(2,128)(2,1)S(1)}, u32[]{:S(2)}, u32[]{:S(2)}) %all-to-all-start) | async-done | bytes 524320 | tf_op jit(solution)/shard_map/all_to_all | solution.py:333
  29.0 0.2 reshape.239
  29.3 4.6 %convolution_convert_fusion.q_ref.kn_ref.vn_ref = bf16[256,3072]{1,0:T(8,128)(2,1)S(1)} fusion(bf16[256,1024]{1,0:T(8,128)(2,1)S(1)} %reshape.239, bf16[1024,3072]{1,0:T(8,128)(2,1)} %param.20), kind=kOutput, calls=%fused_computation | convolution fusion | flops 1611399168 | bytes 8388608 | tf_op jit(solution)/shard_map/dot_general | solution.py:340
  33.8 0.0 copy-start.1
  33.9 0.0 copy-start.2
  33.9 19.1 %shard_map.136 = bf16[256,1024]{1,0:T(8,128)(2,1)S(1)} custom-call(bf16[256,3072]{1,0:T(8,128)(2,1)S(1)} %convolution_convert_fusion.q_ref.kn_ref.vn_ref, bf16[256,3072]{1,0:T(8,128)(2,1)S(1)} %convolution_convert_fusion.q_ref.kn_ref.vn_ref, bf16[256,3072]{1,0:T(8,128)(2,1)S(1)} %convolution_convert_fusion.q_ref.kn_ref.vn_ref, bf16[2048,1024]{1,0:T(8,128)(2,1)} %bitcast.28, ...), custom_call_target="tpu_custom_call" | custom-call | tf_op jit(solution)/shard_map/pallas_call | solution.py:93
  52.9 1.0 reshape.243
  53.9 4.6 %all-to-all-start.1 = ((bf16[128,2,1024]{2,1,0:T(2,128)(2,1)}), bf16[128,2,1024]{2,1,0:T(2,128)(2,1)S(1)}, u32[]{:S(2)}, u32[]{:S(2)}) async-start(bf16[128,2,1024]{2,1,0:T(2,128)(2,1)} %reshape.243), calls=%async_computation.1 | async-start | bytes 1048576 | tf_op jit(solution)/shard_map/all_to_all | solution.py:347
  58.6 0.0 copy-start.5
  58.6 0.0 copy-start.6
  58.6 13.7 %all-to-all-done.1 = bf16[128,2,1024]{2,1,0:T(2,128)(2,1)S(1)} async-done(((bf16[128,2,1024]{2,1,0:T(2,128)(2,1)}), bf16[128,2,1024]{2,1,0:T(2,128)(2,1)S(1)}, u32[]{:S(2)}, u32[]{:S(2)}) %all-to-all-start.1) | async-done | bytes 524320 | tf_op jit(solution)/shard_map/all_to_all | solution.py:347
  72.3 0.0 copy-done.1
  72.3 0.0 copy-done.2
  72.3 1.4 %convolution_add_fusion.y_ref = f32[128,1024]{1,0:T(8,128)} fusion(bf16[1024,1024]{1,0:T(8,128)(2,1)S(1)} %copy-done.1, bf16[128,2,1024]{2,1,0:T(2,128)(2,1)S(1)} %all-to-all-done.1, bf16[128,1024]{1,0:T(8,128)(2,1)S(1)} %copy-done.2, s32[128,2]{0,1:T(2,128)S(1)} %multiply_add_fusion, s32[128]{0:T(128)S(1)} %fusion.13), kind=kOutput, calls=%fused_computation.3 | convolution fusion | flops 335970304 | bytes 3409408 | tf_op jit(solution)/shard_map/dot_general | solution.py:360
  73.7 32.8 %shard_map.137 = f32[128,1024]{1,0:T(8,128)} custom-call(f32[128,1024]{1,0:T(8,128)} %convolution_add_fusion.y_ref, f32[1,1024]{1,0:T(1,128)} %bitcast.34, f32[1,1024]{1,0:T(1,128)} %bitcast.35, bf16[1024,512]{1,0:T(8,128)(2,1)} %w1_hbm.1, bf16[512,1024]{1,0:T(8,128)(2,1)} %w2_hbm.1), custom_call_target="tpu_custom_call" | custom-call | tf_op jit(solution)/shard_map/pallas_call | solution.py:266
  106.5 1.2 %reduce_sum.64 = f32[128]{0:T(128)S(1)} reduce(f32[128,1024]{1,0:T(8,128)} %shard_map.137, f32[]{:T(128)} %constant.71.clone.1), dimensions={1}, to_apply=%region_6.7 | reduce | flops 130944 | bytes 524804 | tf_op jit(solution)/shard_map/reduce_sum | solution.py:15
  107.6 1.2 %multiply_reduce_fusion = f32[128]{0:T(128)S(1)} fusion(f32[128,1024]{1,0:T(8,128)} %shard_map.137, f32[128]{0:T(128)S(1)} %broadcast_multiply_fusion), kind=kLoop, calls=%fused_computation.7 | loop fusion | flops 393088 | bytes 525312 | tf_op jit(solution)/shard_map/reduce_sum | solution.py:16
  108.9 0.0 copy-done.5
  108.9 0.0 copy-done.6
  108.9 1.9 %add_convert_fusion = bf16[128,1024]{1,0:T(8,128)(2,1)} fusion(f32[128,1024]{1,0:T(8,128)} %shard_map.137, f32[1024]{0:T(1024)S(1)} %copy-done.5, f32[1024]{0:T(1024)S(1)} %copy-done.6, f32[128]{0:T(128)S(1)} %add_rsqrt_fusion, f32[128]{0:T(128)S(1)} %broadcast_multiply_fusion), kind=kLoop, calls=%fused_computation.6 | loop fusion | flops 655360 | bytes 795648 | tf_op jit(solution)/shard_map/convert_element_type | solution.py:364
  (9 shorter events, 0.1 us)
Async XLA Ops:
  0.0 16.4 %copy-start = (s32[4]{0:T(128)S(1)}, s32[4]{0:T(128)}, u32[]{:S(2)}) copy-start(s32[4]{0:T(128)} %param.17) | copy-start | bytes 52
  0.0 15.3 %copy-start.3 = (s32[16384,1]{0,1:T(1,128)S(1)}, s32[16384,1]{0,1:T(1,128)}, u32[]{:S(2)}) copy-start(s32[16384,1]{0,1:T(1,128)} %param.15) | copy-start | bytes 196612
  0.0 15.8 %copy-start.4 = (s32[16384]{0:T(1024)S(1)}, s32[16384]{0:T(1024)}, u32[]{:S(2)}) copy-start(s32[16384]{0:T(1024)} %param.16) | copy-start | bytes 196612
  4.2 24.9 %all-to-all-start = ((bf16[128,2,1024]{2,1,0:T(2,128)(2,1)}), bf16[128,2,1024]{2,1,0:T(2,128)(2,1)S(1)}, u32[]{:S(2)}, u32[]{:S(2)}) async-start(bf16[128,2,1024]{2,1,0:T(2,128)(2,1)} %reshape.238), calls=%async_computation | async-start | bytes 1048576 | tf_op jit(solution)/shard_map/all_to_all | solution.py:333
  33.8 38.4 %copy-start.1 = (bf16[1024,1024]{1,0:T(8,128)(2,1)S(1)}, bf16[1024,1024]{1,0:T(8,128)(2,1)}, u32[]{:S(2)}) copy-start(bf16[1024,1024]{1,0:T(8,128)(2,1)} %param.21) | copy-start | bytes 6291460
  33.9 38.4 %copy-start.2 = (bf16[128,1024]{1,0:T(8,128)(2,1)S(1)}, bf16[128,1024]{1,0:T(8,128)(2,1)}, u32[]{:S(2)}) copy-start(bf16[128,1024]{1,0:T(8,128)(2,1)} %param.14) | copy-start | bytes 786436
  53.9 18.3 %all-to-all-start.1 = ((bf16[128,2,1024]{2,1,0:T(2,128)(2,1)}), bf16[128,2,1024]{2,1,0:T(2,128)(2,1)S(1)}, u32[]{:S(2)}, u32[]{:S(2)}) async-start(bf16[128,2,1024]{2,1,0:T(2,128)(2,1)} %reshape.243), calls=%async_computation.1 | async-start | bytes 1048576 | tf_op jit(solution)/shard_map/all_to_all | solution.py:347
  58.6 50.3 %copy-start.5 = (f32[1024]{0:T(1024)S(1)}, f32[1024]{0:T(1024)}, u32[]{:S(2)}) copy-start(f32[1024]{0:T(1024)} %param.27) | copy-start | bytes 12292
  58.6 50.3 %copy-start.6 = (f32[1024]{0:T(1024)S(1)}, f32[1024]{0:T(1024)}, u32[]{:S(2)}) copy-start(f32[1024]{0:T(1024)} %param.26) | copy-start | bytes 12292

commit v18 on v16

--- a/solution.py
+++ b/solution.py
@@ -46,17 +46,22 @@
     key_new = kn_ref[...]
     value_new = vn_ref[...]
     row_request = rreq_ref[...]
-    old_mask = ctag_ref[...] == row_request
+    key_tag = ctag_ref[...]
     new_mask = (ntag_ref[...] == row_request) & (nrow_ref[...] <= rrow_ref[...])
     lane = lax.broadcasted_iota(jnp.int32, (1, q.shape[1]), 1)
     contract = (((1,), (1,)), ((), ()))
     result = None
     for half in range(2):
         in_head = (lane // head_dim) == half
+        slot = lane - (1 - half) * head_dim
+        spare = (slot >= 0) & (slot < 8)
         q_head = jnp.where(in_head, q, jnp.zeros_like(q))
-        old_score = lax.dot_general(q_head, keys, contract, preferred_element_type=jnp.float32)
+        q_bias = jnp.where(spare & (row_request == slot), jnp.ones_like(q), q_head)
+        key_bias = jnp.where(key_tag == slot, jnp.float32(0.0), jnp.float32(-1e30)).astype(keys.dtype)
+        keys_bias = jnp.where(spare, key_bias, keys)
+        old_score = lax.dot_general(q_bias, keys_bias, contract, preferred_element_type=jnp.float32)
         new_score = lax.dot_general(q_head, key_new, contract, preferred_element_type=jnp.float32)
-        old_exp = jnp.where(old_mask, jnp.exp(old_score), jnp.float32(0.0))
+        old_exp = jnp.exp(old_score)
         new_exp = jnp.where(new_mask, jnp.exp(new_score), jnp.float32(0.0))
         total = jnp.sum(old_exp, axis=1, keepdims=True) + jnp.sum(new_exp, axis=1, keepdims=True)
         total = jnp.where(total > 0, total, jnp.float32(1.0))
@@ -82,7 +87,7 @@
     key_owner = jnp.arange(requests * context, dtype=jnp.int32) // context
     key_place = jnp.arange(requests * context, dtype=jnp.int32) % context
     key_limit = jnp.repeat(lengths, context)
-    column_tag = jnp.where(key_place < key_limit, key_owner, -1).reshape(1, -1)
+    column_tag = jnp.where(key_place < key_limit, key_owner, -1).reshape(-1, 1)
     new_tag = jnp.where(filled > 0, slot_request, -1).reshape(1, -1)
     new_row = global_row.reshape(1, -1)
     row_request = slot_request.reshape(-1, 1)
@@ -102,7 +107,7 @@
             whole((slot_count, 1)),
             whole((slot_count, 1)),
             whole((slot_count, 1)),
-            whole((1, keyed)),
+            whole((keyed, 1)),
             whole((1, slot_count)),
             whole((1, slot_count)),
         ],

time: 108 us -> 113 us (1.046)
  local copies, waits for them, and re-layouts: 6.83 us -> 11.9 us
  waiting for transfers between devices: 25.5 us -> 22.3 us
  other arithmetic: 2.75 us -> 4.13 us
    all_to_all x1, waiting for transfers between devices: 11.8 us -> 8.61 us  [per_device(): lax.all_to_all(outgoing.reshape(devices, capacity, width), ('req', 'mlp')...]
    unnamed x28 -> x25, local copies, waits for them, and re-layouts: 2.58 us -> 4.71 us
    reshape x1, local copies, waits for them, and re-layouts: 0.2 us -> 2.03 us  [per_device(): arrived.reshape(slot_count, width)]
    select_n x1, other arithmetic: 0.02 us -> 1.4 us  [attend(): column_tag = jnp.where(key_place < key_limit, key_owner, -1).reshape(-1, 1)]
  transfers between devices with their start and end apart: 2 -> 2, of which waited for: 2 -> 2; matrix products, arithmetic and copies ran while one was open for 2% -> 4% of each run, Pallas kernels for 0% -> 0%
where the time goes in v18:
time: 113 us; the launch traced here: 112 us
  Pallas kernels  49.6 us (44%)
  waiting for transfers between devices  22.3 us (20%)
  starting transfers between devices  16.3 us (14%)
  local copies, waits for them, and re-layouts  11.9 us (11%)
  matrix products  7.68 us (7%)
  other arithmetic  4.13 us (4%)
    pallas_call x1, Pallas kernels, feed_forward_block(): pl.pallas_call(block_kernel, in_specs=[pl.BlockSpec(memory_space=pltpu.VM...  30.8 us
    pallas_call x1, Pallas kernels, attend(): pl.pallas_call(attention_kernel, grid=(pairs,), in_specs=[pl.BlockSpec((s...  18.8 us
    all_to_all x1, waiting for transfers between devices, per_device(): lax.all_to_all(attended.reshape(devices, capacity, width), ('req', 'mlp')...  13.7 us
    all_to_all x1, starting transfers between devices, per_device(): lax.all_to_all(outgoing.reshape(devices, capacity, width), ('req', 'mlp')...  11.7 us
    all_to_all x1, waiting for transfers between devices, per_device(): lax.all_to_all(outgoing.reshape(devices, capacity, width), ('req', 'mlp')...  8.61 us
    dot_general x1, matrix products, per_device(): jnp.dot(arrived.reshape(slot_count, width), w_qkv, preferred_element_type...  4.76 us
    unnamed x25, local copies, waits for them, and re-layouts  4.71 us
    all_to_all x1, starting transfers between devices, per_device(): lax.all_to_all(attended.reshape(devices, capacity, width), ('req', 'mlp')...  4.61 us
  transfers between devices with their start and end apart: 2, of which 2 were waited for; matrix products, arithmetic and copies ran while one was open for 4% of the time, Pallas kernels for 0%

profile of v18, /device:TPU:0, one launch (start us, length us, event | category | flops | bytes accessed | tf_op | source)
XLA Modules:
  0.0 112.2 jit_solution(11593179414318505907)
XLA Ops:
  0.0 0.0 copy-start
  0.0 0.0 copy-start.6
  0.0 0.0 copy-start.7
  0.0 0.0 copy-start.10
  0.0 0.8 fusion.21
  0.8 0.1 fusion.17
  0.9 0.2 reduce_window_sum.22
  1.1 0.2 select_reduce_fusion.1
  1.3 0.7 fusion.20
  1.9 1.3 %convolution_convert_fusion.1 = bf16[256,1024]{1,0:T(8,128)(2,1)S(1)} fusion(bf16[128,1024]{1,0:T(8,128)(2,1)} %param.14, s32[128]{0:T(128)S(1)} %fusion.20), kind=kOutput, calls=%fused_computation.5 | convolution fusion | flops 67403776 | bytes 786944 | tf_op jit(solution)/shard_map/tr,td->rd/dot_general | solution.py:326
  3.3 1.0 reshape.238
  4.3 11.7 %all-to-all-start = ((bf16[128,2,1024]{2,1,0:T(2,128)(2,1)}), bf16[128,2,1024]{2,1,0:T(2,128)(2,1)}, u32[]{:S(2)}, u32[]{:S(2)}) async-start(bf16[128,2,1024]{2,1,0:T(2,128)(2,1)} %reshape.238), calls=%async_computation | async-start | bytes 1048576 | tf_op jit(solution)/shard_map/all_to_all | solution.py:329
  16.0 0.0 copy-done.6
  16.0 0.1 compare_convert_fusion
  16.1 0.1 copy.37
  16.2 0.2 reduce_window_sum.23
  16.4 0.1 copy.38
  16.5 0.0 copy-done.7
  16.5 0.2 select_reduce_fusion
  16.7 0.1 copy.40
  16.8 0.1 copy.42
  16.9 0.1 add.101
  17.0 0.1 reduce_sum.66.rfill_ref
  17.1 0.0 copy-done.10
  17.1 0.1 broadcast_bitcast_fusion
  17.2 0.1 copy.39
  17.3 0.1 copy.45
  17.4 0.1 select_n.83.ntag_ref
  17.5 0.1 copy.46
  17.7 0.1 select_n.85.nrow_ref
  17.8 0.1 reshape_reshape.3.rreq_ref
  17.9 1.4 %copy.51 = s32[1,2048]{0,1:T(8,128)} copy(s32[1,2048]{1,0:T(1,128)S(1)} %bitcast.39) | data formatting | bytes 16384
  19.3 1.4 %fusion.3.ctag_ref = s32[2048,1]{1,0:T(8,128)S(1)} fusion(s32[1,2048]{0,1:T(8,128)} %copy.51), kind=kLoop, calls=%fused_computation.11 | loop fusion | flops 28672 | bytes 16384 | tf_op jit(solution)/shard_map/jit(_where)/select_n | solution.py:90
  20.7 8.6 %all-to-all-done = bf16[128,2,1024]{2,1,0:T(2,128)(2,1)} async-done(((bf16[128,2,1024]{2,1,0:T(2,128)(2,1)}), bf16[128,2,1024]{2,1,0:T(2,128)(2,1)}, u32[]{:S(2)}, u32[]{:S(2)}) %all-to-all-start) | async-done | bytes 524320 | tf_op jit(solution)/shard_map/all_to_all | solution.py:329
  29.3 2.0 %reshape.239 = bf16[256,1024]{1,0:T(8,128)(2,1)} reshape(bf16[128,2,1024]{2,1,0:T(2,128)(2,1)} %all-to-all-done) | data formatting | bytes 1048576 | tf_op jit(solution)/shard_map/reshape | solution.py:337
  31.3 4.8 %convolution_convert_fusion.q_ref.kn_ref.vn_ref = bf16[256,3072]{1,0:T(8,128)(2,1)S(1)} fusion(bf16[256,1024]{1,0:T(8,128)(2,1)} %reshape.239, bf16[1024,3072]{1,0:T(8,128)(2,1)} %param.20), kind=kOutput, calls=%fused_computation | convolution fusion | flops 1611399168 | bytes 8388608 | tf_op jit(solution)/shard_map/dot_general | solution.py:336
  36.1 18.8 %shard_map.136 = bf16[256,1024]{1,0:T(8,128)(2,1)S(1)} custom-call(bf16[256,3072]{1,0:T(8,128)(2,1)S(1)} %convolution_convert_fusion.q_ref.kn_ref.vn_ref, bf16[256,3072]{1,0:T(8,128)(2,1)S(1)} %convolution_convert_fusion.q_ref.kn_ref.vn_ref, bf16[256,3072]{1,0:T(8,128)(2,1)S(1)} %convolution_convert_fusion.q_ref.kn_ref.vn_ref, bf16[2048,1024]{1,0:T(8,128)(2,1)} %bitcast.34, ...), custom_call_target="tpu_custom_call" | custom-call | tf_op jit(solution)/shard_map/pallas_call | solution.py:98
  54.9 0.0 copy-start.1
  54.9 0.8 copy-done.1
  55.7 0.0 copy-start.4
  55.7 0.0 copy-start.5
  55.7 2.1 %reshape.243 = bf16[128,2,1024]{2,1,0:T(2,128)(2,1)} reshape(bf16[256,1024]{1,0:T(8,128)(2,1)} %copy-done.1) | data formatting | bytes 1048576 | tf_op jit(solution)/shard_map/reshape | solution.py:344
  57.8 4.6 %all-to-all-start.1 = ((bf16[128,2,1024]{2,1,0:T(2,128)(2,1)}), bf16[128,2,1024]{2,1,0:T(2,128)(2,1)S(1)}, u32[]{:S(2)}, u32[]{:S(2)}) async-start(bf16[128,2,1024]{2,1,0:T(2,128)(2,1)} %reshape.243), calls=%async_computation.1 | async-start | bytes 1048576 | tf_op jit(solution)/shard_map/all_to_all | solution.py:343
  62.4 0.0 copy-start.8
  62.4 0.0 copy-start.9
  62.4 13.7 %all-to-all-done.1 = bf16[128,2,1024]{2,1,0:T(2,128)(2,1)S(1)} async-done(((bf16[128,2,1024]{2,1,0:T(2,128)(2,1)}), bf16[128,2,1024]{2,1,0:T(2,128)(2,1)S(1)}, u32[]{:S(2)}, u32[]{:S(2)}) %all-to-all-start.1) | async-done | bytes 524320 | tf_op jit(solution)/shard_map/all_to_all | solution.py:343
  76.1 0.0 copy-done
  76.1 1.6 %convolution_add_fusion.y_ref = f32[128,1024]{1,0:T(8,128)S(1)} fusion(bf16[1024,1024]{1,0:T(8,128)(2,1)S(1)} %copy-done, bf16[128,2,1024]{2,1,0:T(2,128)(2,1)S(1)} %all-to-all-done.1, bf16[128,1024]{1,0:T(8,128)(2,1)} %param.14, s32[128,2]{0,1:T(2,128)S(1)} %multiply_add_fusion, s32[128]{0:T(128)S(1)} %fusion.20), kind=kOutput, calls=%fused_computation.7 | convolution fusion | flops 335970304 | bytes 3409408 | tf_op jit(solution)/shard_map/dot_general | solution.py:356
  77.7 0.0 copy-done.4
  77.7 0.0 copy-done.5
  77.7 0.0 copy-start.2
  77.7 1.2 %copy-done.2 = bf16[1024,512]{1,0:T(8,128)(2,1)S(1)} copy-done((bf16[1024,512]{1,0:T(8,128)(2,1)S(1)}, bf16[1024,512]{1,0:T(8,128)(2,1)}, u32[]{:S(2)}) %copy-start.2) | copy-done | bytes 1048600
  79.0 0.0 copy-start.3
  79.0 1.2 %copy-done.3 = bf16[512,1024]{1,0:T(8,128)(2,1)S(1)} copy-done((bf16[512,1024]{1,0:T(8,128)(2,1)S(1)}, bf16[512,1024]{1,0:T(8,128)(2,1)}, u32[]{:S(2)}) %copy-start.3) | copy-done | bytes 1048600
  80.2 30.8 %shard_map.137 = f32[128,1024]{1,0:T(8,128)S(1)} custom-call(f32[128,1024]{1,0:T(8,128)S(1)} %convolution_add_fusion.y_ref, f32[1,1024]{1,0:T(1,128)S(1)} %bitcast.32, f32[1,1024]{1,0:T(1,128)S(1)} %bitcast.33, bf16[1024,512]{1,0:T(8,128)(2,1)S(1)} %copy-done.2, bf16[512,1024]{1,0:T(8,128)(2,1)S(1)} %copy-done.3), custom_call_target="tpu_custom_call" | custom-call | tf_op jit(solution)/shard_map/pallas_call | solution.py:265
  111.0 0.1 reduce_sum.64
  111.1 0.2 multiply_reduce_fusion
  111.3 0.0 copy-done.8
  111.3 0.0 copy-done.9
  111.4 0.9 add_convert_fusion
  (8 shorter events, 0.1 us)
Async XLA Ops:
  0.0 76.1 %copy-start = (bf16[1024,1024]{1,0:T(8,128)(2,1)S(1)}, bf16[1024,1024]{1,0:T(8,128)(2,1)}, u32[]{:S(2)}) copy-start(bf16[1024,1024]{1,0:T(8,128)(2,1)} %param.21) | copy-start | bytes 6291460
  0.0 16.0 %copy-start.6 = (s32[16384,1]{0,1:T(1,128)S(1)}, s32[16384,1]{0,1:T(1,128)}, u32[]{:S(2)}) copy-start(s32[16384,1]{0,1:T(1,128)} %param.15) | copy-start | bytes 196612
  0.0 16.5 %copy-start.7 = (s32[16384]{0:T(1024)S(1)}, s32[16384]{0:T(1024)}, u32[]{:S(2)}) copy-start(s32[16384]{0:T(1024)} %param.16) | copy-start | bytes 196612
  0.0 17.1 %copy-start.10 = (s32[4]{0:T(128)S(1)}, s32[4]{0:T(128)}, u32[]{:S(2)}) copy-start(s32[4]{0:T(128)} %param.17) | copy-start | bytes 52
  4.3 25.0 %all-to-all-start = ((bf16[128,2,1024]{2,1,0:T(2,128)(2,1)}), bf16[128,2,1024]{2,1,0:T(2,128)(2,1)}, u32[]{:S(2)}, u32[]{:S(2)}) async-start(bf16[128,2,1024]{2,1,0:T(2,128)(2,1)} %reshape.238), calls=%async_computation | async-start | bytes 1048576 | tf_op jit(solution)/shard_map/all_to_all | solution.py:329
  54.9 0.8 copy-start.1
  55.7 22.0 %copy-start.4 = (f32[1024]{0:T(1024)S(1)}, f32[1024]{0:T(1024)}, u32[]{:S(2)}) copy-start(f32[1024]{0:T(1024)} %param.24) | copy-start | bytes 12292
  55.7 22.0 %copy-start.5 = (f32[1024]{0:T(1024)S(1)}, f32[1024]{0:T(1024)}, u32[]{:S(2)}) copy-start(f32[1024]{0:T(1024)} %param.25) | copy-start | bytes 12292
  57.8 18.3 %all-to-all-start.1 = ((bf16[128,2,1024]{2,1,0:T(2,128)(2,1)}), bf16[128,2,1024]{2,1,0:T(2,128)(2,1)S(1)}, u32[]{:S(2)}, u32[]{:S(2)}) async-start(bf16[128,2,1024]{2,1,0:T(2,128)(2,1)} %reshape.243), calls=%async_computation.1 | async-start | bytes 1048576 | tf_op jit(solution)/shard_map/all_to_all | solution.py:343
  62.4 48.9 %copy-start.8 = (f32[1024]{0:T(1024)S(1)}, f32[1024]{0:T(1024)}, u32[]{:S(2)}) copy-start(f32[1024]{0:T(1024)} %param.27) | copy-start | bytes 12292
  62.4 48.9 %copy-start.9 = (f32[1024]{0:T(1024)S(1)}, f32[1024]{0:T(1024)}, u32[]{:S(2)}) copy-start(f32[1024]{0:T(1024)} %param.26) | copy-start | bytes 12292
  77.7 1.2 %copy-start.2 = (bf16[1024,512]{1,0:T(8,128)(2,1)S(1)}, bf16[1024,512]{1,0:T(8,128)(2,1)}, u32[]{:S(2)}) copy-start(bf16[1024,512]{1,0:T(8,128)(2,1)} %w1_ref.1) | copy-start | bytes 3145732
  79.0 1.2 %copy-start.3 = (bf16[512,1024]{1,0:T(8,128)(2,1)S(1)}, bf16[512,1024]{1,0:T(8,128)(2,1)}, u32[]{:S(2)}) copy-start(bf16[512,1024]{1,0:T(8,128)(2,1)} %w2_ref.1) | copy-start | bytes 3145732

commit v19 on v17

--- a/solution.py
+++ b/solution.py
@@ -288,7 +288,7 @@
             pltpu.SemaphoreType.DMA((3,)),
         ],
         compiler_params=pltpu.CompilerParams(
-            collective_id=2, has_side_effects=True, vmem_limit_bytes=62 * 1024 * 1024
+            collective_id=2, has_side_effects=True, vmem_limit_bytes=53 * 1024 * 1024
         ),
     )(block, gain.reshape(1, -1), shift.reshape(1, -1), w_fc1, w_fc2)
 

time: 111 us -> 107 us (0.964)
  other arithmetic: 5.87 us -> 2.75 us
where the time goes in v19:
time: 107 us
  Pallas kernels  50.8 us (47%)
  waiting for transfers between devices  25.5 us (24%)
  starting transfers between devices  15.8 us (15%)
  matrix products  7.35 us (7%)
  local copies, waits for them, and re-layouts  4.39 us (4%)
  other arithmetic  2.75 us (3%)
    pallas_call x1, Pallas kernels, feed_forward_block(): pl.pallas_call(block_kernel, in_specs=[pl.BlockSpec(memory_space=pltpu.VM...  31.9 us
    pallas_call x1, Pallas kernels, attend(): pl.pallas_call(attention_kernel, grid=(pairs,), in_specs=[pl.BlockSpec((s...  18.9 us
    all_to_all x1, waiting for transfers between devices, per_device(): lax.all_to_all(attended.reshape(devices, capacity, width), ('req', 'mlp')...  13.7 us
    all_to_all x1, waiting for transfers between devices, per_device(): lax.all_to_all(outgoing.reshape(devices, capacity, width), ('req', 'mlp')...  11.8 us
    all_to_all x1, starting transfers between devices, per_device(): lax.all_to_all(outgoing.reshape(devices, capacity, width), ('req', 'mlp')...  11.2 us
    all_to_all x1, starting transfers between devices, per_device(): lax.all_to_all(attended.reshape(devices, capacity, width), ('req', 'mlp')...  4.61 us
    dot_general x1, matrix products, per_device(): jnp.dot(arrived.reshape(slot_count, width), w_qkv, preferred_element_type...  4.58 us
  transfers between devices with their start and end apart: 2, of which 2 were waited for; matrix products, arithmetic and copies ran while one was open for 2% of the time, Pallas kernels for 0%

profile of v19, /device:TPU:0, one launch (start us, length us, event | category | flops | bytes accessed | tf_op | source)
XLA Modules:
  0.0 106.8 jit_solution(10189675500188857245)
XLA Ops:
  0.0 0.0 copy-start
  0.0 0.0 copy-start.4
  0.0 0.0 copy-start.5
  0.0 0.0 copy-start.10
  0.0 0.8 fusion.14
  0.8 0.1 fusion.10
  0.9 0.2 reduce_window_sum.22
  1.1 0.2 select_reduce_fusion.1
  1.3 0.7 fusion.13
  1.9 0.0 copy-start.6
  1.9 1.3 %convolution_convert_fusion.1 = bf16[256,1024]{1,0:T(8,128)(2,1)S(1)} fusion(bf16[128,1024]{1,0:T(8,128)(2,1)} %param.14, s32[128]{0:T(128)S(1)} %fusion.13), kind=kOutput, calls=%fused_computation.1 | convolution fusion | flops 67403776 | bytes 786944 | tf_op jit(solution)/shard_map/tr,td->rd/dot_general | solution.py:330
  3.3 1.0 reshape.238
  4.3 0.0 copy-done.6
  4.3 11.2 %all-to-all-start = ((bf16[128,2,1024]{2,1,0:T(2,128)(2,1)}), bf16[128,2,1024]{2,1,0:T(2,128)(2,1)S(1)}, u32[]{:S(2)}, u32[]{:S(2)}) async-start(bf16[128,2,1024]{2,1,0:T(2,128)(2,1)} %reshape.238), calls=%async_computation | async-start | bytes 1048576 | tf_op jit(solution)/shard_map/all_to_all | solution.py:333
  15.4 0.0 copy-done.4
  15.5 0.1 compare_convert_fusion
  15.5 0.1 copy.35
  15.6 0.2 reduce_window_sum.23
  15.8 0.1 copy.36
  15.9 0.0 copy-done.5
  15.9 0.2 select_reduce_fusion
  16.1 0.1 copy.38
  16.2 0.1 copy.40
  16.3 0.1 add.101
  16.4 0.1 reduce_sum.66.rfill_ref
  16.5 0.0 copy-done.10
  16.6 0.1 broadcast_bitcast_fusion
  16.6 0.1 copy.37
  16.7 0.1 copy.42
  16.9 0.1 select_n.83.ntag_ref
  17.0 0.1 copy.43
  17.1 0.1 select_n.85.nrow_ref
  17.3 0.1 reshape_reshape.3.rreq_ref
  17.4 11.8 %all-to-all-done = bf16[128,2,1024]{2,1,0:T(2,128)(2,1)S(1)} async-done(((bf16[128,2,1024]{2,1,0:T(2,128)(2,1)}), bf16[128,2,1024]{2,1,0:T(2,128)(2,1)S(1)}, u32[]{:S(2)}, u32[]{:S(2)}) %all-to-all-start) | async-done | bytes 524320 | tf_op jit(solution)/shard_map/all_to_all | solution.py:333
  29.2 0.2 reshape.239
  29.4 4.6 %convolution_convert_fusion.q_ref.kn_ref.vn_ref = bf16[256,3072]{1,0:T(8,128)(2,1)S(1)} fusion(bf16[256,1024]{1,0:T(8,128)(2,1)S(1)} %reshape.239, bf16[1024,3072]{1,0:T(8,128)(2,1)} %param.20), kind=kOutput, calls=%fused_computation | convolution fusion | flops 1611399168 | bytes 8388608 | tf_op jit(solution)/shard_map/dot_general | solution.py:340
  34.0 0.0 copy-start.3
  34.0 0.0 copy-start.7
  34.0 18.9 %shard_map.136 = bf16[256,1024]{1,0:T(8,128)(2,1)S(1)} custom-call(bf16[256,3072]{1,0:T(8,128)(2,1)S(1)} %convolution_convert_fusion.q_ref.kn_ref.vn_ref, bf16[256,3072]{1,0:T(8,128)(2,1)S(1)} %convolution_convert_fusion.q_ref.kn_ref.vn_ref, bf16[256,3072]{1,0:T(8,128)(2,1)S(1)} %convolution_convert_fusion.q_ref.kn_ref.vn_ref, bf16[2048,1024]{1,0:T(8,128)(2,1)} %bitcast.30, ...), custom_call_target="tpu_custom_call" | custom-call | tf_op jit(solution)/shard_map/pallas_call | solution.py:93
  52.9 0.0 copy-start.1
  52.9 0.0 copy-start.2
  52.9 1.0 reshape.243
  53.9 4.6 %all-to-all-start.1 = ((bf16[128,2,1024]{2,1,0:T(2,128)(2,1)}), bf16[128,2,1024]{2,1,0:T(2,128)(2,1)S(1)}, u32[]{:S(2)}, u32[]{:S(2)}) async-start(bf16[128,2,1024]{2,1,0:T(2,128)(2,1)} %reshape.243), calls=%async_computation.1 | async-start | bytes 1048576 | tf_op jit(solution)/shard_map/all_to_all | solution.py:347
  58.6 0.0 copy-start.8
  58.6 0.0 copy-start.9
  58.6 13.7 %all-to-all-done.1 = bf16[128,2,1024]{2,1,0:T(2,128)(2,1)S(1)} async-done(((bf16[128,2,1024]{2,1,0:T(2,128)(2,1)}), bf16[128,2,1024]{2,1,0:T(2,128)(2,1)S(1)}, u32[]{:S(2)}, u32[]{:S(2)}) %all-to-all-start.1) | async-done | bytes 524320 | tf_op jit(solution)/shard_map/all_to_all | solution.py:347
  72.3 0.0 copy-done
  72.3 0.0 copy-done.3
  72.3 0.0 copy-done.7
  72.3 1.4 %convolution_add_fusion.y_ref = f32[128,1024]{1,0:T(8,128)} fusion(bf16[1024,1024]{1,0:T(8,128)(2,1)S(1)} %copy-done, bf16[128,2,1024]{2,1,0:T(2,128)(2,1)S(1)} %all-to-all-done.1, bf16[128,1024]{1,0:T(8,128)(2,1)S(1)} %copy-done.3, s32[128,2]{0,1:T(2,128)S(1)} %multiply_add_fusion, s32[128]{0:T(128)S(1)} %copy-done.7), kind=kOutput, calls=%fused_computation.3 | convolution fusion | flops 335970304 | bytes 3409408 | tf_op jit(solution)/shard_map/dot_general | solution.py:360
  73.7 0.0 copy-done.1
  73.7 0.0 copy-done.2
  73.7 31.9 %shard_map.137 = f32[128,1024]{1,0:T(8,128)S(1)} custom-call(f32[128,1024]{1,0:T(8,128)} %convolution_add_fusion.y_ref, f32[1,1024]{1,0:T(1,128)S(1)} %bitcast.28, f32[1,1024]{1,0:T(1,128)S(1)} %bitcast.29, bf16[1024,512]{1,0:T(8,128)(2,1)} %w1_hbm.1, bf16[512,1024]{1,0:T(8,128)(2,1)} %w2_hbm.1), custom_call_target="tpu_custom_call" | custom-call | tf_op jit(solution)/shard_map/pallas_call | solution.py:266
  105.6 0.1 reduce_sum.64
  105.7 0.2 multiply_reduce_fusion
  106.0 0.0 copy-done.8
  106.0 0.0 copy-done.9
  106.0 0.9 add_convert_fusion
  (9 shorter events, 0.1 us)
Async XLA Ops:
  0.0 72.3 %copy-start = (bf16[1024,1024]{1,0:T(8,128)(2,1)S(1)}, bf16[1024,1024]{1,0:T(8,128)(2,1)}, u32[]{:S(2)}) copy-start(bf16[1024,1024]{1,0:T(8,128)(2,1)} %param.21) | copy-start | bytes 6291460
  0.0 15.4 %copy-start.4 = (s32[16384,1]{0,1:T(1,128)S(1)}, s32[16384,1]{0,1:T(1,128)}, u32[]{:S(2)}) copy-start(s32[16384,1]{0,1:T(1,128)} %param.15) | copy-start | bytes 196612
  0.0 15.9 %copy-start.5 = (s32[16384]{0:T(1024)S(1)}, s32[16384]{0:T(1024)}, u32[]{:S(2)}) copy-start(s32[16384]{0:T(1024)} %param.16) | copy-start | bytes 196612
  0.0 16.5 %copy-start.10 = (s32[4]{0:T(128)S(1)}, s32[4]{0:T(128)}, u32[]{:S(2)}) copy-start(s32[4]{0:T(128)} %param.17) | copy-start | bytes 52
  1.9 2.4 %copy-start.6 = (s32[128]{0:T(128)}, s32[128]{0:T(128)S(1)}, u32[]{:S(2)}) copy-start(s32[128]{0:T(128)S(1)} %fusion.13) | copy-start | bytes 1540
  4.3 24.9 %all-to-all-start = ((bf16[128,2,1024]{2,1,0:T(2,128)(2,1)}), bf16[128,2,1024]{2,1,0:T(2,128)(2,1)S(1)}, u32[]{:S(2)}, u32[]{:S(2)}) async-start(bf16[128,2,1024]{2,1,0:T(2,128)(2,1)} %reshape.238), calls=%async_computation | async-start | bytes 1048576 | tf_op jit(solution)/shard_map/all_to_all | solution.py:333
  34.0 38.3 %copy-start.3 = (bf16[128,1024]{1,0:T(8,128)(2,1)S(1)}, bf16[128,1024]{1,0:T(8,128)(2,1)}, u32[]{:S(2)}) copy-start(bf16[128,1024]{1,0:T(8,128)(2,1)} %param.14) | copy-start | bytes 786436
  34.0 38.3 %copy-start.7 = (s32[128]{0:T(128)S(1)}, s32[128]{0:T(128)}, u32[]{:S(2)}) copy-start(s32[128]{0:T(128)} %copy-done.6) | copy-start | bytes 1540
  52.9 20.8 %copy-start.1 = (f32[1024]{0:T(1024)S(1)}, f32[1024]{0:T(1024)}, u32[]{:S(2)}) copy-start(f32[1024]{0:T(1024)} %param.24) | copy-start | bytes 12292
  52.9 20.8 %copy-start.2 = (f32[1024]{0:T(1024)S(1)}, f32[1024]{0:T(1024)}, u32[]{:S(2)}) copy-start(f32[1024]{0:T(1024)} %param.25) | copy-start | bytes 12292
  53.9 18.3 %all-to-all-start.1 = ((bf16[128,2,1024]{2,1,0:T(2,128)(2,1)}), bf16[128,2,1024]{2,1,0:T(2,128)(2,1)S(1)}, u32[]{:S(2)}, u32[]{:S(2)}) async-start(bf16[128,2,1024]{2,1,0:T(2,128)(2,1)} %reshape.243), calls=%async_computation.1 | async-start | bytes 1048576 | tf_op jit(solution)/shard_map/all_to_all | solution.py:347
  58.6 47.4 %copy-start.8 = (f32[1024]{0:T(1024)S(1)}, f32[1024]{0:T(1024)}, u32[]{:S(2)}) copy-start(f32[1024]{0:T(1024)} %param.27) | copy-start | bytes 12292
  58.6 47.4 %copy-start.9 = (f32[1024]{0:T(1024)S(1)}, f32[1024]{0:T(1024)}, u32[]{:S(2)}) copy-start(f32[1024]{0:T(1024)} %param.26) | copy-start | bytes 12292

commit v20 on v19

--- a/solution.py
+++ b/solution.py
@@ -288,7 +288,7 @@
             pltpu.SemaphoreType.DMA((3,)),
         ],
         compiler_params=pltpu.CompilerParams(
-            collective_id=2, has_side_effects=True, vmem_limit_bytes=53 * 1024 * 1024
+            collective_id=2, has_side_effects=True, vmem_limit_bytes=52 * 1024 * 1024
         ),
     )(block, gain.reshape(1, -1), shift.reshape(1, -1), w_fc1, w_fc2)
 

time: 107 us -> 105 us (0.981)
  no operation moved by 1% of the time
where the time goes in v20:
time: 105 us
  Pallas kernels  49.8 us (47%)
  waiting for transfers between devices  25.5 us (24%)
  starting transfers between devices  15.8 us (15%)
  matrix products  6.56 us (6%)
  local copies, waits for them, and re-layouts  4.39 us (4%)
  other arithmetic  2.75 us (3%)
    pallas_call x1, Pallas kernels, feed_forward_block(): pl.pallas_call(block_kernel, in_specs=[pl.BlockSpec(memory_space=pltpu.VM...  30.9 us
    pallas_call x1, Pallas kernels, attend(): pl.pallas_call(attention_kernel, grid=(pairs,), in_specs=[pl.BlockSpec((s...  19 us
    all_to_all x1, waiting for transfers between devices, per_device(): lax.all_to_all(attended.reshape(devices, capacity, width), ('req', 'mlp')...  13.7 us
    all_to_all x1, waiting for transfers between devices, per_device(): lax.all_to_all(outgoing.reshape(devices, capacity, width), ('req', 'mlp')...  11.8 us
    all_to_all x1, starting transfers between devices, per_device(): lax.all_to_all(outgoing.reshape(devices, capacity, width), ('req', 'mlp')...  11.2 us
    all_to_all x1, starting transfers between devices, per_device(): lax.all_to_all(attended.reshape(devices, capacity, width), ('req', 'mlp')...  4.61 us
    dot_general x1, matrix products, per_device(): jnp.dot(arrived.reshape(slot_count, width), w_qkv, preferred_element_type...  4.58 us
  transfers between devices with their start and end apart: 2, of which 2 were waited for; matrix products, arithmetic and copies ran while one was open for 2% of the time, Pallas kernels for 0%

profile of v20, /device:TPU:0, one launch (start us, length us, event | category | flops | bytes accessed | tf_op | source)
XLA Modules:
  0.0 105.1 jit_solution(5231532033458234880)
XLA Ops:
  0.0 0.0 copy-start
  0.0 0.0 copy-start.4
  0.0 0.0 copy-start.5
  0.0 0.0 copy-start.10
  0.0 0.8 fusion.14
  0.8 0.1 fusion.10
  0.9 0.2 reduce_window_sum.22
  1.1 0.2 select_reduce_fusion.1
  1.3 0.7 fusion.13
  1.9 0.0 copy-start.6
  1.9 1.3 %convolution_convert_fusion.1 = bf16[256,1024]{1,0:T(8,128)(2,1)S(1)} fusion(bf16[128,1024]{1,0:T(8,128)(2,1)} %param.14, s32[128]{0:T(128)S(1)} %fusion.13), kind=kOutput, calls=%fused_computation.1 | convolution fusion | flops 67403776 | bytes 786944 | tf_op jit(solution)/shard_map/tr,td->rd/dot_general | solution.py:330
  3.3 1.0 reshape.238
  4.3 0.0 copy-done.6
  4.3 11.2 %all-to-all-start = ((bf16[128,2,1024]{2,1,0:T(2,128)(2,1)}), bf16[128,2,1024]{2,1,0:T(2,128)(2,1)S(1)}, u32[]{:S(2)}, u32[]{:S(2)}) async-start(bf16[128,2,1024]{2,1,0:T(2,128)(2,1)} %reshape.238), calls=%async_computation | async-start | bytes 1048576 | tf_op jit(solution)/shard_map/all_to_all | solution.py:333
  15.4 0.0 copy-done.4
  15.5 0.1 compare_convert_fusion
  15.5 0.1 copy.35
  15.6 0.2 reduce_window_sum.23
  15.8 0.1 copy.36
  15.9 0.0 copy-done.5
  15.9 0.2 select_reduce_fusion
  16.1 0.1 copy.38
  16.2 0.1 copy.40
  16.3 0.1 add.101
  16.4 0.1 reduce_sum.66.rfill_ref
  16.5 0.0 copy-done.10
  16.6 0.1 broadcast_bitcast_fusion
  16.6 0.1 copy.37
  16.7 0.1 copy.42
  16.9 0.1 select_n.83.ntag_ref
  17.0 0.1 copy.43
  17.1 0.1 select_n.85.nrow_ref
  17.3 0.1 reshape_reshape.3.rreq_ref
  17.4 11.8 %all-to-all-done = bf16[128,2,1024]{2,1,0:T(2,128)(2,1)S(1)} async-done(((bf16[128,2,1024]{2,1,0:T(2,128)(2,1)}), bf16[128,2,1024]{2,1,0:T(2,128)(2,1)S(1)}, u32[]{:S(2)}, u32[]{:S(2)}) %all-to-all-start) | async-done | bytes 524320 | tf_op jit(solution)/shard_map/all_to_all | solution.py:333
  29.2 0.2 reshape.239
  29.4 4.6 %convolution_convert_fusion.q_ref.kn_ref.vn_ref = bf16[256,3072]{1,0:T(8,128)(2,1)S(1)} fusion(bf16[256,1024]{1,0:T(8,128)(2,1)S(1)} %reshape.239, bf16[1024,3072]{1,0:T(8,128)(2,1)} %param.20), kind=kOutput, calls=%fused_computation | convolution fusion | flops 1611399168 | bytes 8388608 | tf_op jit(solution)/shard_map/dot_general | solution.py:340
  33.9 0.0 copy-start.3
  34.0 0.0 copy-start.7
  34.0 19.0 %shard_map.136 = bf16[256,1024]{1,0:T(8,128)(2,1)S(1)} custom-call(bf16[256,3072]{1,0:T(8,128)(2,1)S(1)} %convolution_convert_fusion.q_ref.kn_ref.vn_ref, bf16[256,3072]{1,0:T(8,128)(2,1)S(1)} %convolution_convert_fusion.q_ref.kn_ref.vn_ref, bf16[256,3072]{1,0:T(8,128)(2,1)S(1)} %convolution_convert_fusion.q_ref.kn_ref.vn_ref, bf16[2048,1024]{1,0:T(8,128)(2,1)} %bitcast.30, ...), custom_call_target="tpu_custom_call" | custom-call | tf_op jit(solution)/shard_map/pallas_call | solution.py:93
  52.9 0.0 copy-start.1
  53.0 0.0 copy-start.2
  53.0 1.0 reshape.243
  54.0 4.6 %all-to-all-start.1 = ((bf16[128,2,1024]{2,1,0:T(2,128)(2,1)}), bf16[128,2,1024]{2,1,0:T(2,128)(2,1)S(1)}, u32[]{:S(2)}, u32[]{:S(2)}) async-start(bf16[128,2,1024]{2,1,0:T(2,128)(2,1)} %reshape.243), calls=%async_computation.1 | async-start | bytes 1048576 | tf_op jit(solution)/shard_map/all_to_all | solution.py:347
  58.6 0.0 copy-start.8
  58.6 0.0 copy-start.9
  58.6 13.7 %all-to-all-done.1 = bf16[128,2,1024]{2,1,0:T(2,128)(2,1)S(1)} async-done(((bf16[128,2,1024]{2,1,0:T(2,128)(2,1)}), bf16[128,2,1024]{2,1,0:T(2,128)(2,1)S(1)}, u32[]{:S(2)}, u32[]{:S(2)}) %all-to-all-start.1) | async-done | bytes 524320 | tf_op jit(solution)/shard_map/all_to_all | solution.py:347
  72.3 0.0 copy-done
  72.3 0.0 copy-done.3
  72.3 0.0 copy-done.7
  72.3 0.6 convolution_add_fusion.y_ref
  72.9 0.0 copy-done.1
  73.0 0.0 copy-done.2
  73.0 30.9 %shard_map.137 = f32[128,1024]{1,0:T(8,128)S(1)} custom-call(f32[128,1024]{1,0:T(8,128)S(1)} %convolution_add_fusion.y_ref, f32[1,1024]{1,0:T(1,128)S(1)} %bitcast.28, f32[1,1024]{1,0:T(1,128)S(1)} %bitcast.29, bf16[1024,512]{1,0:T(8,128)(2,1)} %w1_hbm.1, bf16[512,1024]{1,0:T(8,128)(2,1)} %w2_hbm.1), custom_call_target="tpu_custom_call" | custom-call | tf_op jit(solution)/shard_map/pallas_call | solution.py:266
  103.9 0.1 reduce_sum.64
  104.0 0.2 multiply_reduce_fusion
  104.2 0.0 copy-done.8
  104.2 0.0 copy-done.9
  104.2 0.9 add_convert_fusion
  (9 shorter events, 0.1 us)
Async XLA Ops:
  0.0 72.3 %copy-start = (bf16[1024,1024]{1,0:T(8,128)(2,1)S(1)}, bf16[1024,1024]{1,0:T(8,128)(2,1)}, u32[]{:S(2)}) copy-start(bf16[1024,1024]{1,0:T(8,128)(2,1)} %param.21) | copy-start | bytes 6291460
  0.0 15.4 %copy-start.4 = (s32[16384,1]{0,1:T(1,128)S(1)}, s32[16384,1]{0,1:T(1,128)}, u32[]{:S(2)}) copy-start(s32[16384,1]{0,1:T(1,128)} %param.15) | copy-start | bytes 196612
  0.0 15.9 %copy-start.5 = (s32[16384]{0:T(1024)S(1)}, s32[16384]{0:T(1024)}, u32[]{:S(2)}) copy-start(s32[16384]{0:T(1024)} %param.16) | copy-start | bytes 196612
  0.0 16.5 %copy-start.10 = (s32[4]{0:T(128)S(1)}, s32[4]{0:T(128)}, u32[]{:S(2)}) copy-start(s32[4]{0:T(128)} %param.17) | copy-start | bytes 52
  1.9 2.4 %copy-start.6 = (s32[128]{0:T(128)}, s32[128]{0:T(128)S(1)}, u32[]{:S(2)}) copy-start(s32[128]{0:T(128)S(1)} %fusion.13) | copy-start | bytes 1540
  4.3 24.9 %all-to-all-start = ((bf16[128,2,1024]{2,1,0:T(2,128)(2,1)}), bf16[128,2,1024]{2,1,0:T(2,128)(2,1)S(1)}, u32[]{:S(2)}, u32[]{:S(2)}) async-start(bf16[128,2,1024]{2,1,0:T(2,128)(2,1)} %reshape.238), calls=%async_computation | async-start | bytes 1048576 | tf_op jit(solution)/shard_map/all_to_all | solution.py:333
  33.9 38.3 %copy-start.3 = (bf16[128,1024]{1,0:T(8,128)(2,1)S(1)}, bf16[128,1024]{1,0:T(8,128)(2,1)}, u32[]{:S(2)}) copy-start(bf16[128,1024]{1,0:T(8,128)(2,1)} %param.14) | copy-start | bytes 786436
  34.0 38.3 %copy-start.7 = (s32[128]{0:T(128)S(1)}, s32[128]{0:T(128)}, u32[]{:S(2)}) copy-start(s32[128]{0:T(128)} %copy-done.6) | copy-start | bytes 1540
  52.9 20.0 %copy-start.1 = (f32[1024]{0:T(1024)S(1)}, f32[1024]{0:T(1024)}, u32[]{:S(2)}) copy-start(f32[1024]{0:T(1024)} %param.24) | copy-start | bytes 12292
  53.0 20.0 %copy-start.2 = (f32[1024]{0:T(1024)S(1)}, f32[1024]{0:T(1024)}, u32[]{:S(2)}) copy-start(f32[1024]{0:T(1024)} %param.25) | copy-start | bytes 12292
  54.0 18.3 %all-to-all-start.1 = ((bf16[128,2,1024]{2,1,0:T(2,128)(2,1)}), bf16[128,2,1024]{2,1,0:T(2,128)(2,1)S(1)}, u32[]{:S(2)}, u32[]{:S(2)}) async-start(bf16[128,2,1024]{2,1,0:T(2,128)(2,1)} %reshape.243), calls=%async_computation.1 | async-start | bytes 1048576 | tf_op jit(solution)/shard_map/all_to_all | solution.py:347
  58.6 45.6 %copy-start.8 = (f32[1024]{0:T(1024)S(1)}, f32[1024]{0:T(1024)}, u32[]{:S(2)}) copy-start(f32[1024]{0:T(1024)} %param.27) | copy-start | bytes 12292
  58.6 45.6 %copy-start.9 = (f32[1024]{0:T(1024)S(1)}, f32[1024]{0:T(1024)}, u32[]{:S(2)}) copy-start(f32[1024]{0:T(1024)} %param.26) | copy-start | bytes 12292
